TPU v7x, 512 devices: a whole 4x8x8 slice. The times are simulated.
512 devices in a mesh: dp: 8 (over z), section: 4 (over x), tm: 16 (over y, core).
Axes of the slice: x: 4, y: 8, z: 8, core: 2. Of those that a mesh axis runs over, the one named last changes fastest.
Arguments:
- frames: bfloat16 [16, 2048, 1280], P('dp', 'tm'), may hold values from -6 to 6
- block_mask: int32 [16, 32, 2], P('dp', 'tm'), may hold values 0 or 1
- span_segment: int32 [16, 32], P('dp'), may hold values from 0 to 15, as said below
- dec_states: bfloat16 [8192, 1280], P(('dp', 'tm')), may hold values from -6 to 6
- enc_qkv: bfloat16 [4, 1280, 1920], P('section', ('dp', 'tm')), may hold values from -0.15625 to 0.15625
- enc_out: bfloat16 [4, 640, 1280], P('section', None, ('dp', 'tm')), may hold values from -0.75 to 0.75
- cross_query: bfloat16 [1280, 768], P(('dp', 'tm'), 'section'), may hold values from -0.15625 to 0.15625
- cross_key: bfloat16 [1280, 768], P(('dp', 'tm'), 'section'), may hold values from -0.15625 to 0.15625
- cross_value: bfloat16 [1280, 768], P(('dp', 'tm'), 'section'), may hold values from -0.75 to 0.75
- cotangent: bfloat16 [8192, 1280], P(('dp', 'tm')), may hold values from -1 to 1
Outputs:
- context: bfloat16 [8192, 768], P(('dp', 'tm'), 'section')
- out_grad: float32 [768, 1280], P('section', ('dp', 'tm'))
Inputs may be any that keep to these rules, and one draw needn't show every extreme that they name: `span_segment`: the first of every 2 blocks, block d * 2, serves segment (d + 8) mod 16; every other block serves a segment drawn evenly.
All inputs are finite; a program needn't handle non-finite values. No bound on the sum of `block_mask` on one device may be relied on, other than what follows from the above.
Results may differ from a plain program's by a relative error of at most 0.011.
Values may be sent and summed in bfloat16 or wider, within the bound.
No kernel may reach another device: no remote copies, remote signals or barrier semaphores. Data moves between devices by JAX's collectives and lax.ppermute only.
A program may use at most 64 MiB of HBM per device.

v0:
```python
import jax
import jax.numpy as jnp
from jax import lax
from jax.sharding import PartitionSpec as P

HD = 64
BLK = 64
MB = 2


epsilon = 1e-05


def padded_2(shard, sides, width):
    for axis, dim in sides:
        size, length = (lax.axis_size(axis), shard.shape[dim])
        up = [(i, (i + 1) % size) for i in range(size - 1)]
        down = [(j, i) for i, j in up]
        last = lax.slice_in_dim(shard, length - width, length, axis=dim)
        initial = lax.slice_in_dim(shard, 0, width, axis=dim)
        before = lax.ppermute(last, axis, up)
        after = lax.ppermute(initial, axis, down)
        shard = jnp.concatenate([before, shard, after], axis=dim)
    return shard


def passed_along(block, axis, distance):
    devices = range(lax.axis_size(axis))
    route = [(i - distance, i) for i in devices if i - distance in devices]
    return lax.ppermute(block, axis, route)


def spread_2(value, axis, source):
    kept = jnp.where(lax.axis_index(axis) == source, value, 0).astype(value.dtype)
    return lax.psum(kept, axis)


def norm_rows(inputs):
    values32 = inputs.astype(jnp.float32)
    center = values32 - jnp.mean(values32, axis=-1, keepdims=True)
    spread = jnp.mean(center * center, axis=-1, keepdims=True)
    return (center * lax.rsqrt(spread + epsilon)).astype(jnp.bfloat16)


def allowed_keys(mask_rows, first_block, total_blocks):
    block_count = mask_rows.shape[0]
    block_index = first_block + jnp.arange(block_count, dtype=jnp.int32)
    left_open = (mask_rows[:, 0] == 1) & (block_index > 0)
    right_open = (mask_rows[:, 1] == 1) & (block_index < total_blocks - 1)
    middle = jnp.ones((block_count, BLK), dtype=jnp.bool_)
    return jnp.concatenate(
        [
            jnp.broadcast_to(left_open[:, None], (block_count, BLK)),
            middle,
            jnp.broadcast_to(right_open[:, None], (block_count, BLK)),
        ],
        axis=1,
    )


def window_attention(queries, key_rows, value_rows, allowed):
    frame_count = queries.shape[0]
    block_count = frame_count // BLK
    head_count = queries.shape[1] // HD

    def windows(padded):
        return jnp.concatenate(
            [
                padded[offset * BLK : offset * BLK + frame_count].reshape(
                    block_count, BLK, head_count, HD
                )
                for offset in range(3)
            ],
            axis=1,
        )

    query_blocks = queries.reshape(block_count, BLK, head_count, HD)
    scores = jnp.einsum(
        "bqhd,bkhd->bhqk", query_blocks, windows(key_rows), preferred_element_type=jnp.float32
    ) * HD ** (-0.5)
    weights = jnp.where(allowed[:, None, None, :], jnp.exp(scores), 0.0)
    totals = jnp.sum(weights, axis=-1)
    summed = jnp.einsum(
        "bhqk,bkhd->bqhd",
        weights.astype(jnp.bfloat16),
        windows(value_rows),
        preferred_element_type=jnp.float32,
    )
    context = summed / jnp.transpose(totals, (0, 2, 1))[..., None]
    return context.reshape(frame_count, head_count * HD).astype(jnp.bfloat16)


def per_device(
    frames,
    block_mask,
    span_segment,
    dec_states,
    enc_qkv,
    enc_out,
    cross_query,
    cross_key,
    cross_value,
    cotangent,
):
    qkv_full, out_full, query_weight, key_weight, value_weight = (
        lax.all_gather(enc_qkv, ("dp", "tm"), axis=1, tiled=True),
        lax.all_gather(enc_out, ("dp", "tm"), axis=2, tiled=True),
        lax.all_gather(cross_query, ("dp", "tm"), axis=0, tiled=True),
        lax.all_gather(cross_key, ("dp", "tm"), axis=0, tiled=True),
        lax.all_gather(cross_value, ("dp", "tm"), axis=0, tiled=True),
    )
    proj_qkv = qkv_full[0]
    proj_out = out_full[0]
    enc_width = proj_out.shape[0]
    sections = lax.axis_size("section")
    section_index = lax.axis_index("section")
    shard_index = lax.axis_index("tm")
    shard_count = lax.axis_size("tm")
    local_frames = frames.shape[1]
    local_blocks = local_frames // BLK
    first_block = shard_index * local_blocks
    total_blocks = local_blocks * shard_count
    carried = jnp.zeros_like(frames[0])
    results = []
    for moment in range(MB + sections - 1):
        if moment < MB:
            carried = jnp.where(section_index == 0, frames[moment], carried)
        sequence_index = jnp.clip(moment - section_index, 0, MB - 1)
        mask_rows = lax.dynamic_index_in_dim(block_mask, sequence_index, 0, keepdims=False)
        normed = norm_rows(carried)
        packed = jnp.dot(normed, proj_qkv, preferred_element_type=jnp.float32).astype(jnp.bfloat16)
        encoder_key_value = padded_2(packed[:, enc_width:], (("tm", 0),), BLK)
        encoder_allowed = allowed_keys(mask_rows, first_block, total_blocks)
        encoder_context = window_attention(
            packed[:, :enc_width],
            encoder_key_value[:, :enc_width],
            encoder_key_value[:, enc_width:],
            encoder_allowed,
        )
        update = jnp.dot(encoder_context, proj_out, preferred_element_type=jnp.float32)
        finished = (carried.astype(jnp.float32) + update).astype(jnp.bfloat16)
        if moment >= sections - 1:
            results.append(finished)
        if moment < MB + sections - 2:
            carried = passed_along(finished, "section", 1)
    memory = spread_2(jnp.stack(results), "section", sections - 1)
    cross_width = query_weight.shape[1]
    cross_heads = cross_width // HD
    mem_norm = norm_rows(memory)
    both_weights = jnp.concatenate([key_weight, value_weight], axis=1)
    key_value = jnp.dot(mem_norm, both_weights, preferred_element_type=jnp.float32).astype(
        jnp.bfloat16
    )
    tokens = dec_states.shape[0] // MB
    queries = jnp.dot(
        norm_rows(dec_states), query_weight, preferred_element_type=jnp.float32
    ).astype(jnp.bfloat16)
    queries = queries.reshape(MB, tokens, cross_heads, HD)
    score_scale = HD ** (-0.5)
    frame_segment = jnp.repeat(span_segment, BLK, axis=1)
    block_piece = lax.all_gather(key_value, "tm", axis=1, tiled=True)
    row_count = block_piece.shape[1]
    allowed = frame_segment == shard_index
    piece_keys = block_piece[..., :cross_width].reshape(MB, row_count, cross_heads, HD)
    piece_values = block_piece[..., cross_width:].reshape(MB, row_count, cross_heads, HD)
    scores = (
        jnp.einsum("mqhd,mkhd->mhqk", queries, piece_keys, preferred_element_type=jnp.float32)
        * score_scale
    )
    weights = jnp.where(allowed[:, None, None, :], jnp.exp(scores), 0.0)
    summed_run = jnp.einsum(
        "mhqk,mkhd->mhqd",
        weights.astype(jnp.bfloat16),
        piece_values,
        preferred_element_type=jnp.float32,
    )
    totals = jnp.sum(weights, axis=-1)
    context = summed_run / totals[..., None]
    context = context.transpose(0, 2, 1, 3).reshape(MB * tokens, cross_width).astype(jnp.bfloat16)
    partial_value = jnp.dot(context.T, cotangent, preferred_element_type=jnp.float32)
    grad_shard = lax.psum_scatter(partial_value, ("dp", "tm"), scatter_dimension=1, tiled=True)
    return (context, grad_shard)


def solution(mesh):
    in_specs = (
        P("dp", "tm", None),
        P("dp", "tm", None),
        P("dp", None),
        P(("dp", "tm"), None),
        P("section", ("dp", "tm"), None),
        P("section", None, ("dp", "tm")),
        P(("dp", "tm"), "section"),
        P(("dp", "tm"), "section"),
        P(("dp", "tm"), "section"),
        P(("dp", "tm"), None),
    )
    out_specs = (P(("dp", "tm"), "section"), P("section", ("dp", "tm")))
    return jax.shard_map(
        per_device, mesh=mesh, in_specs=in_specs, out_specs=out_specs, check_vma=False
    )
```

profile of v0, /device:TPU:30, one launch (start us, length us, event | category | flops | bytes accessed | tf_op | source)
XLA Modules:
  0.0 754.7 jit_solution(8843299660056833524)
XLA Ops:
  7.2 1.4 copy.226
  8.7 1.5 copy.210
  14.9 84.7 %all-gather.9.cloned.1.call-done = bf16[1,640,1280]{1,0,2:T(2,128)(2,1)} async-done(((bf16[1,640,10]{1,0,2:T(2,128)(2,1)}), bf16[1,640,1280]{1,0,2:T(2,128)(2,1)}) %all-gather.9.cloned.1.call-update) | async-done | bytes 1638416 | tf_op jit(solution)/shard_map/all_gather | solution.py:107
  99.6 6.1 copy.227
  105.7 82.7 %all-gather.7.cloned.1.call-done = bf16[1,1280,1920]{2,0,1:T(2,128)(2,1)} async-done(((bf16[1,10,1920]{2,0,1:T(2,128)(2,1)}), bf16[1,1280,1920]{2,0,1:T(2,128)(2,1)}) %all-gather.7.cloned.1.call-update) | async-done | bytes 4915216 | tf_op jit(solution)/shard_map/all_gather | solution.py:106
  188.5 4.5 copy.362
  196.0 2.1 collective-permute-start
  198.1 3.4 collective-permute-start.1
  202.7 2.1 copy.222
  207.0 2.1 copy.215
  209.1 1.8 pad_maximum_fusion.17
  218.3 2.1 fusion.205
  223.1 10.2 %collective-permute-done.2 = bf16[128,1280]{1,0:T(8,128)(2,1)S(1)} collective-permute-done((bf16[128,1280]{1,0:T(8,128)(2,1)S(1)}, bf16[128,1280]{1,0:T(8,128)(2,1)S(1)}, u32[]{:S(2)}, u32[]{:S(2)}) %collective-permute-start.2) | collective-permute-done | bytes 327712 | tf_op jit(solution)/shard_map/ppermute | solution.py:30
  233.8 3.3 fusion.20
  237.9 1.9 collective-permute-start.3
  239.9 3.8 collective-permute-start.4
  249.2 1.7 pad_maximum_fusion.13
  257.4 1.9 fusion.206
  262.0 9.8 %collective-permute-done.5 = bf16[128,1280]{1,0:T(8,128)(2,1)S(1)} collective-permute-done((bf16[128,1280]{1,0:T(8,128)(2,1)S(1)}, bf16[128,1280]{1,0:T(8,128)(2,1)S(1)}, u32[]{:S(2)}, u32[]{:S(2)}) %collective-permute-start.5) | collective-permute-done | bytes 327712 | tf_op jit(solution)/shard_map/ppermute | solution.py:30
  272.2 3.3 fusion.23
  276.4 1.9 collective-permute-start.6
  278.3 3.9 collective-permute-start.7
  287.7 1.7 pad_maximum_fusion.9
  295.9 1.9 fusion.207
  300.5 9.1 %collective-permute-done.8 = bf16[128,1280]{1,0:T(8,128)(2,1)S(1)} collective-permute-done((bf16[128,1280]{1,0:T(8,128)(2,1)S(1)}, bf16[128,1280]{1,0:T(8,128)(2,1)S(1)}, u32[]{:S(2)}, u32[]{:S(2)}) %collective-permute-start.8) | collective-permute-done | bytes 327712 | tf_op jit(solution)/shard_map/ppermute | solution.py:30
  310.0 3.3 fusion.26
  314.2 1.9 collective-permute-start.10
  316.1 2.7 collective-permute-start.9
  324.3 1.7 pad_maximum_fusion.5
  332.5 1.9 fusion.208
  337.2 10.7 %collective-permute-done.11 = bf16[128,1280]{1,0:T(8,128)(2,1)S(1)} collective-permute-done((bf16[128,1280]{1,0:T(8,128)(2,1)S(1)}, bf16[128,1280]{1,0:T(8,128)(2,1)S(1)}, u32[]{:S(2)}, u32[]{:S(2)}) %collective-permute-start.11) | collective-permute-done | bytes 327712 | tf_op jit(solution)/shard_map/ppermute | solution.py:30
  348.2 3.3 fusion.29
  352.4 1.9 collective-permute-start.12
  354.3 4.1 collective-permute-start.13
  361.5 2.1 reshape.350
  365.9 1.8 pad_maximum_fusion.1
  374.2 2.0 fusion.209
  378.7 49.4 %all-gather.1 = bf16[128,10,192]{2,1,0:T(8,128)(2,1)S(1)} all-gather(bf16[1,10,192]{2,1,0:T(8,128)(2,1)S(1)} %bitcast.141), channel_id=1, replica_groups=mesh['dp'=8,'section'=4,'tm'=16] {'dp','tm'}, dimensions={0}, use_global_device_ids=true | all-gather | bytes 495360 | tf_op jit(solution)/shard_map/all_gather | solution.py:109
  428.6 49.4 %all-gather.2 = bf16[128,10,192]{2,1,0:T(8,128)(2,1)S(1)} all-gather(bf16[1,10,192]{2,1,0:T(8,128)(2,1)S(1)} %bitcast.142), channel_id=1, replica_groups=mesh['dp'=8,'section'=4,'tm'=16] {'dp','tm'}, dimensions={0}, use_global_device_ids=true | all-gather | bytes 495360 | tf_op jit(solution)/shard_map/all_gather | solution.py:110
  479.7 1.4 fusion.50
  482.6 49.0 %all-gather = bf16[128,10,192]{2,1,0:T(8,128)(2,1)S(1)} all-gather(bf16[1,10,192]{2,1,0:T(8,128)(2,1)S(1)} %bitcast.143), channel_id=1, replica_groups=mesh['dp'=8,'section'=4,'tm'=16] {'dp','tm'}, dimensions={0}, use_global_device_ids=true | all-gather | bytes 495360 | tf_op jit(solution)/shard_map/all_gather | solution.py:108
  533.0 4.7 fusion.194
  537.7 3.9 copy.288
  541.6 2.3 copy.290
  543.9 2.1 fusion.210
  546.7 1.4 fusion.211
  550.1 196.5 %all-reduce.6.cloned.1.call-done = f32[192,1280]{0,1:T(8,128)} async-done(((f32[192,1280]{0,1:T(8,128)}), f32[192,1280]{0,1:T(8,128)}) %all-reduce.6.cloned.1.call-update) | async-done | bytes 983056
  746.6 1.3 constant_dynamic-slice_fusion.5
  (267 shorter events, 90.8 us)
Async XLA Ops:
  7.2 539.5 %copy-start = (bf16[64,1280]{1,0:T(8,128)(2,1)S(1)}, bf16[64,1280]{1,0:T(8,128)(2,1)}, u32[]{:S(2)}) copy-start(bf16[64,1280]{1,0:T(8,128)(2,1)} %param.19) | copy-start | bytes 491524
  7.2 92.5 %all-gather.9.cloned.1.call-start = ((), (), s32[]{:S(2)}) async-start(), calls=%async_computation.1 | async-start | bytes 3302400 | tf_op jit(solution)/shard_map/all_gather | solution.py:107
  8.6 179.8 %all-gather.7.cloned.1.call-start = ((), (), s32[]{:S(2)}) async-start(), calls=%async_computation | async-start | bytes 9907200 | tf_op jit(solution)/shard_map/all_gather | solution.py:106
  10.2 468.2 %all-reduce.4.cloned.1.call-start = ((), (), s32[]{:S(2)}) async-start(), calls=%async_computation.2 | async-start | bytes 1310720 | tf_op jit(solution)/shard_map/psum | solution.py:35
  105.7 87.3 %copy-start.8 = (bf16[2,128,1280]{2,1,0:T(8,128)(2,1)S(1)}, bf16[2,128,1280]{2,1,0:T(8,128)(2,1)}, u32[]{:S(2)}) copy-start(bf16[2,128,1280]{2,1,0:T(8,128)(2,1)} %param.10) | copy-start | bytes 1966084
  193.0 2.2 copy-start.1
  195.2 7.5 copy-start.4
  196.0 13.1 %collective-permute-start = (bf16[64,1280]{1,0:T(8,128)(2,1)}, bf16[64,1280]{1,0:T(8,128)(2,1)}, u32[]{:S(2)}, u32[]{:S(2)}) collective-permute-start(bf16[64,1280]{1,0:T(8,128)(2,1)} %get-tuple-element.59), channel_id=1, source_target_pairs={{0,1},{1,2},{2,3},{3,4},{4,5},{5,6},{6,7},{7,8},{8,9},{9,10},{10,1... | collective-permute-start | bytes 491528 | tf_op jit(solution)/shard_map/ppermute | solution.py:21
  198.1 10.9 %collective-permute-start.1 = (bf16[64,1280]{1,0:T(8,128)(2,1)}, bf16[64,1280]{1,0:T(8,128)(2,1)}, u32[]{:S(2)}, u32[]{:S(2)}) collective-permute-start(bf16[64,1280]{1,0:T(8,128)(2,1)} %get-tuple-element.60), channel_id=1, source_target_pairs={{1,0},{2,1},{3,2},{4,3},{5,4},{6,5},{7,6},{8,7},{9,8},{10,9},{11,1... | collective-permute-start | bytes 491528 | tf_op jit(solution)/shard_map/ppermute | solution.py:22
  204.8 4.3 slice-start.1
  218.3 2.1 copy-start.18
  218.3 2.1 copy-start.26
  218.3 2.1 copy-start.31
  221.8 11.5 %collective-permute-start.2 = (bf16[128,1280]{1,0:T(8,128)(2,1)S(1)}, bf16[128,1280]{1,0:T(8,128)(2,1)S(1)}, u32[]{:S(2)}, u32[]{:S(2)}) collective-permute-start(bf16[128,1280]{1,0:T(8,128)(2,1)S(1)} %fusion.12), channel_id=1, source_target_pairs={{0,16},{16,32},{32,48},{1,17},{17,33},{33,49},{2,18},{18,34},{34,5... | collective-permute-start | bytes 983048 | tf_op jit(solution)/shard_map/ppermute | solution.py:30
  237.1 8.5 %copy-start.5 = (bf16[128,1920]{1,0:T(8,128)(2,1)}, bf16[128,1920]{1,0:T(8,128)(2,1)S(1)}, u32[]{:S(2)}) copy-start(bf16[128,1920]{1,0:T(8,128)(2,1)S(1)} %fusion.20) | copy-start | bytes 1474564
  237.9 11.2 %collective-permute-start.3 = (bf16[64,1280]{1,0:T(8,128)(2,1)}, bf16[64,1280]{1,0:T(8,128)(2,1)}, u32[]{:S(2)}, u32[]{:S(2)}) collective-permute-start(bf16[64,1280]{1,0:T(8,128)(2,1)} %get-tuple-element.50), channel_id=1, source_target_pairs={{0,1},{1,2},{2,3},{3,4},{4,5},{5,6},{6,7},{7,8},{8,9},{9,10},{10,1... | collective-permute-start | bytes 491528 | tf_op jit(solution)/shard_map/ppermute | solution.py:21
  239.9 9.3 %collective-permute-start.4 = (bf16[64,1280]{1,0:T(8,128)(2,1)}, bf16[64,1280]{1,0:T(8,128)(2,1)}, u32[]{:S(2)}, u32[]{:S(2)}) collective-permute-start(bf16[64,1280]{1,0:T(8,128)(2,1)} %get-tuple-element.51), channel_id=1, source_target_pairs={{1,0},{2,1},{3,2},{4,3},{5,4},{6,5},{7,6},{8,7},{9,8},{10,9},{11,1... | collective-permute-start | bytes 491528 | tf_op jit(solution)/shard_map/ppermute | solution.py:22
  246.7 2.5 slice-start.2
  254.9 2.5 copy-start.14
  254.9 2.5 copy-start.22
  260.7 11.1 %collective-permute-start.5 = (bf16[128,1280]{1,0:T(8,128)(2,1)S(1)}, bf16[128,1280]{1,0:T(8,128)(2,1)S(1)}, u32[]{:S(2)}, u32[]{:S(2)}) collective-permute-start(bf16[128,1280]{1,0:T(8,128)(2,1)S(1)} %fusion.13), channel_id=1, source_target_pairs={{0,16},{16,32},{32,48},{1,17},{17,33},{33,49},{2,18},{18,34},{34,5... | collective-permute-start | bytes 983048 | tf_op jit(solution)/shard_map/ppermute | solution.py:30
  275.6 8.5 %copy-start.6 = (bf16[128,1920]{1,0:T(8,128)(2,1)}, bf16[128,1920]{1,0:T(8,128)(2,1)S(1)}, u32[]{:S(2)}) copy-start(bf16[128,1920]{1,0:T(8,128)(2,1)S(1)} %fusion.23) | copy-start | bytes 1474564
  276.4 11.2 %collective-permute-start.6 = (bf16[64,1280]{1,0:T(8,128)(2,1)}, bf16[64,1280]{1,0:T(8,128)(2,1)}, u32[]{:S(2)}, u32[]{:S(2)}) collective-permute-start(bf16[64,1280]{1,0:T(8,128)(2,1)} %get-tuple-element.41), channel_id=1, source_target_pairs={{0,1},{1,2},{2,3},{3,4},{4,5},{5,6},{6,7},{7,8},{8,9},{9,10},{10,1... | collective-permute-start | bytes 491528 | tf_op jit(solution)/shard_map/ppermute | solution.py:21
  278.3 9.3 %collective-permute-start.7 = (bf16[64,1280]{1,0:T(8,128)(2,1)}, bf16[64,1280]{1,0:T(8,128)(2,1)}, u32[]{:S(2)}, u32[]{:S(2)}) collective-permute-start(bf16[64,1280]{1,0:T(8,128)(2,1)} %get-tuple-element.42), channel_id=1, source_target_pairs={{1,0},{2,1},{3,2},{4,3},{5,4},{6,5},{7,6},{8,7},{9,8},{10,9},{11,1... | collective-permute-start | bytes 491528 | tf_op jit(solution)/shard_map/ppermute | solution.py:22
  285.2 2.5 slice-start.3
  293.4 2.5 copy-start.15
  293.4 2.5 copy-start.23
  299.2 10.4 %collective-permute-start.8 = (bf16[128,1280]{1,0:T(8,128)(2,1)S(1)}, bf16[128,1280]{1,0:T(8,128)(2,1)S(1)}, u32[]{:S(2)}, u32[]{:S(2)}) collective-permute-start(bf16[128,1280]{1,0:T(8,128)(2,1)S(1)} %fusion.14), channel_id=1, source_target_pairs={{0,16},{16,32},{32,48},{1,17},{17,33},{33,49},{2,18},{18,34},{34,5... | collective-permute-start | bytes 983048 | tf_op jit(solution)/shard_map/ppermute | solution.py:30
  313.4 7.3 copy-start.7
  314.2 10.1 %collective-permute-start.10 = (bf16[64,1280]{1,0:T(8,128)(2,1)}, bf16[64,1280]{1,0:T(8,128)(2,1)}, u32[]{:S(2)}, u32[]{:S(2)}) collective-permute-start(bf16[64,1280]{1,0:T(8,128)(2,1)} %get-tuple-element.33), channel_id=1, source_target_pairs={{1,0},{2,1},{3,2},{4,3},{5,4},{6,5},{7,6},{8,7},{9,8},{10,9},{11,1... | collective-permute-start | bytes 491528 | tf_op jit(solution)/shard_map/ppermute | solution.py:22
  316.1 8.1 %collective-permute-start.9 = (bf16[64,1280]{1,0:T(8,128)(2,1)}, bf16[64,1280]{1,0:T(8,128)(2,1)}, u32[]{:S(2)}, u32[]{:S(2)}) collective-permute-start(bf16[64,1280]{1,0:T(8,128)(2,1)} %get-tuple-element.32), channel_id=1, source_target_pairs={{0,1},{1,2},{2,3},{3,4},{4,5},{5,6},{6,7},{7,8},{8,9},{9,10},{10,1... | collective-permute-start | bytes 491528 | tf_op jit(solution)/shard_map/ppermute | solution.py:21
  321.8 2.5 slice-start.4
  330.0 2.5 copy-start.16
  330.0 2.5 copy-start.24
  335.8 12.0 %collective-permute-start.11 = (bf16[128,1280]{1,0:T(8,128)(2,1)S(1)}, bf16[128,1280]{1,0:T(8,128)(2,1)S(1)}, u32[]{:S(2)}, u32[]{:S(2)}) collective-permute-start(bf16[128,1280]{1,0:T(8,128)(2,1)S(1)} %fusion.15), channel_id=1, source_target_pairs={{0,16},{16,32},{32,48},{1,17},{17,33},{33,49},{2,18},{18,34},{34,5... | collective-permute-start | bytes 983048 | tf_op jit(solution)/shard_map/ppermute | solution.py:30
  351.6 8.9 %copy-start.3 = (bf16[128,1920]{1,0:T(8,128)(2,1)}, bf16[128,1920]{1,0:T(8,128)(2,1)S(1)}, u32[]{:S(2)}) copy-start(bf16[128,1920]{1,0:T(8,128)(2,1)S(1)} %fusion.29) | copy-start | bytes 1474564
  352.4 13.5 %collective-permute-start.12 = (bf16[64,1280]{1,0:T(8,128)(2,1)}, bf16[64,1280]{1,0:T(8,128)(2,1)}, u32[]{:S(2)}, u32[]{:S(2)}) collective-permute-start(bf16[64,1280]{1,0:T(8,128)(2,1)} %get-tuple-element.23), channel_id=1, source_target_pairs={{0,1},{1,2},{2,3},{3,4},{4,5},{5,6},{6,7},{7,8},{8,9},{9,10},{10,1... | collective-permute-start | bytes 491528 | tf_op jit(solution)/shard_map/ppermute | solution.py:21
  354.3 11.6 %collective-permute-start.13 = (bf16[64,1280]{1,0:T(8,128)(2,1)}, bf16[64,1280]{1,0:T(8,128)(2,1)}, u32[]{:S(2)}, u32[]{:S(2)}) collective-permute-start(bf16[64,1280]{1,0:T(8,128)(2,1)} %get-tuple-element.24), channel_id=1, source_target_pairs={{1,0},{2,1},{3,2},{4,3},{5,4},{6,5},{7,6},{8,7},{9,8},{10,9},{11,1... | collective-permute-start | bytes 491528 | tf_op jit(solution)/shard_map/ppermute | solution.py:22
  361.5 4.4 slice-start
  367.7 2.4 copy-start.12
  369.0 2.5 copy-start.11
  371.8 2.4 copy-start.13
  378.6 154.4 %all-gather.11.cloned.1.call-start = ((), (), s32[]{:S(2)}) async-start(), calls=%async_computation.3 | async-start | bytes 3342336 | tf_op jit(solution)/shard_map/all_gather | solution.py:161
  378.7 49.9 %copy-start.37 = (bf16[10,192]{1,0:T(8,128)(2,1)S(1)}, bf16[10,192]{1,0:T(8,128)(2,1)}, u32[]{:S(2)}) copy-start(bf16[10,192]{1,0:T(8,128)(2,1)} %param.18) | copy-start | bytes 11524
  478.4 2.8 copy-start.9
  482.5 264.1 %all-reduce.6.cloned.1.call-start = ((), (), s32[]{:S(2)}) async-start(), calls=%async_computation.4 | async-start | bytes 2621440
  482.6 49.4 %copy-start.10 = (bf16[64,1280]{1,0:T(8,128)(2,1)S(1)}, bf16[64,1280]{1,0:T(8,128)(2,1)}, u32[]{:S(2)}) copy-start(bf16[64,1280]{1,0:T(8,128)(2,1)} %param.13) | copy-start | bytes 491524
  543.9 2.1 copy-start.2
  (16 other events, 28.5 us)
Sparse Core Ops, SparseCore 0:
  11.7 87.8 all-gather.8
  102.9 85.5 all-gather.6
  378.7 51.4 all-reduce.3
  482.6 40.3 all-gather.10
  548.3 198.2 all-reduce.5
where the time goes:
time: 764 us; the launch traced here: 755 us
  waiting for transfers between devices  404 us (53%)
  blocking collectives  148 us (19%)
  local copies, waits for them, and re-layouts  103 us (13%)
  matrix products  34.1 us (4%)
  starting transfers between devices  33 us (4%)
  other arithmetic  17.4 us (2%)
  between operations  15.8 us (2%)
    unnamed x6, waiting for transfers between devices  197 us
    all_gather x1, waiting for transfers between devices, per_device(): lax.all_gather(enc_out, ('dp', 'tm'), axis=2, tiled=True)  84.7 us
    all_gather x1, waiting for transfers between devices, per_device(): lax.all_gather(enc_qkv, ('dp', 'tm'), axis=1, tiled=True)  82.7 us
    reshape x60, local copies, waits for them, and re-layouts, windows(): padded[offset * BLK:offset * BLK + frame_count]  54.9 us
    all_gather x1, blocking collectives, per_device(): lax.all_gather(cross_key, ('dp', 'tm'), axis=0, tiled=True)  49.4 us
    all_gather x1, blocking collectives, per_device(): lax.all_gather(cross_value, ('dp', 'tm'), axis=0, tiled=True)  49.4 us
    all_gather x1, blocking collectives, per_device(): lax.all_gather(cross_query, ('dp', 'tm'), axis=0, tiled=True)  49 us
    ppermute x4, waiting for transfers between devices, passed_along(): return lax.ppermute(block, axis, route)  39.9 us
  transfers between devices with their start and end apart: 19, of which 7 were waited for; matrix products, arithmetic and copies ran while one was open for 6% of the time, Pallas kernels for 0%

commit v1 on v0

v1 whole, which is shorter than its diff:
```python
import functools

import jax
import jax.numpy as jnp
from jax import lax
from jax.experimental import pallas as pl
from jax.experimental.pallas import tpu as pltpu
from jax.sharding import PartitionSpec as P

HD = 64
BLK = 64
MB = 2
EPS = 1e-05
F32 = jnp.float32
BF16 = jnp.bfloat16
VMEM = pl.BlockSpec(memory_space=pltpu.VMEM)
SMEM = pl.BlockSpec(memory_space=pltpu.SMEM)
PARAMS = pltpu.CompilerParams(vmem_limit_bytes=16 * 1024 * 1024)
JOIN_PARAMS = pltpu.CompilerParams()
JOINED = VMEM


def normed_rows(values):
    wide = values.astype(F32)
    center = wide - jnp.mean(wide, axis=-1, keepdims=True)
    spread = jnp.mean(center * center, axis=-1, keepdims=True)
    return (center * lax.rsqrt(spread + EPS)).astype(BF16)


def matmul(a, b):
    return jnp.dot(a, b, preferred_element_type=F32)


def matmul_nt(a, b):
    return lax.dot_general(a, b, (((1,), (1,)), ((), ())), preferred_element_type=F32)


def join_kernel(*refs):
    pieces, outs, sems = refs[:-4], refs[-4:-1], refs[-1]
    copies = []
    start = 0
    for index, out_ref in enumerate(outs):
        cols = slice(start, start + out_ref.shape[1])
        start += out_ref.shape[1]
        for slot, piece in enumerate(pieces):
            height = piece.shape[0]
            copies.append(
                pltpu.make_async_copy(
                    piece.at[:, cols],
                    out_ref.at[pl.ds(slot * height, height), :],
                    sems.at[index, slot],
                )
            )
    for copy in copies:
        copy.start()
    for copy in copies:
        copy.wait()


def kv_kernel(x_ref, w_ref, n_ref, first_ref, last_ref):
    n = normed_rows(x_ref[...])
    n_ref[...] = n
    kv = matmul(n, w_ref[...]).astype(BF16)
    first_ref[...] = kv[:BLK]
    last_ref[...] = kv[BLK:]


def allowed_of(moment, halo, place_ref, mask_ref):
    base = 4 * jnp.clip(moment - place_ref[0], 0, MB - 1)
    shard = place_ref[2]
    row = lax.broadcasted_iota(jnp.int32, (4 * BLK, 2 * BLK), 0)
    col = lax.broadcasted_iota(jnp.int32, (4 * BLK, 2 * BLK), 1)
    same = ((row // BLK) % 2 == 0) == (col < BLK)
    low_row = (row // BLK) % 2 == 0
    if halo:
        before = jnp.where(shard > 0, mask_ref[base], 0)
        after = jnp.where(shard < place_ref[5], mask_ref[base + 3], 0)
        open_side = jnp.where(low_row, before, after) == 1
        return same & open_side
    open_side = jnp.where(low_row, mask_ref[base + 1], mask_ref[base + 2]) == 1
    return same | open_side


def pair_attention(q, k, v, allowed):
    rows = q.shape[0]
    low = lax.broadcasted_iota(jnp.int32, q.shape, 1) < HD
    zero = jnp.zeros_like(q)
    both = jnp.concatenate([jnp.where(low, q, zero), jnp.where(low, zero, q)], axis=0)
    scores = matmul_nt(both, k) * HD ** (-0.5)
    weights = jnp.where(allowed, jnp.exp(scores), 0.0)
    totals = jnp.sum(weights, axis=-1, keepdims=True)
    summed = matmul(weights.astype(BF16), v)
    return (
        jnp.where(low, summed[:rows], summed[rows:]),
        jnp.where(low, totals[:rows], totals[rows:]),
    )


def own_kernel(
    moment, place_ref, mask_ref, n_ref, first_ref, last_ref, w_ref, q_ref, num_ref, den_ref
):
    width = q_ref.shape[1]
    allowed = allowed_of(moment, False, place_ref, mask_ref)
    q = matmul(n_ref[...], w_ref[...]).astype(BF16)
    q_ref[...] = q
    for lane in range(0, width, 2 * HD):
        cols = slice(lane, lane + 2 * HD)
        vcols = slice(width + lane, width + lane + 2 * HD)
        k = jnp.concatenate([first_ref[:, cols], last_ref[:, cols]], axis=0)
        v = jnp.concatenate([first_ref[:, vcols], last_ref[:, vcols]], axis=0)
        num_ref[:, cols], den_ref[:, cols] = pair_attention(q[:, cols], k, v, allowed)


def out_kernel(
    moment, place_ref, mask_ref, q_ref, num_ref, den_ref, left_ref, right_ref, x_ref, w_ref,
    o_ref, ctx_ref
):
    width = q_ref.shape[1]
    allowed = allowed_of(moment, True, place_ref, mask_ref)
    for lane in range(0, width, 2 * HD):
        cols = slice(lane, lane + 2 * HD)
        vcols = slice(width + lane, width + lane + 2 * HD)
        k = jnp.concatenate([left_ref[:, cols], right_ref[:, cols]], axis=0)
        v = jnp.concatenate([left_ref[:, vcols], right_ref[:, vcols]], axis=0)
        num, den = pair_attention(q_ref[:, cols], k, v, allowed)
        ctx_ref[:, cols] = ((num + num_ref[:, cols]) / (den + den_ref[:, cols])).astype(BF16)
    update = matmul_nt(ctx_ref[...], w_ref[...])
    o_ref[...] = (x_ref[...].astype(F32) + update).astype(BF16)


def order_kernel(order_ref, frames_ref, *out_refs):
    seqs, rows, model = frames_ref.shape
    frames = frames_ref[...].reshape(seqs * rows, model)
    for lane in range(0, model, 256):
        source = lax.broadcasted_iota(jnp.int32, (model, 256), 0)
        hit = source == order_ref[:, lane : lane + 256]
        pick = jnp.where(hit, 1.0, 0.0).astype(BF16)
        moved = matmul(frames, pick).astype(BF16)
        for seq, out_ref in enumerate(out_refs):
            out_ref[:, lane : lane + 256] = moved[seq * rows : (seq + 1) * rows]


def reorder_kernel(order_ref, w_ref, out_ref):
    model = w_ref.shape[0]
    for row in range(0, model, 256):
        source = lax.broadcasted_iota(jnp.int32, (256, model), 1)
        hit = source == order_ref[row : row + 256, :]
        pick = jnp.where(hit, 1.0, 0.0).astype(BF16)
        out_ref[row : row + 256, :] = matmul(pick, w_ref[...]).astype(BF16)


def query_kernel(seg_ref, dec_ref, w_ref, q_ref):
    q_ref[...] = matmul(normed_rows(dec_ref[...]), w_ref[...]).astype(BF16)


def cross_kernel(place_ref, q_ref, w_ref, *refs):
    parts, out_ref = refs[:-1], refs[-1]
    owner = place_ref[0] == place_ref[1]
    rows = []
    for start in (0, 4):
        own, a, b, c = (ref[...] for ref in parts[start : start + 4])
        rows.append(jnp.where(owner, own, a + b + c))
    n = normed_rows(jnp.concatenate(rows, axis=0))
    width = q_ref.shape[1]
    both = matmul(n, w_ref[...]).astype(BF16)
    keys, values = both[:, :width], both[:, width:]
    tokens = q_ref.shape[0] // 4
    heads = 3
    lane = lax.broadcasted_iota(jnp.int32, (tokens, width), 1)
    near = lax.broadcasted_iota(jnp.int32, (tokens, 2 * HD), 1)
    sums = jnp.zeros((tokens, 2 * HD), F32)
    thirds = []
    for piece in range(4):
        q = q_ref[piece * tokens : (piece + 1) * tokens, :]
        spots = slice(piece * BLK, (piece + 1) * BLK)
        stacked = jnp.concatenate(
            [jnp.where(lane // HD == head, q, jnp.zeros_like(q)) for head in range(heads)], axis=0
        )
        weights = jnp.exp(matmul_nt(stacked, keys[spots]) * HD ** (-0.5))
        totals = jnp.sum(weights, axis=-1, keepdims=True)
        summed = matmul(weights.astype(BF16), values[spots])
        high = totals.astype(BF16).astype(F32)
        rest = totals - high
        for head in range(heads):
            mine = slice(head * tokens, (head + 1) * tokens)
            sums = jnp.where(near == 32 * piece + head, high[mine], sums)
            sums = jnp.where(near == 32 * piece + heads + head, rest[mine], sums)
        pair = jnp.where(near < HD, summed[:tokens, : 2 * HD], summed[tokens : 2 * tokens, : 2 * HD])
        out_ref[piece * tokens : (piece + 1) * tokens, :] = pair.astype(BF16)
        thirds.append(summed[2 * tokens :, 2 * HD :])
    at = 4 * tokens
    for block in range(2):
        shifted = pltpu.roll(thirds[2 + block], HD, 1)
        out_ref[at + block * tokens : at + (block + 1) * tokens, :] = jnp.where(
            near < HD, thirds[block], shifted
        ).astype(BF16)
    out_ref[at + 2 * tokens :, :] = sums.astype(BF16)


def combine_kernel(
    place_ref, span_ref, parts_ref, cot_ref, ctx_ref, grad_ref, pair_ref, third_ref, sum_ref, all_ref
):
    shards = parts_ref.shape[0]
    tokens = pair_ref.shape[1]
    heads = 3
    for ref in (pair_ref, third_ref, sum_ref):
        ref[...] = jnp.zeros_like(ref)
    lane = lax.broadcasted_iota(jnp.int32, (tokens, 2 * HD), 1)
    for shard in range(shards):
        sums = parts_ref[shard, 6 * tokens : 7 * tokens, :].astype(F32)
        for seq in range(MB):
            for block in range(2):
                segment = span_ref[seq * 2 * shards + shard * 2 + block]
                spot = segment * MB + seq
                piece = seq * 2 + block
                pair = parts_ref[shard, piece * tokens : (piece + 1) * tokens, :]
                third = parts_ref[shard, (4 + block) * tokens : (5 + block) * tokens, :]
                pair_ref[spot] = pair_ref[spot] + pair.astype(F32)
                third_ref[spot] = third_ref[spot] + third.astype(F32)
                sum_ref[spot] = sum_ref[spot] + jnp.where(lane // 32 == piece, sums, 0.0)
    count = shards * tokens
    near = lax.broadcasted_iota(jnp.int32, (count, 2 * HD), 1)
    for seq in range(MB):

        def taken(ref):
            return ref[...].reshape(shards, MB, tokens, 2 * HD)[:, seq].reshape(count, 2 * HD)

        sums = taken(sum_ref)

        def total(head):
            at = 64 * seq + head
            spots = (at, at + heads, at + 32, at + 32 + heads)
            return sum(sums[:, spot : spot + 1] for spot in spots)

        pair = taken(pair_ref) / jnp.where(near < HD, total(0), total(1))
        third = taken(third_ref) / total(2)
        if seq:
            third = pltpu.roll(third, HD, 1)
        third = jnp.where(near < HD, third, 0.0)
        rows = slice(seq * tokens, (seq + 1) * tokens)
        all_ref[:, rows, : 2 * HD] = pair.astype(BF16).reshape(shards, tokens, 2 * HD)
        all_ref[:, rows, 2 * HD :] = third.astype(BF16).reshape(shards, tokens, 2 * HD)
    ctx_ref[...] = all_ref[place_ref[2]][:, : heads * HD]
    context = all_ref[...].reshape(shards * MB * tokens, 4 * HD)
    grad = lax.dot_general(
        cot_ref[...], context, (((0,), (0,)), ((), ())), preferred_element_type=F32
    )
    grad_ref[...] = grad.reshape(grad_ref.shape).astype(BF16)


def columns_kernel(place_ref, cot_ref, out_ref):
    cols = cot_ref.shape[1]
    lanes = out_ref.shape[1]
    each = place_ref[3]
    row = lax.broadcasted_iota(jnp.int32, (cols, lanes), 0)
    lane = lax.broadcasted_iota(jnp.int32, (cols, lanes), 1)
    inside = lane % 16
    hit = (row == (lane // 16) * place_ref[4] + place_ref[2] * each + inside) & (inside < each)
    out_ref[...] = matmul(cot_ref[...], jnp.where(hit, 1.0, 0.0).astype(BF16)).astype(BF16)


def shape(dims, dtype=BF16):
    return jax.ShapeDtypeStruct(dims, dtype)


def per_device(
    frames,
    block_mask,
    span_segment,
    dec_states,
    enc_qkv,
    enc_out,
    cross_query,
    cross_key,
    cross_value,
    cotangent,
):
    sections = lax.axis_size("section")
    shards = lax.axis_size("tm")
    groups = lax.axis_size("dp")
    section = lax.axis_index("section")
    shard = lax.axis_index("tm")
    model = frames.shape[2]
    width = enc_out.shape[1]
    head_width = cross_query.shape[1]
    padded = 256

    def pad_lanes(w):
        return jnp.pad(w, ((0, 0), (0, padded - w.shape[1])))

    def around(value, axis, size, step):
        return lax.ppermute(value, axis, [(i, (i + step) % size) for i in range(size)])

    group = lax.axis_index("dp")
    own = jnp.concatenate([enc_qkv[0], enc_out[0].T], axis=1)
    blocks, steps = [own], [0]
    for step, count in ((1, groups // 2), (-1, (groups - 1) // 2)):
        moving = own
        for hop in range(count):
            moving = around(moving, "dp", groups, step)
            blocks.append(moving)
            steps.append(step * (hop + 1))
    block = jnp.concatenate(blocks, axis=0)
    chips = shards // 2
    ring, source = [block], [shard]
    for step, count in ((2, chips // 2), (-2, (chips - 1) // 2)):
        moving = block
        for hop in range(count):
            moving = around(moving, "tm", shards, step)
            ring.append(moving)
            source.append((shard - step * (hop + 1)) % shards)
    swap = [(i, i ^ 1) for i in range(shards)]
    pieces_w = ring + [lax.ppermute(value, "tm", swap) for value in ring]
    source = jnp.stack(source + [place ^ 1 for place in source])
    each = model // (groups * shards)
    slots = (group - jnp.array(steps)) % groups
    order = (slots[None, :, None] * shards + source[:, None, None]) * each + jnp.arange(each)
    order = order.reshape(-1).astype(jnp.int32)

    cross = jnp.concatenate([pad_lanes(w) for w in (cross_key, cross_value, cross_query)], axis=1)
    cross = lax.all_gather(cross, ("dp", "tm"), axis=0, tiled=True)
    tokens_all = lax.all_gather(
        jnp.concatenate([dec_states, cotangent], axis=1), "tm", axis=0, tiled=True
    )

    place = jnp.stack(
        [
            section,
            jnp.int32(sections - 1),
            shard,
            jnp.int32(each),
            jnp.int32(each * shards),
            jnp.int32(shards - 1),
        ]
    ).astype(jnp.int32)
    mask = block_mask.reshape(-1)
    inputs = pl.pallas_call(
        order_kernel,
        out_shape=(shape(frames.shape[1:]),) * MB,
        in_specs=[VMEM, VMEM],
        out_specs=(VMEM,) * MB,
        compiler_params=PARAMS,
        name="order",
    )(order.reshape(1, -1), frames)

    up = [(i, i + 1) for i in range(shards - 1)]
    down = [(i + 1, i) for i in range(shards - 1)]
    onward = [(i, i + 1) for i in range(sections - 1)]
    rows = frames.shape[1]
    tokens = dec_states.shape[0] // MB
    carried = inputs[0]
    memory = []
    w_q, w_kv, w_out = pl.pallas_call(
        join_kernel,
        out_shape=(shape((model, width)), shape((model, 2 * width)), shape((model, width))),
        in_specs=[pl.BlockSpec(memory_space=pl.ANY)] * len(pieces_w),
        out_specs=(JOINED,) * 3,
        scratch_shapes=[pltpu.SemaphoreType.DMA((3, len(pieces_w)))],
        compiler_params=JOIN_PARAMS,
        name="join",
    )(*pieces_w)
    for moment in range(MB + sections - 1):
        if 0 < moment < MB:
            carried = jnp.where(section == 0, inputs[moment], carried)
        if moment == 2:
            w_cross = pl.pallas_call(
                reorder_kernel,
                grid=(1,),
                out_shape=shape((model, 2 * padded)),
                in_specs=[
                    pl.BlockSpec((model, 1), lambda i: (0, 0)),
                    pl.BlockSpec((model, 2 * padded), lambda i: (0, 0)),
                ],
                out_specs=pl.BlockSpec((model, 2 * padded), lambda i: (0, 0)),
                compiler_params=PARAMS,
                name="reorder",
            )(order.reshape(-1, 1), cross)
            carried, w_cross = lax.optimization_barrier((carried, w_cross))
        if moment == 3:
            mine = lax.dynamic_slice_in_dim(span_segment, shard * 2, 2, axis=1).reshape(-1)
            queries = pl.pallas_call(
                query_kernel,
                grid_spec=pltpu.PrefetchScalarGridSpec(
                    num_scalar_prefetch=1,
                    grid=(4,),
                    in_specs=[
                        pl.BlockSpec((tokens, model), lambda i, seg: (seg[i] * MB + i // 2, 0)),
                        pl.BlockSpec((model, padded), lambda i, seg: (0, 2)),
                    ],
                    out_specs=pl.BlockSpec((tokens, padded), lambda i, seg: (i, 0)),
                ),
                out_shape=shape((4 * tokens, padded)),
                compiler_params=PARAMS,
                name="queries",
            )(mine, tokens_all, cross)
            carried, queries = lax.optimization_barrier((carried, queries))
        if moment == 4:
            cot_cols = pl.pallas_call(
                columns_kernel,
                grid=(1,),
                out_shape=shape((shards * MB * tokens, groups * 16)),
                in_specs=[
                    SMEM,
                    pl.BlockSpec((shards * MB * tokens, model), lambda i: (0, 1)),
                ],
                out_specs=pl.BlockSpec((shards * MB * tokens, groups * 16), lambda i: (0, 0)),
                compiler_params=PARAMS,
                name="columns",
            )(place, tokens_all)
            carried, cot_cols = lax.optimization_barrier((carried, cot_cols))

        n, first, last = pl.pallas_call(
            kv_kernel,
            out_shape=(shape((rows, model)), shape((BLK, 2 * width)), shape((BLK, 2 * width))),
            in_specs=[VMEM, VMEM],
            out_specs=(VMEM, VMEM, VMEM),
            compiler_params=PARAMS,
            name="keys_values",
        )(carried, w_kv)
        left = lax.ppermute(last, "tm", up)
        right = lax.ppermute(first, "tm", down)
        q, num, den = pl.pallas_call(
            functools.partial(own_kernel, moment),
            out_shape=(shape((rows, width)), shape((rows, width), F32), shape((rows, width), F32)),
            in_specs=[SMEM, SMEM] + [VMEM] * 4,
            out_specs=(VMEM, VMEM, VMEM),
            compiler_params=PARAMS,
            name="own_blocks",
        )(place, mask, n, first, last, w_q)
        finished = pl.pallas_call(
            functools.partial(out_kernel, moment),
            out_shape=shape((rows, model)),
            in_specs=[SMEM, SMEM] + [VMEM] * 7,
            out_specs=VMEM,
            scratch_shapes=[pltpu.VMEM((rows, width), BF16)],
            compiler_params=PARAMS,
            name="layer_out",
        )(place, mask, q, num, den, left, right, carried, w_out)
        if moment >= sections - 1:
            memory.append(finished)
            for target in (0, 1, 2):
                memory.append(lax.ppermute(finished, "section", [(sections - 1, target)]))
        if moment < MB + sections - 2:
            carried = lax.ppermute(finished, "section", onward)

    pieces = pl.pallas_call(
        cross_kernel,
        out_shape=shape((7 * tokens, 2 * HD)),
        in_specs=[SMEM] + [VMEM] * 10,
        out_specs=VMEM,
        compiler_params=PARAMS,
        name="cross",
    )(place, queries, w_cross, *memory)
    everyone = lax.all_gather(pieces, "tm", axis=0)
    context, grad = pl.pallas_call(
        combine_kernel,
        out_shape=(
            shape((MB * tokens, head_width)),
            shape((groups, 16, padded)),
        ),
        in_specs=[SMEM, SMEM, VMEM, VMEM],
        out_specs=(VMEM, VMEM),
        scratch_shapes=[pltpu.VMEM((shards * MB, tokens, 2 * HD), F32)] * 3
        + [pltpu.VMEM((shards, MB * tokens, padded), BF16)],
        compiler_params=PARAMS,
        name="combine",
    )(place, span_segment.reshape(-1), everyone, cot_cols)
    grad = lax.all_to_all(grad, "dp", 0, 0, tiled=True)
    grad_shard = jnp.sum(grad.astype(F32), axis=0)[:each, :head_width].T
    return (context, grad_shard)


def solution(mesh):
    in_specs = (
        P("dp", "tm", None),
        P("dp", "tm", None),
        P("dp", None),
        P(("dp", "tm"), None),
        P("section", ("dp", "tm"), None),
        P("section", None, ("dp", "tm")),
        P(("dp", "tm"), "section"),
        P(("dp", "tm"), "section"),
        P(("dp", "tm"), "section"),
        P(("dp", "tm"), None),
    )
    out_specs = (P(("dp", "tm"), "section"), P("section", ("dp", "tm")))
    return jax.shard_map(
        per_device, mesh=mesh, in_specs=in_specs, out_specs=out_specs, check_vma=False
    )
```

time: 764 us -> 305 us (0.40)
  the two profiles are of different devices: /device:TPU:30 before, /device:TPU:2 now
where the time goes in v1:
time: 305 us; the launch traced here: 303 us
  starting transfers between devices  122 us (40%)
  waiting for transfers between devices  51.6 us (17%)
  Pallas kernels  42.2 us (14%)
  blocking collectives  41.5 us (14%)
  local copies, waits for them, and re-layouts  24.6 us (8%)
  between operations  15.1 us (5%)
  other arithmetic  5.21 us (2%)
    ppermute x14, starting transfers between devices, around(): lax.ppermute(value, axis, [(i, (i + step) % size) for i in range(size)])  52.3 us
    ppermute x5, starting transfers between devices, per_device(): left = lax.ppermute(last, 'tm', up)  29.3 us
    all_gather x1, blocking collectives, per_device(): everyone = lax.all_gather(pieces, 'tm', axis=0)  25.6 us
    ppermute x14, waiting for transfers between devices, around(): lax.ppermute(value, axis, [(i, (i + step) % size) for i in range(size)])  22 us
    unnamed x71, local copies, waits for them, and re-layouts  21 us
    ppermute x6, waiting for transfers between devices, per_device(): memory.append(lax.ppermute(finished, 'section', [(sections - 1, target)]))  18.2 us
    ppermute x8, starting transfers between devices, per_device(): pieces_w = ring + [lax.ppermute(value, 'tm', swap) for value in ring]  16.5 us
    all_to_all x1, blocking collectives, per_device(): grad = lax.all_to_all(grad, 'dp', 0, 0, tiled=True)  15.9 us
  transfers between devices with their start and end apart: 44, of which 13 were waited for; matrix products, arithmetic and copies ran while one was open for 4% of the time, Pallas kernels for 11%

profile of v1, /device:TPU:2, one launch (start us, length us, event | category | flops | bytes accessed | tf_op | source)
XLA Modules:
  0.0 302.7 jit_solution(16995877710736645589)
XLA Ops:
  11.4 4.3 %collective-permute-start = (bf16[10,2560]{1,0:T(8,128)(2,1)S(1)}, bf16[10,2560]{1,0:T(8,128)(2,1)S(1)}, u32[]{:S(2)}, u32[]{:S(2)}) collective-permute-start(bf16[10,2560]{1,0:T(8,128)(2,1)S(1)} %pad_maximum_fusion.1), channel_id=1, source_target_pairs={{0,64},{64,128},{128,192},{192,256},{256,320},{320,384},{384,448},... | collective-permute-start | bytes 153608 | tf_op jit(solution)/shard_map/ppermute | solution.py:292
  15.6 8.6 %collective-permute-start.4 = (bf16[10,2560]{1,0:T(8,128)(2,1)S(1)}, bf16[10,2560]{1,0:T(8,128)(2,1)S(1)}, u32[]{:S(2)}, u32[]{:S(2)}) collective-permute-start(bf16[10,2560]{1,0:T(8,128)(2,1)S(1)} %pad_maximum_fusion.1), channel_id=1, source_target_pairs={{0,448},{64,0},{128,64},{192,128},{256,192},{320,256},{384,320},{4... | collective-permute-start | bytes 153608 | tf_op jit(solution)/shard_map/ppermute | solution.py:292
  26.7 5.1 %collective-permute-start.5 = (bf16[10,2560]{1,0:T(8,128)(2,1)S(1)}, bf16[10,2560]{1,0:T(8,128)(2,1)S(1)}, u32[]{:S(2)}, u32[]{:S(2)}) collective-permute-start(bf16[10,2560]{1,0:T(8,128)(2,1)S(1)} %collective-permute-done.4), channel_id=1, source_target_pairs={{0,448},{64,0},{128,64},{192,128},{256,192},{320,256},{384,320},{4... | collective-permute-start | bytes 153608 | tf_op jit(solution)/shard_map/ppermute | solution.py:292
  34.2 5.2 %collective-permute-start.6 = (bf16[10,2560]{1,0:T(8,128)(2,1)S(1)}, bf16[10,2560]{1,0:T(8,128)(2,1)S(1)}, u32[]{:S(2)}, u32[]{:S(2)}) collective-permute-start(bf16[10,2560]{1,0:T(8,128)(2,1)S(1)} %collective-permute-done.5), channel_id=1, source_target_pairs={{0,448},{64,0},{128,64},{192,128},{256,192},{320,256},{384,320},{4... | collective-permute-start | bytes 153608 | tf_op jit(solution)/shard_map/ppermute | solution.py:292
  41.7 5.6 %collective-permute-done.3 = bf16[10,2560]{1,0:T(8,128)(2,1)S(1)} collective-permute-done((bf16[10,2560]{1,0:T(8,128)(2,1)S(1)}, bf16[10,2560]{1,0:T(8,128)(2,1)S(1)}, u32[]{:S(2)}, u32[]{:S(2)}) %collective-permute-start.3) | collective-permute-done | bytes 51232 | tf_op jit(solution)/shard_map/ppermute | solution.py:292
  48.6 3.6 %collective-permute-start.7 = (bf16[80,2560]{1,0:T(8,128)(2,1)S(1)}, bf16[80,2560]{1,0:T(8,128)(2,1)S(1)}, u32[]{:S(2)}, u32[]{:S(2)}) collective-permute-start(bf16[80,2560]{1,0:T(8,128)(2,1)S(1)} %concatenate.13.refs_0_), channel_id=1, source_target_pairs={{0,2},{1,3},{2,4},{3,5},{4,6},{5,7},{6,8},{7,9},{8,10},{9,11},{10,... | collective-permute-start | bytes 1228808 | tf_op jit(solution)/shard_map/ppermute | solution.py:292
  52.2 3.9 %collective-permute-start.11 = (bf16[80,2560]{1,0:T(8,128)(2,1)S(1)}, bf16[80,2560]{1,0:T(8,128)(2,1)S(1)}, u32[]{:S(2)}, u32[]{:S(2)}) collective-permute-start(bf16[80,2560]{1,0:T(8,128)(2,1)S(1)} %concatenate.13.refs_0_), channel_id=1, source_target_pairs={{0,14},{1,15},{2,0},{3,1},{4,2},{5,3},{6,4},{7,5},{8,6},{9,7},{10,... | collective-permute-start | bytes 1228808 | tf_op jit(solution)/shard_map/ppermute | solution.py:292
  56.0 4.4 %collective-permute-done.7.refs_1_ = bf16[80,2560]{1,0:T(8,128)(2,1)S(1)} collective-permute-done((bf16[80,2560]{1,0:T(8,128)(2,1)S(1)}, bf16[80,2560]{1,0:T(8,128)(2,1)S(1)}, u32[]{:S(2)}, u32[]{:S(2)}) %collective-permute-start.7) | collective-permute-done | bytes 409632 | tf_op jit(solution)/shard_map/ppermute | solution.py:292
  62.4 5.1 %collective-permute-start.12 = (bf16[80,2560]{1,0:T(8,128)(2,1)S(1)}, bf16[80,2560]{1,0:T(8,128)(2,1)}, u32[]{:S(2)}, u32[]{:S(2)}) collective-permute-start(bf16[80,2560]{1,0:T(8,128)(2,1)S(1)} %collective-permute-done.11.refs_5_), channel_id=1, source_target_pairs={{0,14},{1,15},{2,0},{3,1},{4,2},{5,3},{6,4},{7,5},{8,6},{9,7},{10,... | collective-permute-start | bytes 1228808 | tf_op jit(solution)/shard_map/ppermute | solution.py:292
  67.5 4.0 %collective-permute-done.8.refs_2_ = bf16[80,2560]{1,0:T(8,128)(2,1)S(1)} collective-permute-done((bf16[80,2560]{1,0:T(8,128)(2,1)S(1)}, bf16[80,2560]{1,0:T(8,128)(2,1)S(1)}, u32[]{:S(2)}, u32[]{:S(2)}) %collective-permute-start.8) | collective-permute-done | bytes 409632 | tf_op jit(solution)/shard_map/ppermute | solution.py:292
  71.5 1.9 collective-permute-start.9
  73.4 1.9 collective-permute-start.14
  75.3 2.4 collective-permute-start.19
  77.8 1.9 collective-permute-start.15
  79.7 5.1 %collective-permute-start.13 = (bf16[80,2560]{1,0:T(8,128)(2,1)}, bf16[80,2560]{1,0:T(8,128)(2,1)}, u32[]{:S(2)}, u32[]{:S(2)}) collective-permute-start(bf16[80,2560]{1,0:T(8,128)(2,1)} %collective-permute-done.12.refs_6_), channel_id=1, source_target_pairs={{0,14},{1,15},{2,0},{3,1},{4,2},{5,3},{6,4},{7,5},{8,6},{9,7},{10,... | collective-permute-start | bytes 1228808 | tf_op jit(solution)/shard_map/ppermute | solution.py:292
  84.9 1.9 collective-permute-start.10
  87.0 2.1 collective-permute-start.20
  89.2 2.2 collective-permute-start.16
  91.4 2.1 collective-permute-start.17
  93.5 4.2 %collective-permute-done.13.refs_7_ = bf16[80,2560]{1,0:T(8,128)(2,1)} collective-permute-done((bf16[80,2560]{1,0:T(8,128)(2,1)}, bf16[80,2560]{1,0:T(8,128)(2,1)}, u32[]{:S(2)}, u32[]{:S(2)}) %collective-permute-start.13) | collective-permute-done | bytes 409632 | tf_op jit(solution)/shard_map/ppermute | solution.py:292
  99.6 2.4 collective-permute-done.10.refs_4_
  102.0 1.9 collective-permute-start.18
  106.0 6.1 %join.1 = (bf16[1280,640]{1,0:T(8,128)(2,1)}, bf16[1280,1280]{1,0:T(8,128)(2,1)}, bf16[1280,640]{1,0:T(8,128)(2,1)}) custom-call(bf16[80,2560]{1,0:T(8,128)(2,1)} %copy-done.27, bf16[80,2560]{1,0:T(8,128)(2,1)} %copy-done.28, bf16[80,2560]{1,0:T(8,128)(2,1)} %copy-done.30, bf16[80,2560]{1,0:T(8,128)(2,1)} %collective-permute-done.9.refs_3_, ...), custom_call_target="tpu_custom_call" | custom-call | tf_op jit(solution)/shard_map/join/pallas_call | solution.py:353
  112.2 1.9 copy-done
  116.2 3.0 %collective-permute-start.22 = (bf16[64,1280]{1,0:T(8,128)(2,1)S(1)}, bf16[64,1280]{1,0:T(8,128)(2,1)S(1)}, u32[]{:S(2)}, u32[]{:S(2)}) collective-permute-start(bf16[64,1280]{1,0:T(8,128)(2,1)S(1)} %get-tuple-element.50.last_ref), channel_id=1, source_target_pairs={{0,1},{1,2},{2,3},{3,4},{4,5},{5,6},{6,7},{7,8},{8,9},{9,10},{10,1... | collective-permute-start | bytes 491528 | tf_op jit(solution)/shard_map/ppermute | solution.py:420
  123.8 2.4 layer_out.5
  126.2 3.4 %collective-permute-start.24 = (bf16[128,1280]{1,0:T(8,128)(2,1)}, bf16[128,1280]{1,0:T(8,128)(2,1)}, u32[]{:S(2)}, u32[]{:S(2)}) collective-permute-start(bf16[128,1280]{1,0:T(8,128)(2,1)} %layer_out.5), channel_id=1, source_target_pairs={{0,16},{16,32},{32,48},{1,17},{17,33},{33,49},{2,18},{18,34},{34,5... | collective-permute-start | bytes 983048 | tf_op jit(solution)/shard_map/ppermute | solution.py:444
  129.6 5.9 %collective-permute-done.24 = bf16[128,1280]{1,0:T(8,128)(2,1)} collective-permute-done((bf16[128,1280]{1,0:T(8,128)(2,1)}, bf16[128,1280]{1,0:T(8,128)(2,1)}, u32[]{:S(2)}, u32[]{:S(2)}) %collective-permute-start.24) | collective-permute-done | bytes 327712 | tf_op jit(solution)/shard_map/ppermute | solution.py:444
  138.7 7.1 %collective-permute-start.25 = (bf16[64,1280]{1,0:T(8,128)(2,1)S(1)}, bf16[64,1280]{1,0:T(8,128)(2,1)S(1)}, u32[]{:S(2)}, u32[]{:S(2)}) collective-permute-start(bf16[64,1280]{1,0:T(8,128)(2,1)S(1)} %get-tuple-element.58.last_ref), channel_id=1, source_target_pairs={{0,1},{1,2},{2,3},{3,4},{4,5},{5,6},{6,7},{7,8},{8,9},{9,10},{10,1... | collective-permute-start | bytes 491528 | tf_op jit(solution)/shard_map/ppermute | solution.py:420
  147.1 2.4 layer_out.6
  149.5 3.5 %collective-permute-start.27 = (bf16[128,1280]{1,0:T(8,128)(2,1)}, bf16[128,1280]{1,0:T(8,128)(2,1)}, u32[]{:S(2)}, u32[]{:S(2)}) collective-permute-start(bf16[128,1280]{1,0:T(8,128)(2,1)} %layer_out.6), channel_id=1, source_target_pairs={{0,16},{16,32},{32,48},{1,17},{17,33},{33,49},{2,18},{18,34},{34,5... | collective-permute-start | bytes 983048 | tf_op jit(solution)/shard_map/ppermute | solution.py:444
  154.2 4.9 %reshape.97.w_ref = bf16[1280,768]{1,0:T(8,128)(2,1)} reshape(bf16[128,10,768]{2,1,0:T(8,128)(2,1)} %all-gather.7.cloned.1.call-done) | data formatting | bytes 3932160
  168.1 7.1 %collective-permute-start.28 = (bf16[64,1280]{1,0:T(8,128)(2,1)S(1)}, bf16[64,1280]{1,0:T(8,128)(2,1)S(1)}, u32[]{:S(2)}, u32[]{:S(2)}) collective-permute-start(bf16[64,1280]{1,0:T(8,128)(2,1)S(1)} %get-tuple-element.65.last_ref), channel_id=1, source_target_pairs={{0,1},{1,2},{2,3},{3,4},{4,5},{5,6},{6,7},{7,8},{8,9},{9,10},{10,1... | collective-permute-start | bytes 491528 | tf_op jit(solution)/shard_map/ppermute | solution.py:420
  176.6 2.8 layer_out.7
  179.5 3.1 %collective-permute-start.30 = (bf16[128,1280]{1,0:T(8,128)(2,1)}, bf16[128,1280]{1,0:T(8,128)(2,1)}, u32[]{:S(2)}, u32[]{:S(2)}) collective-permute-start(bf16[128,1280]{1,0:T(8,128)(2,1)} %layer_out.7), channel_id=1, source_target_pairs={{0,16},{16,32},{32,48},{1,17},{17,33},{33,49},{2,18},{18,34},{34,5... | collective-permute-start | bytes 983048 | tf_op jit(solution)/shard_map/ppermute | solution.py:444
  182.7 2.5 copy-done.10
  186.7 2.2 queries.1.q_ref
  193.0 5.9 %collective-permute-start.31 = (bf16[64,1280]{1,0:T(8,128)(2,1)S(1)}, bf16[64,1280]{1,0:T(8,128)(2,1)S(1)}, u32[]{:S(2)}, u32[]{:S(2)}) collective-permute-start(bf16[64,1280]{1,0:T(8,128)(2,1)S(1)} %get-tuple-element.74.last_ref), channel_id=1, source_target_pairs={{0,1},{1,2},{2,3},{3,4},{4,5},{5,6},{6,7},{7,8},{8,9},{9,10},{10,1... | collective-permute-start | bytes 491528 | tf_op jit(solution)/shard_map/ppermute | solution.py:420
  200.2 2.9 layer_out.8.refs_0_
  203.1 2.2 collective-permute-start.36
  207.4 4.9 %collective-permute-done.36.x_ref = bf16[128,1280]{1,0:T(8,128)(2,1)S(1)} collective-permute-done((bf16[128,1280]{1,0:T(8,128)(2,1)}, bf16[128,1280]{1,0:T(8,128)(2,1)S(1)}, u32[]{:S(2)}, u32[]{:S(2)}) %collective-permute-start.36) | collective-permute-done | bytes 327712 | tf_op jit(solution)/shard_map/ppermute | solution.py:444
  214.3 6.1 %collective-permute-start.37 = (bf16[64,1280]{1,0:T(8,128)(2,1)S(1)}, bf16[64,1280]{1,0:T(8,128)(2,1)S(1)}, u32[]{:S(2)}, u32[]{:S(2)}) collective-permute-start(bf16[64,1280]{1,0:T(8,128)(2,1)S(1)} %get-tuple-element.81.last_ref), channel_id=1, source_target_pairs={{0,1},{1,2},{2,3},{3,4},{4,5},{5,6},{6,7},{7,8},{8,9},{9,10},{10,1... | collective-permute-start | bytes 491528 | tf_op jit(solution)/shard_map/ppermute | solution.py:420
  228.9 2.2 collective-permute-done.34.refs_2_
  231.1 15.9 %collective-permute-done.40.refs_6_ = bf16[128,1280]{1,0:T(8,128)(2,1)S(1)} collective-permute-done((bf16[128,1280]{1,0:T(8,128)(2,1)S(1)}, bf16[128,1280]{1,0:T(8,128)(2,1)S(1)}, u32[]{:S(2)}, u32[]{:S(2)}) %collective-permute-start.40) | collective-permute-done | bytes 327712 | tf_op jit(solution)/shard_map/ppermute | solution.py:442
  248.9 2.2 cross.1
  251.1 25.6 %all-gather = bf16[3584,128]{1,0:T(8,128)(2,1)S(1)} all-gather(bf16[224,128]{1,0:T(8,128)(2,1)S(1)} %cross.1), channel_id=2, replica_groups=mesh['dp'=8,'section'=4,'tm'=16] {'tm'}, dimensions={0}, use_global_device_ids=true | all-gather | bytes 974848 | tf_op jit(solution)/shard_map/all_gather | solution.py:454
  276.7 2.7 combine.1
  279.4 15.9 %all_to_all.5 = bf16[8,16,256]{2,1,0:T(8,128)(2,1)S(1)} all-to-all(bf16[8,16,256]{2,1,0:T(8,128)(2,1)S(1)} %get-tuple-element.87), channel_id=1, replica_groups=mesh['dp'=8,'section'=4,'tm'=16] {'dp'}, dimensions={0} | all-to-all | bytes 131072 | tf_op jit(solution)/shard_map/all_to_all | solution.py:468
  (155 shorter events, 63.1 us)
Async XLA Ops:
  7.2 79.8 %copy-start.34 = (s32[8]{0:T(128)S(1)}, s32[8]{0:T(128)}, u32[]{:S(2)}) copy-start(s32[8]{0:T(128)} %constant.125) | copy-start | bytes 100
  7.2 97.0 %copy-start.19 = (bf16[2,128,1280]{2,1,0:T(8,128)(2,1)S(1)}, bf16[2,128,1280]{2,1,0:T(8,128)(2,1)}, u32[]{:S(2)}) copy-start(bf16[2,128,1280]{2,1,0:T(8,128)(2,1)} %frames_ref.1) | copy-start | bytes 1966084
  7.2 147.0 %all-gather.7.cloned.1.call-start = ((), (), s32[]{:S(2)}) async-start(), calls=%async_computation.2 | async-start | bytes 3170304 | tf_op jit(solution)/shard_map/all_gather | solution.py:321
  8.7 174.0 %all-gather.5.cloned.1.call-start = ((), (), s32[]{:S(2)}) async-start(), calls=%async_computation.1 | async-start | bytes 5570560 | tf_op jit(solution)/shard_map/all_gather | solution.py:322
  11.4 13.4 %collective-permute-start = (bf16[10,2560]{1,0:T(8,128)(2,1)S(1)}, bf16[10,2560]{1,0:T(8,128)(2,1)S(1)}, u32[]{:S(2)}, u32[]{:S(2)}) collective-permute-start(bf16[10,2560]{1,0:T(8,128)(2,1)S(1)} %pad_maximum_fusion.1), channel_id=1, source_target_pairs={{0,64},{64,128},{128,192},{192,256},{256,320},{320,384},{384,448},... | collective-permute-start | bytes 153608 | tf_op jit(solution)/shard_map/ppermute | solution.py:292
  15.6 11.0 %collective-permute-start.4 = (bf16[10,2560]{1,0:T(8,128)(2,1)S(1)}, bf16[10,2560]{1,0:T(8,128)(2,1)S(1)}, u32[]{:S(2)}, u32[]{:S(2)}) collective-permute-start(bf16[10,2560]{1,0:T(8,128)(2,1)S(1)} %pad_maximum_fusion.1), channel_id=1, source_target_pairs={{0,448},{64,0},{128,64},{192,128},{256,192},{320,256},{384,320},{4... | collective-permute-start | bytes 153608 | tf_op jit(solution)/shard_map/ppermute | solution.py:292
  24.7 7.5 %collective-permute-start.1 = (bf16[10,2560]{1,0:T(8,128)(2,1)S(1)}, bf16[10,2560]{1,0:T(8,128)(2,1)S(1)}, u32[]{:S(2)}, u32[]{:S(2)}) collective-permute-start(bf16[10,2560]{1,0:T(8,128)(2,1)S(1)} %collective-permute-done), channel_id=1, source_target_pairs={{0,64},{64,128},{128,192},{192,256},{256,320},{320,384},{384,448},... | collective-permute-start | bytes 153608 | tf_op jit(solution)/shard_map/ppermute | solution.py:292
  26.7 7.5 %collective-permute-start.5 = (bf16[10,2560]{1,0:T(8,128)(2,1)S(1)}, bf16[10,2560]{1,0:T(8,128)(2,1)S(1)}, u32[]{:S(2)}, u32[]{:S(2)}) collective-permute-start(bf16[10,2560]{1,0:T(8,128)(2,1)S(1)} %collective-permute-done.4), channel_id=1, source_target_pairs={{0,448},{64,0},{128,64},{192,128},{256,192},{320,256},{384,320},{4... | collective-permute-start | bytes 153608 | tf_op jit(solution)/shard_map/ppermute | solution.py:292
  32.3 7.5 %collective-permute-start.2 = (bf16[10,2560]{1,0:T(8,128)(2,1)S(1)}, bf16[10,2560]{1,0:T(8,128)(2,1)S(1)}, u32[]{:S(2)}, u32[]{:S(2)}) collective-permute-start(bf16[10,2560]{1,0:T(8,128)(2,1)S(1)} %collective-permute-done.1), channel_id=1, source_target_pairs={{0,64},{64,128},{128,192},{192,256},{256,320},{320,384},{384,448},... | collective-permute-start | bytes 153608 | tf_op jit(solution)/shard_map/ppermute | solution.py:292
  34.2 7.5 %collective-permute-start.6 = (bf16[10,2560]{1,0:T(8,128)(2,1)S(1)}, bf16[10,2560]{1,0:T(8,128)(2,1)S(1)}, u32[]{:S(2)}, u32[]{:S(2)}) collective-permute-start(bf16[10,2560]{1,0:T(8,128)(2,1)S(1)} %collective-permute-done.5), channel_id=1, source_target_pairs={{0,448},{64,0},{128,64},{192,128},{256,192},{320,256},{384,320},{4... | collective-permute-start | bytes 153608 | tf_op jit(solution)/shard_map/ppermute | solution.py:292
  39.8 7.5 %collective-permute-start.3 = (bf16[10,2560]{1,0:T(8,128)(2,1)S(1)}, bf16[10,2560]{1,0:T(8,128)(2,1)S(1)}, u32[]{:S(2)}, u32[]{:S(2)}) collective-permute-start(bf16[10,2560]{1,0:T(8,128)(2,1)S(1)} %collective-permute-done.2), channel_id=1, source_target_pairs={{0,64},{64,128},{128,192},{192,256},{256,320},{320,384},{384,448},... | collective-permute-start | bytes 153608 | tf_op jit(solution)/shard_map/ppermute | solution.py:292
  48.6 57.4 %copy-start.27 = (bf16[80,2560]{1,0:T(8,128)(2,1)}, bf16[80,2560]{1,0:T(8,128)(2,1)S(1)}, u32[]{:S(2)}) copy-start(bf16[80,2560]{1,0:T(8,128)(2,1)S(1)} %concatenate.13.refs_0_) | copy-start | bytes 1228804
  48.6 11.8 %collective-permute-start.7 = (bf16[80,2560]{1,0:T(8,128)(2,1)S(1)}, bf16[80,2560]{1,0:T(8,128)(2,1)S(1)}, u32[]{:S(2)}, u32[]{:S(2)}) collective-permute-start(bf16[80,2560]{1,0:T(8,128)(2,1)S(1)} %concatenate.13.refs_0_), channel_id=1, source_target_pairs={{0,2},{1,3},{2,4},{3,5},{4,6},{5,7},{6,8},{7,9},{8,10},{9,11},{10,... | collective-permute-start | bytes 1228808 | tf_op jit(solution)/shard_map/ppermute | solution.py:292
  52.2 10.2 %collective-permute-start.11 = (bf16[80,2560]{1,0:T(8,128)(2,1)S(1)}, bf16[80,2560]{1,0:T(8,128)(2,1)S(1)}, u32[]{:S(2)}, u32[]{:S(2)}) collective-permute-start(bf16[80,2560]{1,0:T(8,128)(2,1)S(1)} %concatenate.13.refs_0_), channel_id=1, source_target_pairs={{0,14},{1,15},{2,0},{3,1},{4,2},{5,3},{6,4},{7,5},{8,6},{9,7},{10,... | collective-permute-start | bytes 1228808 | tf_op jit(solution)/shard_map/ppermute | solution.py:292
  60.4 45.5 %copy-start.28 = (bf16[80,2560]{1,0:T(8,128)(2,1)}, bf16[80,2560]{1,0:T(8,128)(2,1)S(1)}, u32[]{:S(2)}) copy-start(bf16[80,2560]{1,0:T(8,128)(2,1)S(1)} %collective-permute-done.7.refs_1_) | copy-start | bytes 1228804
  60.4 11.0 %collective-permute-start.8 = (bf16[80,2560]{1,0:T(8,128)(2,1)S(1)}, bf16[80,2560]{1,0:T(8,128)(2,1)S(1)}, u32[]{:S(2)}, u32[]{:S(2)}) collective-permute-start(bf16[80,2560]{1,0:T(8,128)(2,1)S(1)} %collective-permute-done.7.refs_1_), channel_id=1, source_target_pairs={{0,2},{1,3},{2,4},{3,5},{4,6},{5,7},{6,8},{7,9},{8,10},{9,11},{10,... | collective-permute-start | bytes 1228808 | tf_op jit(solution)/shard_map/ppermute | solution.py:292
  62.4 17.3 %collective-permute-start.12 = (bf16[80,2560]{1,0:T(8,128)(2,1)S(1)}, bf16[80,2560]{1,0:T(8,128)(2,1)}, u32[]{:S(2)}, u32[]{:S(2)}) collective-permute-start(bf16[80,2560]{1,0:T(8,128)(2,1)S(1)} %collective-permute-done.11.refs_5_), channel_id=1, source_target_pairs={{0,14},{1,15},{2,0},{3,1},{4,2},{5,3},{6,4},{7,5},{8,6},{9,7},{10,... | collective-permute-start | bytes 1228808 | tf_op jit(solution)/shard_map/ppermute | solution.py:292
  71.5 13.4 %collective-permute-start.9 = (bf16[80,2560]{1,0:T(8,128)(2,1)S(1)}, bf16[80,2560]{1,0:T(8,128)(2,1)}, u32[]{:S(2)}, u32[]{:S(2)}) collective-permute-start(bf16[80,2560]{1,0:T(8,128)(2,1)S(1)} %collective-permute-done.8.refs_2_), channel_id=1, source_target_pairs={{0,2},{1,3},{2,4},{3,5},{4,6},{5,7},{6,8},{7,9},{8,10},{9,11},{10,... | collective-permute-start | bytes 1228808 | tf_op jit(solution)/shard_map/ppermute | solution.py:292
  73.4 13.6 %collective-permute-start.14 = (bf16[80,2560]{1,0:T(8,128)(2,1)S(1)}, bf16[80,2560]{1,0:T(8,128)(2,1)S(1)}, u32[]{:S(2)}, u32[]{:S(2)}) collective-permute-start(bf16[80,2560]{1,0:T(8,128)(2,1)S(1)} %concatenate.13.refs_0_), channel_id=1, source_target_pairs={{0,1},{1,0},{2,3},{3,2},{4,5},{5,4},{6,7},{7,6},{8,9},{9,8},{10,11... | collective-permute-start | bytes 1228808 | tf_op jit(solution)/shard_map/ppermute | solution.py:313
  75.3 13.8 %collective-permute-start.19 = (bf16[80,2560]{1,0:T(8,128)(2,1)S(1)}, bf16[80,2560]{1,0:T(8,128)(2,1)}, u32[]{:S(2)}, u32[]{:S(2)}) collective-permute-start(bf16[80,2560]{1,0:T(8,128)(2,1)S(1)} %collective-permute-done.11.refs_5_), channel_id=1, source_target_pairs={{0,1},{1,0},{2,3},{3,2},{4,5},{5,4},{6,7},{7,6},{8,9},{9,8},{10,11... | collective-permute-start | bytes 1228808 | tf_op jit(solution)/shard_map/ppermute | solution.py:313
  77.8 13.6 %collective-permute-start.15 = (bf16[80,2560]{1,0:T(8,128)(2,1)S(1)}, bf16[80,2560]{1,0:T(8,128)(2,1)}, u32[]{:S(2)}, u32[]{:S(2)}) collective-permute-start(bf16[80,2560]{1,0:T(8,128)(2,1)S(1)} %collective-permute-done.7.refs_1_), channel_id=1, source_target_pairs={{0,1},{1,0},{2,3},{3,2},{4,5},{5,4},{6,7},{7,6},{8,9},{9,8},{10,11... | collective-permute-start | bytes 1228808 | tf_op jit(solution)/shard_map/ppermute | solution.py:313
  79.7 18.0 %collective-permute-start.13 = (bf16[80,2560]{1,0:T(8,128)(2,1)}, bf16[80,2560]{1,0:T(8,128)(2,1)}, u32[]{:S(2)}, u32[]{:S(2)}) collective-permute-start(bf16[80,2560]{1,0:T(8,128)(2,1)} %collective-permute-done.12.refs_6_), channel_id=1, source_target_pairs={{0,14},{1,15},{2,0},{3,1},{4,2},{5,3},{6,4},{7,5},{8,6},{9,7},{10,... | collective-permute-start | bytes 1228808 | tf_op jit(solution)/shard_map/ppermute | solution.py:292
  84.9 17.1 %collective-permute-start.10 = (bf16[80,2560]{1,0:T(8,128)(2,1)}, bf16[80,2560]{1,0:T(8,128)(2,1)}, u32[]{:S(2)}, u32[]{:S(2)}) collective-permute-start(bf16[80,2560]{1,0:T(8,128)(2,1)} %collective-permute-done.9.refs_3_), channel_id=1, source_target_pairs={{0,2},{1,3},{2,4},{3,5},{4,6},{5,7},{6,8},{7,9},{8,10},{9,11},{10,... | collective-permute-start | bytes 1228808 | tf_op jit(solution)/shard_map/ppermute | solution.py:292
  87.0 18.3 %collective-permute-start.20 = (bf16[80,2560]{1,0:T(8,128)(2,1)}, bf16[80,2560]{1,0:T(8,128)(2,1)}, u32[]{:S(2)}, u32[]{:S(2)}) collective-permute-start(bf16[80,2560]{1,0:T(8,128)(2,1)} %collective-permute-done.12.refs_6_), channel_id=1, source_target_pairs={{0,1},{1,0},{2,3},{3,2},{4,5},{5,4},{6,7},{7,6},{8,9},{9,8},{10,11... | collective-permute-start | bytes 1228808 | tf_op jit(solution)/shard_map/ppermute | solution.py:313
  89.2 16.2 %collective-permute-start.16 = (bf16[80,2560]{1,0:T(8,128)(2,1)S(1)}, bf16[80,2560]{1,0:T(8,128)(2,1)}, u32[]{:S(2)}, u32[]{:S(2)}) collective-permute-start(bf16[80,2560]{1,0:T(8,128)(2,1)S(1)} %collective-permute-done.8.refs_2_), channel_id=1, source_target_pairs={{0,1},{1,0},{2,3},{3,2},{4,5},{5,4},{6,7},{7,6},{8,9},{9,8},{10,11... | collective-permute-start | bytes 1228808 | tf_op jit(solution)/shard_map/ppermute | solution.py:313
  91.4 13.9 %collective-permute-start.17 = (bf16[80,2560]{1,0:T(8,128)(2,1)}, bf16[80,2560]{1,0:T(8,128)(2,1)}, u32[]{:S(2)}, u32[]{:S(2)}) collective-permute-start(bf16[80,2560]{1,0:T(8,128)(2,1)} %collective-permute-done.9.refs_3_), channel_id=1, source_target_pairs={{0,1},{1,0},{2,3},{3,2},{4,5},{5,4},{6,7},{7,6},{8,9},{9,8},{10,11... | collective-permute-start | bytes 1228808 | tf_op jit(solution)/shard_map/ppermute | solution.py:313
  97.7 7.7 %collective-permute-start.21 = (bf16[80,2560]{1,0:T(8,128)(2,1)}, bf16[80,2560]{1,0:T(8,128)(2,1)}, u32[]{:S(2)}, u32[]{:S(2)}) collective-permute-start(bf16[80,2560]{1,0:T(8,128)(2,1)} %collective-permute-done.13.refs_7_), channel_id=1, source_target_pairs={{0,1},{1,0},{2,3},{3,2},{4,5},{5,4},{6,7},{7,6},{8,9},{9,8},{10,11... | collective-permute-start | bytes 1228808 | tf_op jit(solution)/shard_map/ppermute | solution.py:313
  102.0 4.0 %collective-permute-start.18 = (bf16[80,2560]{1,0:T(8,128)(2,1)}, bf16[80,2560]{1,0:T(8,128)(2,1)}, u32[]{:S(2)}, u32[]{:S(2)}) collective-permute-start(bf16[80,2560]{1,0:T(8,128)(2,1)} %collective-permute-done.10.refs_4_), channel_id=1, source_target_pairs={{0,1},{1,0},{2,3},{3,2},{4,5},{5,4},{6,7},{7,6},{8,9},{9,8},{10,11... | collective-permute-start | bytes 1228808 | tf_op jit(solution)/shard_map/ppermute | solution.py:313
  114.9 5.8 %collective-permute-start.23 = (bf16[64,1280]{1,0:T(8,128)(2,1)S(1)}, bf16[64,1280]{1,0:T(8,128)(2,1)S(1)}, u32[]{:S(2)}, u32[]{:S(2)}) collective-permute-start(bf16[64,1280]{1,0:T(8,128)(2,1)S(1)} %get-tuple-element.49.first_ref), channel_id=1, source_target_pairs={{1,0},{2,1},{3,2},{4,3},{5,4},{6,5},{7,6},{8,7},{9,8},{10,9},{11,1... | collective-permute-start | bytes 491528 | tf_op jit(solution)/shard_map/ppermute | solution.py:421
  116.2 4.5 %collective-permute-start.22 = (bf16[64,1280]{1,0:T(8,128)(2,1)S(1)}, bf16[64,1280]{1,0:T(8,128)(2,1)S(1)}, u32[]{:S(2)}, u32[]{:S(2)}) collective-permute-start(bf16[64,1280]{1,0:T(8,128)(2,1)S(1)} %get-tuple-element.50.last_ref), channel_id=1, source_target_pairs={{0,1},{1,2},{2,3},{3,4},{4,5},{5,6},{6,7},{7,8},{8,9},{9,10},{10,1... | collective-permute-start | bytes 491528 | tf_op jit(solution)/shard_map/ppermute | solution.py:420
  126.2 9.3 %collective-permute-start.24 = (bf16[128,1280]{1,0:T(8,128)(2,1)}, bf16[128,1280]{1,0:T(8,128)(2,1)}, u32[]{:S(2)}, u32[]{:S(2)}) collective-permute-start(bf16[128,1280]{1,0:T(8,128)(2,1)} %layer_out.5), channel_id=1, source_target_pairs={{0,16},{16,32},{32,48},{1,17},{17,33},{33,49},{2,18},{18,34},{34,5... | collective-permute-start | bytes 983048 | tf_op jit(solution)/shard_map/ppermute | solution.py:444
  137.3 9.8 %collective-permute-start.26 = (bf16[64,1280]{1,0:T(8,128)(2,1)S(1)}, bf16[64,1280]{1,0:T(8,128)(2,1)S(1)}, u32[]{:S(2)}, u32[]{:S(2)}) collective-permute-start(bf16[64,1280]{1,0:T(8,128)(2,1)S(1)} %get-tuple-element.57.first_ref), channel_id=1, source_target_pairs={{1,0},{2,1},{3,2},{4,3},{5,4},{6,5},{7,6},{8,7},{9,8},{10,9},{11,1... | collective-permute-start | bytes 491528 | tf_op jit(solution)/shard_map/ppermute | solution.py:421
  138.7 8.4 %collective-permute-start.25 = (bf16[64,1280]{1,0:T(8,128)(2,1)S(1)}, bf16[64,1280]{1,0:T(8,128)(2,1)S(1)}, u32[]{:S(2)}, u32[]{:S(2)}) collective-permute-start(bf16[64,1280]{1,0:T(8,128)(2,1)S(1)} %get-tuple-element.58.last_ref), channel_id=1, source_target_pairs={{0,1},{1,2},{2,3},{3,4},{4,5},{5,6},{6,7},{7,8},{8,9},{9,10},{10,1... | collective-permute-start | bytes 491528 | tf_op jit(solution)/shard_map/ppermute | solution.py:420
  149.5 15.3 %collective-permute-start.27 = (bf16[128,1280]{1,0:T(8,128)(2,1)}, bf16[128,1280]{1,0:T(8,128)(2,1)}, u32[]{:S(2)}, u32[]{:S(2)}) collective-permute-start(bf16[128,1280]{1,0:T(8,128)(2,1)} %layer_out.6), channel_id=1, source_target_pairs={{0,16},{16,32},{32,48},{1,17},{17,33},{33,49},{2,18},{18,34},{34,5... | collective-permute-start | bytes 983048 | tf_op jit(solution)/shard_map/ppermute | solution.py:444
  166.7 9.9 %collective-permute-start.29 = (bf16[64,1280]{1,0:T(8,128)(2,1)S(1)}, bf16[64,1280]{1,0:T(8,128)(2,1)S(1)}, u32[]{:S(2)}, u32[]{:S(2)}) collective-permute-start(bf16[64,1280]{1,0:T(8,128)(2,1)S(1)} %get-tuple-element.64.first_ref), channel_id=1, source_target_pairs={{1,0},{2,1},{3,2},{4,3},{5,4},{6,5},{7,6},{8,7},{9,8},{10,9},{11,1... | collective-permute-start | bytes 491528 | tf_op jit(solution)/shard_map/ppermute | solution.py:421
  168.1 8.5 %collective-permute-start.28 = (bf16[64,1280]{1,0:T(8,128)(2,1)S(1)}, bf16[64,1280]{1,0:T(8,128)(2,1)S(1)}, u32[]{:S(2)}, u32[]{:S(2)}) collective-permute-start(bf16[64,1280]{1,0:T(8,128)(2,1)S(1)} %get-tuple-element.65.last_ref), channel_id=1, source_target_pairs={{0,1},{1,2},{2,3},{3,4},{4,5},{5,6},{6,7},{7,8},{8,9},{9,10},{10,1... | collective-permute-start | bytes 491528 | tf_op jit(solution)/shard_map/ppermute | solution.py:420
  179.5 10.2 %collective-permute-start.30 = (bf16[128,1280]{1,0:T(8,128)(2,1)}, bf16[128,1280]{1,0:T(8,128)(2,1)}, u32[]{:S(2)}, u32[]{:S(2)}) collective-permute-start(bf16[128,1280]{1,0:T(8,128)(2,1)} %layer_out.7), channel_id=1, source_target_pairs={{0,16},{16,32},{32,48},{1,17},{17,33},{33,49},{2,18},{18,34},{34,5... | collective-permute-start | bytes 983048 | tf_op jit(solution)/shard_map/ppermute | solution.py:444
  191.5 8.7 %collective-permute-start.32 = (bf16[64,1280]{1,0:T(8,128)(2,1)S(1)}, bf16[64,1280]{1,0:T(8,128)(2,1)S(1)}, u32[]{:S(2)}, u32[]{:S(2)}) collective-permute-start(bf16[64,1280]{1,0:T(8,128)(2,1)S(1)} %get-tuple-element.73.first_ref), channel_id=1, source_target_pairs={{1,0},{2,1},{3,2},{4,3},{5,4},{6,5},{7,6},{8,7},{9,8},{10,9},{11,1... | collective-permute-start | bytes 491528 | tf_op jit(solution)/shard_map/ppermute | solution.py:421
  193.0 7.2 %collective-permute-start.31 = (bf16[64,1280]{1,0:T(8,128)(2,1)S(1)}, bf16[64,1280]{1,0:T(8,128)(2,1)S(1)}, u32[]{:S(2)}, u32[]{:S(2)}) collective-permute-start(bf16[64,1280]{1,0:T(8,128)(2,1)S(1)} %get-tuple-element.74.last_ref), channel_id=1, source_target_pairs={{0,1},{1,2},{2,3},{3,4},{4,5},{5,6},{6,7},{7,8},{8,9},{9,10},{10,1... | collective-permute-start | bytes 491528 | tf_op jit(solution)/shard_map/ppermute | solution.py:420
  203.1 9.2 %collective-permute-start.36 = (bf16[128,1280]{1,0:T(8,128)(2,1)}, bf16[128,1280]{1,0:T(8,128)(2,1)S(1)}, u32[]{:S(2)}, u32[]{:S(2)}) collective-permute-start(bf16[128,1280]{1,0:T(8,128)(2,1)} %layer_out.8.refs_0_), channel_id=1, source_target_pairs={{0,16},{16,32},{32,48},{1,17},{17,33},{33,49},{2,18},{18,34},{34,5... | collective-permute-start | bytes 983048 | tf_op jit(solution)/shard_map/ppermute | solution.py:444
  205.3 22.1 %collective-permute-start.35 = (bf16[128,1280]{1,0:T(8,128)(2,1)}, bf16[128,1280]{1,0:T(8,128)(2,1)S(1)}, u32[]{:S(2)}, u32[]{:S(2)}) collective-permute-start(bf16[128,1280]{1,0:T(8,128)(2,1)} %layer_out.8.refs_0_), channel_id=1, source_target_pairs={{48,32},{49,33},{50,34},{51,35},{52,36},{53,37},{54,38},{55,39},{5... | collective-permute-start | bytes 983048 | tf_op jit(solution)/shard_map/ppermute | solution.py:442
  213.0 10.7 %collective-permute-start.38 = (bf16[64,1280]{1,0:T(8,128)(2,1)S(1)}, bf16[64,1280]{1,0:T(8,128)(2,1)S(1)}, u32[]{:S(2)}, u32[]{:S(2)}) collective-permute-start(bf16[64,1280]{1,0:T(8,128)(2,1)S(1)} %get-tuple-element.80.first_ref), channel_id=1, source_target_pairs={{1,0},{2,1},{3,2},{4,3},{5,4},{6,5},{7,6},{8,7},{9,8},{10,9},{11,1... | collective-permute-start | bytes 491528 | tf_op jit(solution)/shard_map/ppermute | solution.py:421
  214.3 9.4 %collective-permute-start.37 = (bf16[64,1280]{1,0:T(8,128)(2,1)S(1)}, bf16[64,1280]{1,0:T(8,128)(2,1)S(1)}, u32[]{:S(2)}, u32[]{:S(2)}) collective-permute-start(bf16[64,1280]{1,0:T(8,128)(2,1)S(1)} %get-tuple-element.81.last_ref), channel_id=1, source_target_pairs={{0,1},{1,2},{2,3},{3,4},{4,5},{5,6},{6,7},{7,8},{8,9},{9,10},{10,1... | collective-permute-start | bytes 491528 | tf_op jit(solution)/shard_map/ppermute | solution.py:420
  220.4 10.7 %collective-permute-start.34 = (bf16[128,1280]{1,0:T(8,128)(2,1)}, bf16[128,1280]{1,0:T(8,128)(2,1)S(1)}, u32[]{:S(2)}, u32[]{:S(2)}) collective-permute-start(bf16[128,1280]{1,0:T(8,128)(2,1)} %layer_out.8.refs_0_), channel_id=1, source_target_pairs={{48,16},{49,17},{50,18},{51,19},{52,20},{53,21},{54,22},{55,23},{5... | collective-permute-start | bytes 983048 | tf_op jit(solution)/shard_map/ppermute | solution.py:442
  221.7 9.4 %collective-permute-start.33 = (bf16[128,1280]{1,0:T(8,128)(2,1)}, bf16[128,1280]{1,0:T(8,128)(2,1)S(1)}, u32[]{:S(2)}, u32[]{:S(2)}) collective-permute-start(bf16[128,1280]{1,0:T(8,128)(2,1)} %layer_out.8.refs_0_), channel_id=1, source_target_pairs={{48,0},{49,1},{50,2},{51,3},{52,4},{53,5},{54,6},{55,7},{56,8},{57... | collective-permute-start | bytes 983048 | tf_op jit(solution)/shard_map/ppermute | solution.py:442
  225.4 5.7 %collective-permute-start.41 = (bf16[128,1280]{1,0:T(8,128)(2,1)S(1)}, bf16[128,1280]{1,0:T(8,128)(2,1)S(1)}, u32[]{:S(2)}, u32[]{:S(2)}) collective-permute-start(bf16[128,1280]{1,0:T(8,128)(2,1)S(1)} %layer_out.9.refs_4_), channel_id=1, source_target_pairs={{48,32},{49,33},{50,34},{51,35},{52,36},{53,37},{54,38},{55,39},{5... | collective-permute-start | bytes 983048 | tf_op jit(solution)/shard_map/ppermute | solution.py:442
  226.1 21.0 %collective-permute-start.40 = (bf16[128,1280]{1,0:T(8,128)(2,1)S(1)}, bf16[128,1280]{1,0:T(8,128)(2,1)S(1)}, u32[]{:S(2)}, u32[]{:S(2)}) collective-permute-start(bf16[128,1280]{1,0:T(8,128)(2,1)S(1)} %layer_out.9.refs_4_), channel_id=1, source_target_pairs={{48,16},{49,17},{50,18},{51,19},{52,20},{53,21},{54,22},{55,23},{5... | collective-permute-start | bytes 983048 | tf_op jit(solution)/shard_map/ppermute | solution.py:442
  228.2 18.9 %collective-permute-start.39 = (bf16[128,1280]{1,0:T(8,128)(2,1)S(1)}, bf16[128,1280]{1,0:T(8,128)(2,1)S(1)}, u32[]{:S(2)}, u32[]{:S(2)}) collective-permute-start(bf16[128,1280]{1,0:T(8,128)(2,1)S(1)} %layer_out.9.refs_4_), channel_id=1, source_target_pairs={{48,0},{49,1},{50,2},{51,3},{52,4},{53,5},{54,6},{55,7},{56,8},{57... | collective-permute-start | bytes 983048 | tf_op jit(solution)/shard_map/ppermute | solution.py:442
  (31 other events, 258.1 us)
Sparse Core Ops, SparseCore 0:
  11.7 89.5 all-gather.6
  103.4 43.9 all-gather.4

commit v2 on v1

--- a/solution.py
+++ b/solution.py
@@ -57,12 +57,13 @@
         copy.wait()
 
 
-def kv_kernel(x_ref, w_ref, n_ref, first_ref, last_ref):
+def kv_kernel(place_ref, x_ref, w_ref, n_ref, a_ref, b_ref):
     n = normed_rows(x_ref[...])
     n_ref[...] = n
     kv = matmul(n, w_ref[...]).astype(BF16)
-    first_ref[...] = kv[:BLK]
-    last_ref[...] = kv[BLK:]
+    even = place_ref[2] % 2 == 0
+    a_ref[...] = jnp.where(even, kv[BLK:], kv[:BLK])
+    b_ref[...] = jnp.where(even, kv[:BLK], kv[BLK:])
 
 
 def allowed_of(moment, halo, place_ref, mask_ref):
@@ -70,8 +71,9 @@
     shard = place_ref[2]
     row = lax.broadcasted_iota(jnp.int32, (4 * BLK, 2 * BLK), 0)
     col = lax.broadcasted_iota(jnp.int32, (4 * BLK, 2 * BLK), 1)
-    same = ((row // BLK) % 2 == 0) == (col < BLK)
     low_row = (row // BLK) % 2 == 0
+    block = jnp.where(shard % 2 == 1, col // BLK, 1 - col // BLK)
+    same = (row // BLK) % 2 == block
     if halo:
         before = jnp.where(shard > 0, mask_ref[base], 0)
         after = jnp.where(shard < place_ref[5], mask_ref[base + 3], 0)
@@ -97,7 +99,7 @@
 
 
 def own_kernel(
-    moment, place_ref, mask_ref, n_ref, first_ref, last_ref, w_ref, q_ref, num_ref, den_ref
+    moment, place_ref, mask_ref, n_ref, a_ref, b_ref, w_ref, q_ref, num_ref, den_ref
 ):
     width = q_ref.shape[1]
     allowed = allowed_of(moment, False, place_ref, mask_ref)
@@ -106,13 +108,13 @@
     for lane in range(0, width, 2 * HD):
         cols = slice(lane, lane + 2 * HD)
         vcols = slice(width + lane, width + lane + 2 * HD)
-        k = jnp.concatenate([first_ref[:, cols], last_ref[:, cols]], axis=0)
-        v = jnp.concatenate([first_ref[:, vcols], last_ref[:, vcols]], axis=0)
+        k = jnp.concatenate([a_ref[:, cols], b_ref[:, cols]], axis=0)
+        v = jnp.concatenate([a_ref[:, vcols], b_ref[:, vcols]], axis=0)
         num_ref[:, cols], den_ref[:, cols] = pair_attention(q[:, cols], k, v, allowed)
 
 
 def out_kernel(
-    moment, place_ref, mask_ref, q_ref, num_ref, den_ref, left_ref, right_ref, x_ref, w_ref,
+    moment, place_ref, mask_ref, q_ref, num_ref, den_ref, a_ref, b_ref, x_ref, w_ref,
     o_ref, ctx_ref
 ):
     width = q_ref.shape[1]
@@ -120,8 +122,8 @@
     for lane in range(0, width, 2 * HD):
         cols = slice(lane, lane + 2 * HD)
         vcols = slice(width + lane, width + lane + 2 * HD)
-        k = jnp.concatenate([left_ref[:, cols], right_ref[:, cols]], axis=0)
-        v = jnp.concatenate([left_ref[:, vcols], right_ref[:, vcols]], axis=0)
+        k = jnp.concatenate([a_ref[:, cols], b_ref[:, cols]], axis=0)
+        v = jnp.concatenate([a_ref[:, vcols], b_ref[:, vcols]], axis=0)
         num, den = pair_attention(q_ref[:, cols], k, v, allowed)
         ctx_ref[:, cols] = ((num + num_ref[:, cols]) / (den + den_ref[:, cols])).astype(BF16)
     update = matmul_nt(ctx_ref[...], w_ref[...])
@@ -293,13 +295,22 @@
 
     group = lax.axis_index("dp")
     own = jnp.concatenate([enc_qkv[0], enc_out[0].T], axis=1)
-    blocks, steps = [own], [0]
-    for step, count in ((1, groups // 2), (-1, (groups - 1) // 2)):
-        moving = own
-        for hop in range(count):
-            moving = around(moving, "dp", groups, step)
-            blocks.append(moving)
-            steps.append(step * (hop + 1))
+    def pairs(size, wrap):
+        even = [(i, i ^ 1) for i in range(size)]
+        odd = [(i, i - 1 if i % 2 == 0 else i + 1) for i in range(size)]
+        if wrap:
+            return even, [(i, j % size) for i, j in odd]
+        return even, [(i, j) for i, j in odd if 0 <= j < size]
+
+    swaps = pairs(groups, True)
+    first = lax.ppermute(own, "dp", swaps[0])
+    blocks, steps = [own, first], [0, 1]
+    moving = jnp.stack([own, first])
+    for turn in range(2, groups // 2 + 1):
+        moving = lax.ppermute(moving, "dp", swaps[(turn - 1) % 2])
+        blocks += [moving[0], moving[1]]
+        sign = 1 if turn % 2 else -1
+        steps += [sign * (turn - 1), sign * turn]
     block = jnp.concatenate(blocks, axis=0)
     chips = shards // 2
     ring, source = [block], [shard]
@@ -313,7 +324,8 @@
     pieces_w = ring + [lax.ppermute(value, "tm", swap) for value in ring]
     source = jnp.stack(source + [place ^ 1 for place in source])
     each = model // (groups * shards)
-    slots = (group - jnp.array(steps)) % groups
+    side = 1 - 2 * (group % 2)
+    slots = (group + side * jnp.array(steps)) % groups
     order = (slots[None, :, None] * shards + source[:, None, None]) * each + jnp.arange(each)
     order = order.reshape(-1).astype(jnp.int32)
 
@@ -343,8 +355,7 @@
         name="order",
     )(order.reshape(1, -1), frames)
 
-    up = [(i, i + 1) for i in range(shards - 1)]
-    down = [(i + 1, i) for i in range(shards - 1)]
+    halos = pairs(shards, False)
     onward = [(i, i + 1) for i in range(sections - 1)]
     rows = frames.shape[1]
     tokens = dec_states.shape[0] // MB
@@ -360,6 +371,8 @@
         name="join",
     )(*pieces_w)
     for moment in range(MB + sections - 1):
+        if moment == 1:
+            carried, cross = lax.optimization_barrier((carried, cross))
         if 0 < moment < MB:
             carried = jnp.where(section == 0, inputs[moment], carried)
         if moment == 2:
@@ -409,16 +422,16 @@
             )(place, tokens_all)
             carried, cot_cols = lax.optimization_barrier((carried, cot_cols))
 
-        n, first, last = pl.pallas_call(
+        n, near, far = pl.pallas_call(
             kv_kernel,
             out_shape=(shape((rows, model)), shape((BLK, 2 * width)), shape((BLK, 2 * width))),
-            in_specs=[VMEM, VMEM],
+            in_specs=[SMEM, VMEM, VMEM],
             out_specs=(VMEM, VMEM, VMEM),
             compiler_params=PARAMS,
             name="keys_values",
-        )(carried, w_kv)
-        left = lax.ppermute(last, "tm", up)
-        right = lax.ppermute(first, "tm", down)
+        )(place, carried, w_kv)
+        from_near = lax.ppermute(near, "tm", halos[0])
+        from_far = lax.ppermute(far, "tm", halos[1])
         q, num, den = pl.pallas_call(
             functools.partial(own_kernel, moment),
             out_shape=(shape((rows, width)), shape((rows, width), F32), shape((rows, width), F32)),
@@ -426,7 +439,7 @@
             out_specs=(VMEM, VMEM, VMEM),
             compiler_params=PARAMS,
             name="own_blocks",
-        )(place, mask, n, first, last, w_q)
+        )(place, mask, n, near, far, w_q)
         finished = pl.pallas_call(
             functools.partial(out_kernel, moment),
             out_shape=shape((rows, model)),
@@ -435,7 +448,7 @@
             scratch_shapes=[pltpu.VMEM((rows, width), BF16)],
             compiler_params=PARAMS,
             name="layer_out",
-        )(place, mask, q, num, den, left, right, carried, w_out)
+        )(place, mask, q, num, den, from_near, from_far, carried, w_out)
         if moment >= sections - 1:
             memory.append(finished)
             for target in (0, 1, 2):

time: 305 us -> 309 us (1.013)
  the two profiles are of different devices: /device:TPU:2 before, /device:TPU:4 now
where the time goes in v2:
time: 309 us; the launch traced here: 307 us
  starting transfers between devices  118 us (38%)
  waiting for transfers between devices  55.3 us (18%)
  Pallas kernels  45.6 us (15%)
  blocking collectives  43.6 us (14%)
  local copies, waits for them, and re-layouts  24.1 us (8%)
  between operations  15.1 us (5%)
  other arithmetic  5.25 us (2%)
    ppermute x5, starting transfers between devices, per_device(): from_near = lax.ppermute(near, 'tm', halos[0])  36.7 us
    all_gather x1, blocking collectives, per_device(): everyone = lax.all_gather(pieces, 'tm', axis=0)  32 us
    ppermute x7, starting transfers between devices, around(): lax.ppermute(value, axis, [(i, (i + step) % size) for i in range(size)])  23.4 us
    ppermute x6, waiting for transfers between devices, per_device(): memory.append(lax.ppermute(finished, 'section', [(sections - 1, target)]))  19.6 us
    ppermute x3, starting transfers between devices, per_device(): moving = lax.ppermute(moving, 'dp', swaps[(turn - 1) % 2])  17.6 us
    ppermute x8, starting transfers between devices, per_device(): pieces_w = ring + [lax.ppermute(value, 'tm', swap) for value in ring]  16.4 us
    unnamed x72, local copies, waits for them, and re-layouts  15.4 us
    ppermute x7, waiting for transfers between devices, around(): lax.ppermute(value, axis, [(i, (i + step) % size) for i in range(size)])  14.7 us
  transfers between devices with their start and end apart: 41, of which 14 were waited for; matrix products, arithmetic and copies ran while one was open for 4% of the time, Pallas kernels for 12%

profile of v2, /device:TPU:4, one launch (start us, length us, event | category | flops | bytes accessed | tf_op | source)
XLA Modules:
  0.0 306.8 jit_solution(16480814039758727648)
XLA Ops:
  11.4 4.3 %collective-permute-start = (bf16[10,2560]{1,0:T(8,128)(2,1)S(1)}, bf16[10,2560]{1,0:T(8,128)(2,1)S(1)}, u32[]{:S(2)}, u32[]{:S(2)}) collective-permute-start(bf16[10,2560]{1,0:T(8,128)(2,1)S(1)} %get-tuple-element.99), channel_id=1, source_target_pairs={{0,64},{64,0},{128,192},{192,128},{256,320},{320,256},{384,448},{4... | collective-permute-start | bytes 153608 | tf_op jit(solution)/shard_map/ppermute | solution.py:306
  15.6 2.4 collective-permute-done
  18.1 10.6 %collective-permute-start.1 = (bf16[2,10,2560]{2,1,0:T(8,128)(2,1)S(1)}, bf16[2,10,2560]{2,1,0:T(8,128)(2,1)S(1)}, u32[]{:S(2)}, u32[]{:S(2)}) collective-permute-start(bf16[2,10,2560]{2,1,0:T(8,128)(2,1)S(1)} %pad_maximum_fusion.1), channel_id=1, source_target_pairs={{0,448},{64,128},{128,64},{192,256},{256,192},{320,384},{384,320},... | collective-permute-start | bytes 307208 | tf_op jit(solution)/shard_map/ppermute | solution.py:310
  28.7 3.3 %collective-permute-done.1 = bf16[2,10,2560]{2,1,0:T(8,128)(2,1)S(1)} collective-permute-done((bf16[2,10,2560]{2,1,0:T(8,128)(2,1)S(1)}, bf16[2,10,2560]{2,1,0:T(8,128)(2,1)S(1)}, u32[]{:S(2)}, u32[]{:S(2)}) %collective-permute-start.1) | collective-permute-done | bytes 102432 | tf_op jit(solution)/shard_map/ppermute | solution.py:310
  33.9 5.3 %collective-permute-done.2 = bf16[2,10,2560]{2,1,0:T(8,128)(2,1)S(1)} collective-permute-done((bf16[2,10,2560]{2,1,0:T(8,128)(2,1)S(1)}, bf16[2,10,2560]{2,1,0:T(8,128)(2,1)S(1)}, u32[]{:S(2)}, u32[]{:S(2)}) %collective-permute-start.2) | collective-permute-done | bytes 102432 | tf_op jit(solution)/shard_map/ppermute | solution.py:310
  39.2 5.1 %collective-permute-start.3 = (bf16[2,10,2560]{2,1,0:T(8,128)(2,1)S(1)}, bf16[2,10,2560]{2,1,0:T(8,128)(2,1)S(1)}, u32[]{:S(2)}, u32[]{:S(2)}) collective-permute-start(bf16[2,10,2560]{2,1,0:T(8,128)(2,1)S(1)} %collective-permute-done.2), channel_id=1, source_target_pairs={{0,448},{64,128},{128,64},{192,256},{256,192},{320,384},{384,320},... | collective-permute-start | bytes 307208 | tf_op jit(solution)/shard_map/ppermute | solution.py:310
  44.4 3.3 %collective-permute-done.3 = bf16[2,10,2560]{2,1,0:T(8,128)(2,1)S(1)} collective-permute-done((bf16[2,10,2560]{2,1,0:T(8,128)(2,1)S(1)}, bf16[2,10,2560]{2,1,0:T(8,128)(2,1)S(1)}, u32[]{:S(2)}, u32[]{:S(2)}) %collective-permute-start.3) | collective-permute-done | bytes 102432 | tf_op jit(solution)/shard_map/ppermute | solution.py:310
  48.9 3.5 %collective-permute-start.4 = (bf16[80,2560]{1,0:T(8,128)(2,1)S(1)}, bf16[80,2560]{1,0:T(8,128)(2,1)S(1)}, u32[]{:S(2)}, u32[]{:S(2)}) collective-permute-start(bf16[80,2560]{1,0:T(8,128)(2,1)S(1)} %concatenate.13.refs_0_), channel_id=1, source_target_pairs={{0,2},{1,3},{2,4},{3,5},{4,6},{5,7},{6,8},{7,9},{8,10},{9,11},{10,... | collective-permute-start | bytes 1228808 | tf_op jit(solution)/shard_map/ppermute | solution.py:294
  52.5 3.9 %collective-permute-start.8 = (bf16[80,2560]{1,0:T(8,128)(2,1)S(1)}, bf16[80,2560]{1,0:T(8,128)(2,1)S(1)}, u32[]{:S(2)}, u32[]{:S(2)}) collective-permute-start(bf16[80,2560]{1,0:T(8,128)(2,1)S(1)} %concatenate.13.refs_0_), channel_id=1, source_target_pairs={{0,14},{1,15},{2,0},{3,1},{4,2},{5,3},{6,4},{7,5},{8,6},{9,7},{10,... | collective-permute-start | bytes 1228808 | tf_op jit(solution)/shard_map/ppermute | solution.py:294
  56.4 4.1 %collective-permute-done.4.refs_1_ = bf16[80,2560]{1,0:T(8,128)(2,1)S(1)} collective-permute-done((bf16[80,2560]{1,0:T(8,128)(2,1)S(1)}, bf16[80,2560]{1,0:T(8,128)(2,1)S(1)}, u32[]{:S(2)}, u32[]{:S(2)}) %collective-permute-start.4) | collective-permute-done | bytes 409632 | tf_op jit(solution)/shard_map/ppermute | solution.py:294
  62.4 5.1 %collective-permute-start.9 = (bf16[80,2560]{1,0:T(8,128)(2,1)S(1)}, bf16[80,2560]{1,0:T(8,128)(2,1)S(1)}, u32[]{:S(2)}, u32[]{:S(2)}) collective-permute-start(bf16[80,2560]{1,0:T(8,128)(2,1)S(1)} %collective-permute-done.8.refs_5_), channel_id=1, source_target_pairs={{0,14},{1,15},{2,0},{3,1},{4,2},{5,3},{6,4},{7,5},{8,6},{9,7},{10,... | collective-permute-start | bytes 1228808 | tf_op jit(solution)/shard_map/ppermute | solution.py:294
  67.5 4.0 %collective-permute-done.5.refs_2_ = bf16[80,2560]{1,0:T(8,128)(2,1)S(1)} collective-permute-done((bf16[80,2560]{1,0:T(8,128)(2,1)S(1)}, bf16[80,2560]{1,0:T(8,128)(2,1)S(1)}, u32[]{:S(2)}, u32[]{:S(2)}) %collective-permute-start.5) | collective-permute-done | bytes 409632 | tf_op jit(solution)/shard_map/ppermute | solution.py:294
  71.5 1.9 collective-permute-start.6
  73.4 1.9 collective-permute-start.11
  75.4 2.4 collective-permute-start.12
  77.8 1.9 collective-permute-start.16
  79.7 5.1 %collective-permute-start.10 = (bf16[80,2560]{1,0:T(8,128)(2,1)S(1)}, bf16[80,2560]{1,0:T(8,128)(2,1)}, u32[]{:S(2)}, u32[]{:S(2)}) collective-permute-start(bf16[80,2560]{1,0:T(8,128)(2,1)S(1)} %collective-permute-done.9.refs_6_), channel_id=1, source_target_pairs={{0,14},{1,15},{2,0},{3,1},{4,2},{5,3},{6,4},{7,5},{8,6},{9,7},{10,... | collective-permute-start | bytes 1228808 | tf_op jit(solution)/shard_map/ppermute | solution.py:294
  85.0 1.9 collective-permute-start.7
  87.2 2.0 collective-permute-start.13
  89.2 2.3 collective-permute-start.17
  91.5 2.0 collective-permute-start.14
  93.6 4.0 %collective-permute-done.10.refs_7_ = bf16[80,2560]{1,0:T(8,128)(2,1)} collective-permute-done((bf16[80,2560]{1,0:T(8,128)(2,1)S(1)}, bf16[80,2560]{1,0:T(8,128)(2,1)}, u32[]{:S(2)}, u32[]{:S(2)}) %collective-permute-start.10) | collective-permute-done | bytes 409632 | tf_op jit(solution)/shard_map/ppermute | solution.py:294
  99.5 2.5 collective-permute-done.7.refs_4_
  106.2 6.1 %join.1 = (bf16[1280,640]{1,0:T(8,128)(2,1)}, bf16[1280,1280]{1,0:T(8,128)(2,1)}, bf16[1280,640]{1,0:T(8,128)(2,1)}) custom-call(bf16[80,2560]{1,0:T(8,128)(2,1)} %copy-done.27, bf16[80,2560]{1,0:T(8,128)(2,1)} %copy-done.28, bf16[80,2560]{1,0:T(8,128)(2,1)} %copy-done.30, bf16[80,2560]{1,0:T(8,128)(2,1)} %collective-permute-done.6.refs_3_, ...), custom_call_target="tpu_custom_call" | custom-call | tf_op jit(solution)/shard_map/join/pallas_call | solution.py:364
  112.3 1.9 copy-done
  114.3 2.1 keys_values.5
  117.1 2.7 collective-permute-start.19
  124.0 2.8 layer_out.5
  126.8 3.1 %collective-permute-start.21 = (bf16[128,1280]{1,0:T(8,128)(2,1)}, bf16[128,1280]{1,0:T(8,128)(2,1)}, u32[]{:S(2)}, u32[]{:S(2)}) collective-permute-start(bf16[128,1280]{1,0:T(8,128)(2,1)} %layer_out.5), channel_id=1, source_target_pairs={{0,16},{16,32},{32,48},{1,17},{17,33},{33,49},{2,18},{18,34},{34,5... | collective-permute-start | bytes 983048 | tf_op jit(solution)/shard_map/ppermute | solution.py:457
  130.0 5.1 %reshape.97.w_ref = bf16[1280,768]{1,0:T(8,128)(2,1)} reshape(bf16[128,10,768]{2,1,0:T(8,128)(2,1)} %all-gather.7.cloned.1.call-done) | data formatting | bytes 3932160 | tf_op jit(solution)/shard_map/optimization_barrier | solution.py:375
  138.5 7.5 %collective-permute-start.22 = (bf16[64,1280]{1,0:T(8,128)(2,1)S(1)}, bf16[64,1280]{1,0:T(8,128)(2,1)S(1)}, u32[]{:S(2)}, u32[]{:S(2)}) collective-permute-start(bf16[64,1280]{1,0:T(8,128)(2,1)S(1)} %get-tuple-element.60.a_ref), channel_id=1, source_target_pairs={{0,1},{1,0},{2,3},{3,2},{4,5},{5,4},{6,7},{7,6},{8,9},{9,8},{10,11... | collective-permute-start | bytes 491528 | tf_op jit(solution)/shard_map/ppermute | solution.py:433
  147.9 2.4 layer_out.6
  150.3 3.2 %collective-permute-start.24 = (bf16[128,1280]{1,0:T(8,128)(2,1)}, bf16[128,1280]{1,0:T(8,128)(2,1)}, u32[]{:S(2)}, u32[]{:S(2)}) collective-permute-start(bf16[128,1280]{1,0:T(8,128)(2,1)} %layer_out.6), channel_id=1, source_target_pairs={{0,16},{16,32},{32,48},{1,17},{17,33},{33,49},{2,18},{18,34},{34,5... | collective-permute-start | bytes 983048 | tf_op jit(solution)/shard_map/ppermute | solution.py:457
  162.2 8.6 %collective-permute-start.25 = (bf16[64,1280]{1,0:T(8,128)(2,1)S(1)}, bf16[64,1280]{1,0:T(8,128)(2,1)S(1)}, u32[]{:S(2)}, u32[]{:S(2)}) collective-permute-start(bf16[64,1280]{1,0:T(8,128)(2,1)S(1)} %get-tuple-element.68.a_ref), channel_id=1, source_target_pairs={{0,1},{1,0},{2,3},{3,2},{4,5},{5,4},{6,7},{7,6},{8,9},{9,8},{10,11... | collective-permute-start | bytes 491528 | tf_op jit(solution)/shard_map/ppermute | solution.py:433
  172.9 2.8 layer_out.7
  177.8 2.5 copy-done.10
  181.8 2.2 queries.1.q_ref
  185.0 1.9 keys_values.8
  186.9 10.5 %collective-permute-start.28 = (bf16[64,1280]{1,0:T(8,128)(2,1)S(1)}, bf16[64,1280]{1,0:T(8,128)(2,1)S(1)}, u32[]{:S(2)}, u32[]{:S(2)}) collective-permute-start(bf16[64,1280]{1,0:T(8,128)(2,1)S(1)} %get-tuple-element.77.a_ref), channel_id=1, source_target_pairs={{0,1},{1,0},{2,3},{3,2},{4,5},{5,4},{6,7},{7,6},{8,9},{9,8},{10,11... | collective-permute-start | bytes 491528 | tf_op jit(solution)/shard_map/ppermute | solution.py:433
  199.4 2.9 layer_out.8.refs_0_
  206.3 5.2 %collective-permute-done.33.x_ref = bf16[128,1280]{1,0:T(8,128)(2,1)S(1)} collective-permute-done((bf16[128,1280]{1,0:T(8,128)(2,1)}, bf16[128,1280]{1,0:T(8,128)(2,1)S(1)}, u32[]{:S(2)}, u32[]{:S(2)}) %collective-permute-start.33) | collective-permute-done | bytes 327712 | tf_op jit(solution)/shard_map/ppermute | solution.py:457
  212.8 7.4 %collective-permute-start.34 = (bf16[64,1280]{1,0:T(8,128)(2,1)S(1)}, bf16[64,1280]{1,0:T(8,128)(2,1)S(1)}, u32[]{:S(2)}, u32[]{:S(2)}) collective-permute-start(bf16[64,1280]{1,0:T(8,128)(2,1)S(1)} %get-tuple-element.84.a_ref), channel_id=1, source_target_pairs={{0,1},{1,0},{2,3},{3,2},{4,5},{5,4},{6,7},{7,6},{8,9},{9,8},{10,11... | collective-permute-start | bytes 491528 | tf_op jit(solution)/shard_map/ppermute | solution.py:433
  229.4 5.6 %collective-permute-done.32.refs_3_ = bf16[128,1280]{1,0:T(8,128)(2,1)S(1)} collective-permute-done((bf16[128,1280]{1,0:T(8,128)(2,1)}, bf16[128,1280]{1,0:T(8,128)(2,1)S(1)}, u32[]{:S(2)}, u32[]{:S(2)}) %collective-permute-start.32) | collective-permute-done | bytes 327712 | tf_op jit(solution)/shard_map/ppermute | solution.py:455
  235.0 14.0 %collective-permute-done.38.refs_7_ = bf16[128,1280]{1,0:T(8,128)(2,1)S(1)} collective-permute-done((bf16[128,1280]{1,0:T(8,128)(2,1)S(1)}, bf16[128,1280]{1,0:T(8,128)(2,1)S(1)}, u32[]{:S(2)}, u32[]{:S(2)}) %collective-permute-start.38) | collective-permute-done | bytes 327712 | tf_op jit(solution)/shard_map/ppermute | solution.py:455
  250.9 2.2 cross.1
  253.1 32.0 %all-gather = bf16[3584,128]{1,0:T(8,128)(2,1)S(1)} all-gather(bf16[224,128]{1,0:T(8,128)(2,1)S(1)} %cross.1), channel_id=2, replica_groups=mesh['dp'=8,'section'=4,'tm'=16] {'tm'}, dimensions={0}, use_global_device_ids=true | all-gather | bytes 974848 | tf_op jit(solution)/shard_map/all_gather | solution.py:467
  285.1 2.7 combine.1
  287.8 11.6 %all_to_all.5 = bf16[8,16,256]{2,1,0:T(8,128)(2,1)S(1)} all-to-all(bf16[8,16,256]{2,1,0:T(8,128)(2,1)S(1)} %get-tuple-element.91), channel_id=1, replica_groups=mesh['dp'=8,'section'=4,'tm'=16] {'dp'}, dimensions={0} | all-to-all | bytes 131072 | tf_op jit(solution)/shard_map/all_to_all | solution.py:481
  (155 shorter events, 59.8 us)
Async XLA Ops:
  7.2 122.8 %all-gather.7.cloned.1.call-start = ((), (), s32[]{:S(2)}) async-start(), calls=%async_computation.2 | async-start | bytes 3170304 | tf_op jit(solution)/shard_map/all_gather | solution.py:333
  8.6 78.6 %copy-start.35 = (s32[8]{0:T(128)S(1)}, s32[8]{0:T(128)}, u32[]{:S(2)}) copy-start(s32[8]{0:T(128)} %constant.115.clone) | copy-start | bytes 100
  8.6 95.7 %copy-start.19 = (bf16[2,128,1280]{2,1,0:T(8,128)(2,1)S(1)}, bf16[2,128,1280]{2,1,0:T(8,128)(2,1)}, u32[]{:S(2)}) copy-start(bf16[2,128,1280]{2,1,0:T(8,128)(2,1)} %frames_ref.1) | copy-start | bytes 1966084
  8.6 169.2 %all-gather.5.cloned.1.call-start = ((), (), s32[]{:S(2)}) async-start(), calls=%async_computation.1 | async-start | bytes 5570560 | tf_op jit(solution)/shard_map/all_gather | solution.py:334
  11.4 6.7 %collective-permute-start = (bf16[10,2560]{1,0:T(8,128)(2,1)S(1)}, bf16[10,2560]{1,0:T(8,128)(2,1)S(1)}, u32[]{:S(2)}, u32[]{:S(2)}) collective-permute-start(bf16[10,2560]{1,0:T(8,128)(2,1)S(1)} %get-tuple-element.99), channel_id=1, source_target_pairs={{0,64},{64,0},{128,192},{192,128},{256,320},{320,256},{384,448},{4... | collective-permute-start | bytes 153608 | tf_op jit(solution)/shard_map/ppermute | solution.py:306
  18.1 13.9 %collective-permute-start.1 = (bf16[2,10,2560]{2,1,0:T(8,128)(2,1)S(1)}, bf16[2,10,2560]{2,1,0:T(8,128)(2,1)S(1)}, u32[]{:S(2)}, u32[]{:S(2)}) collective-permute-start(bf16[2,10,2560]{2,1,0:T(8,128)(2,1)S(1)} %pad_maximum_fusion.1), channel_id=1, source_target_pairs={{0,448},{64,128},{128,64},{192,256},{256,192},{320,384},{384,320},... | collective-permute-start | bytes 307208 | tf_op jit(solution)/shard_map/ppermute | solution.py:310
  32.0 7.3 %collective-permute-start.2 = (bf16[2,10,2560]{2,1,0:T(8,128)(2,1)S(1)}, bf16[2,10,2560]{2,1,0:T(8,128)(2,1)S(1)}, u32[]{:S(2)}, u32[]{:S(2)}) collective-permute-start(bf16[2,10,2560]{2,1,0:T(8,128)(2,1)S(1)} %collective-permute-done.1), channel_id=1, source_target_pairs={{0,64},{64,0},{128,192},{192,128},{256,320},{320,256},{384,448},{4... | collective-permute-start | bytes 307208 | tf_op jit(solution)/shard_map/ppermute | solution.py:310
  39.2 8.4 %collective-permute-start.3 = (bf16[2,10,2560]{2,1,0:T(8,128)(2,1)S(1)}, bf16[2,10,2560]{2,1,0:T(8,128)(2,1)S(1)}, u32[]{:S(2)}, u32[]{:S(2)}) collective-permute-start(bf16[2,10,2560]{2,1,0:T(8,128)(2,1)S(1)} %collective-permute-done.2), channel_id=1, source_target_pairs={{0,448},{64,128},{128,64},{192,256},{256,192},{320,384},{384,320},... | collective-permute-start | bytes 307208 | tf_op jit(solution)/shard_map/ppermute | solution.py:310
  48.9 57.3 %copy-start.27 = (bf16[80,2560]{1,0:T(8,128)(2,1)}, bf16[80,2560]{1,0:T(8,128)(2,1)S(1)}, u32[]{:S(2)}) copy-start(bf16[80,2560]{1,0:T(8,128)(2,1)S(1)} %concatenate.13.refs_0_) | copy-start | bytes 1228804
  48.9 11.5 %collective-permute-start.4 = (bf16[80,2560]{1,0:T(8,128)(2,1)S(1)}, bf16[80,2560]{1,0:T(8,128)(2,1)S(1)}, u32[]{:S(2)}, u32[]{:S(2)}) collective-permute-start(bf16[80,2560]{1,0:T(8,128)(2,1)S(1)} %concatenate.13.refs_0_), channel_id=1, source_target_pairs={{0,2},{1,3},{2,4},{3,5},{4,6},{5,7},{6,8},{7,9},{8,10},{9,11},{10,... | collective-permute-start | bytes 1228808 | tf_op jit(solution)/shard_map/ppermute | solution.py:294
  52.5 9.9 %collective-permute-start.8 = (bf16[80,2560]{1,0:T(8,128)(2,1)S(1)}, bf16[80,2560]{1,0:T(8,128)(2,1)S(1)}, u32[]{:S(2)}, u32[]{:S(2)}) collective-permute-start(bf16[80,2560]{1,0:T(8,128)(2,1)S(1)} %concatenate.13.refs_0_), channel_id=1, source_target_pairs={{0,14},{1,15},{2,0},{3,1},{4,2},{5,3},{6,4},{7,5},{8,6},{9,7},{10,... | collective-permute-start | bytes 1228808 | tf_op jit(solution)/shard_map/ppermute | solution.py:294
  60.5 45.7 %copy-start.28 = (bf16[80,2560]{1,0:T(8,128)(2,1)}, bf16[80,2560]{1,0:T(8,128)(2,1)S(1)}, u32[]{:S(2)}) copy-start(bf16[80,2560]{1,0:T(8,128)(2,1)S(1)} %collective-permute-done.4.refs_1_) | copy-start | bytes 1228804
  60.5 11.0 %collective-permute-start.5 = (bf16[80,2560]{1,0:T(8,128)(2,1)S(1)}, bf16[80,2560]{1,0:T(8,128)(2,1)S(1)}, u32[]{:S(2)}, u32[]{:S(2)}) collective-permute-start(bf16[80,2560]{1,0:T(8,128)(2,1)S(1)} %collective-permute-done.4.refs_1_), channel_id=1, source_target_pairs={{0,2},{1,3},{2,4},{3,5},{4,6},{5,7},{6,8},{7,9},{8,10},{9,11},{10,... | collective-permute-start | bytes 1228808 | tf_op jit(solution)/shard_map/ppermute | solution.py:294
  62.4 43.8 %copy-start.29 = (bf16[80,2560]{1,0:T(8,128)(2,1)}, bf16[80,2560]{1,0:T(8,128)(2,1)S(1)}, u32[]{:S(2)}) copy-start(bf16[80,2560]{1,0:T(8,128)(2,1)S(1)} %collective-permute-done.8.refs_5_) | copy-start | bytes 1228804
  62.4 17.3 %collective-permute-start.9 = (bf16[80,2560]{1,0:T(8,128)(2,1)S(1)}, bf16[80,2560]{1,0:T(8,128)(2,1)S(1)}, u32[]{:S(2)}, u32[]{:S(2)}) collective-permute-start(bf16[80,2560]{1,0:T(8,128)(2,1)S(1)} %collective-permute-done.8.refs_5_), channel_id=1, source_target_pairs={{0,14},{1,15},{2,0},{3,1},{4,2},{5,3},{6,4},{7,5},{8,6},{9,7},{10,... | collective-permute-start | bytes 1228808 | tf_op jit(solution)/shard_map/ppermute | solution.py:294
  71.5 34.7 %copy-start.30 = (bf16[80,2560]{1,0:T(8,128)(2,1)}, bf16[80,2560]{1,0:T(8,128)(2,1)S(1)}, u32[]{:S(2)}) copy-start(bf16[80,2560]{1,0:T(8,128)(2,1)S(1)} %collective-permute-done.5.refs_2_) | copy-start | bytes 1228804
  71.5 13.5 %collective-permute-start.6 = (bf16[80,2560]{1,0:T(8,128)(2,1)S(1)}, bf16[80,2560]{1,0:T(8,128)(2,1)}, u32[]{:S(2)}, u32[]{:S(2)}) collective-permute-start(bf16[80,2560]{1,0:T(8,128)(2,1)S(1)} %collective-permute-done.5.refs_2_), channel_id=1, source_target_pairs={{0,2},{1,3},{2,4},{3,5},{4,6},{5,7},{6,8},{7,9},{8,10},{9,11},{10,... | collective-permute-start | bytes 1228808 | tf_op jit(solution)/shard_map/ppermute | solution.py:294
  73.4 13.7 %collective-permute-start.11 = (bf16[80,2560]{1,0:T(8,128)(2,1)S(1)}, bf16[80,2560]{1,0:T(8,128)(2,1)S(1)}, u32[]{:S(2)}, u32[]{:S(2)}) collective-permute-start(bf16[80,2560]{1,0:T(8,128)(2,1)S(1)} %concatenate.13.refs_0_), channel_id=1, source_target_pairs={{0,1},{1,0},{2,3},{3,2},{4,5},{5,4},{6,7},{7,6},{8,9},{9,8},{10,11... | collective-permute-start | bytes 1228808 | tf_op jit(solution)/shard_map/ppermute | solution.py:324
  75.4 13.8 %collective-permute-start.12 = (bf16[80,2560]{1,0:T(8,128)(2,1)S(1)}, bf16[80,2560]{1,0:T(8,128)(2,1)}, u32[]{:S(2)}, u32[]{:S(2)}) collective-permute-start(bf16[80,2560]{1,0:T(8,128)(2,1)S(1)} %collective-permute-done.4.refs_1_), channel_id=1, source_target_pairs={{0,1},{1,0},{2,3},{3,2},{4,5},{5,4},{6,7},{7,6},{8,9},{9,8},{10,11... | collective-permute-start | bytes 1228808 | tf_op jit(solution)/shard_map/ppermute | solution.py:324
  77.8 13.8 %collective-permute-start.16 = (bf16[80,2560]{1,0:T(8,128)(2,1)S(1)}, bf16[80,2560]{1,0:T(8,128)(2,1)}, u32[]{:S(2)}, u32[]{:S(2)}) collective-permute-start(bf16[80,2560]{1,0:T(8,128)(2,1)S(1)} %collective-permute-done.8.refs_5_), channel_id=1, source_target_pairs={{0,1},{1,0},{2,3},{3,2},{4,5},{5,4},{6,7},{7,6},{8,9},{9,8},{10,11... | collective-permute-start | bytes 1228808 | tf_op jit(solution)/shard_map/ppermute | solution.py:324
  79.7 26.5 %copy-start.31 = (bf16[80,2560]{1,0:T(8,128)(2,1)}, bf16[80,2560]{1,0:T(8,128)(2,1)S(1)}, u32[]{:S(2)}) copy-start(bf16[80,2560]{1,0:T(8,128)(2,1)S(1)} %collective-permute-done.9.refs_6_) | copy-start | bytes 1228804
  79.7 17.9 %collective-permute-start.10 = (bf16[80,2560]{1,0:T(8,128)(2,1)S(1)}, bf16[80,2560]{1,0:T(8,128)(2,1)}, u32[]{:S(2)}, u32[]{:S(2)}) collective-permute-start(bf16[80,2560]{1,0:T(8,128)(2,1)S(1)} %collective-permute-done.9.refs_6_), channel_id=1, source_target_pairs={{0,14},{1,15},{2,0},{3,1},{4,2},{5,3},{6,4},{7,5},{8,6},{9,7},{10,... | collective-permute-start | bytes 1228808 | tf_op jit(solution)/shard_map/ppermute | solution.py:294
  85.0 17.0 %collective-permute-start.7 = (bf16[80,2560]{1,0:T(8,128)(2,1)}, bf16[80,2560]{1,0:T(8,128)(2,1)}, u32[]{:S(2)}, u32[]{:S(2)}) collective-permute-start(bf16[80,2560]{1,0:T(8,128)(2,1)} %collective-permute-done.6.refs_3_), channel_id=1, source_target_pairs={{0,2},{1,3},{2,4},{3,5},{4,6},{5,7},{6,8},{7,9},{8,10},{9,11},{10,... | collective-permute-start | bytes 1228808 | tf_op jit(solution)/shard_map/ppermute | solution.py:294
  87.2 18.9 %collective-permute-start.13 = (bf16[80,2560]{1,0:T(8,128)(2,1)S(1)}, bf16[80,2560]{1,0:T(8,128)(2,1)}, u32[]{:S(2)}, u32[]{:S(2)}) collective-permute-start(bf16[80,2560]{1,0:T(8,128)(2,1)S(1)} %collective-permute-done.5.refs_2_), channel_id=1, source_target_pairs={{0,1},{1,0},{2,3},{3,2},{4,5},{5,4},{6,7},{7,6},{8,9},{9,8},{10,11... | collective-permute-start | bytes 1228808 | tf_op jit(solution)/shard_map/ppermute | solution.py:324
  89.2 16.9 %collective-permute-start.17 = (bf16[80,2560]{1,0:T(8,128)(2,1)S(1)}, bf16[80,2560]{1,0:T(8,128)(2,1)}, u32[]{:S(2)}, u32[]{:S(2)}) collective-permute-start(bf16[80,2560]{1,0:T(8,128)(2,1)S(1)} %collective-permute-done.9.refs_6_), channel_id=1, source_target_pairs={{0,1},{1,0},{2,3},{3,2},{4,5},{5,4},{6,7},{7,6},{8,9},{9,8},{10,11... | collective-permute-start | bytes 1228808 | tf_op jit(solution)/shard_map/ppermute | solution.py:324
  91.5 14.6 %collective-permute-start.14 = (bf16[80,2560]{1,0:T(8,128)(2,1)}, bf16[80,2560]{1,0:T(8,128)(2,1)}, u32[]{:S(2)}, u32[]{:S(2)}) collective-permute-start(bf16[80,2560]{1,0:T(8,128)(2,1)} %collective-permute-done.6.refs_3_), channel_id=1, source_target_pairs={{0,1},{1,0},{2,3},{3,2},{4,5},{5,4},{6,7},{7,6},{8,9},{9,8},{10,11... | collective-permute-start | bytes 1228808 | tf_op jit(solution)/shard_map/ppermute | solution.py:324
  97.6 8.5 %collective-permute-start.18 = (bf16[80,2560]{1,0:T(8,128)(2,1)}, bf16[80,2560]{1,0:T(8,128)(2,1)}, u32[]{:S(2)}, u32[]{:S(2)}) collective-permute-start(bf16[80,2560]{1,0:T(8,128)(2,1)} %collective-permute-done.10.refs_7_), channel_id=1, source_target_pairs={{0,1},{1,0},{2,3},{3,2},{4,5},{5,4},{6,7},{7,6},{8,9},{9,8},{10,11... | collective-permute-start | bytes 1228808 | tf_op jit(solution)/shard_map/ppermute | solution.py:324
  102.0 4.2 %collective-permute-start.15 = (bf16[80,2560]{1,0:T(8,128)(2,1)}, bf16[80,2560]{1,0:T(8,128)(2,1)}, u32[]{:S(2)}, u32[]{:S(2)}) collective-permute-start(bf16[80,2560]{1,0:T(8,128)(2,1)} %collective-permute-done.7.refs_4_), channel_id=1, source_target_pairs={{0,1},{1,0},{2,3},{3,2},{4,5},{5,4},{6,7},{7,6},{8,9},{9,8},{10,11... | collective-permute-start | bytes 1228808 | tf_op jit(solution)/shard_map/ppermute | solution.py:324
  117.1 6.9 %collective-permute-start.19 = (bf16[64,1280]{1,0:T(8,128)(2,1)}, bf16[64,1280]{1,0:T(8,128)(2,1)S(1)}, u32[]{:S(2)}, u32[]{:S(2)}) collective-permute-start(bf16[64,1280]{1,0:T(8,128)(2,1)} %get-tuple-element.51.a_ref), channel_id=1, source_target_pairs={{0,1},{1,0},{2,3},{3,2},{4,5},{5,4},{6,7},{7,6},{8,9},{9,8},{10,11... | collective-permute-start | bytes 491528 | tf_op jit(solution)/shard_map/ppermute | solution.py:433
  119.8 4.2 %collective-permute-start.20 = (bf16[64,1280]{1,0:T(8,128)(2,1)}, bf16[64,1280]{1,0:T(8,128)(2,1)}, u32[]{:S(2)}, u32[]{:S(2)}) collective-permute-start(bf16[64,1280]{1,0:T(8,128)(2,1)} %get-tuple-element.52.b_ref), channel_id=1, source_target_pairs={{1,2},{2,1},{3,4},{4,3},{5,6},{6,5},{7,8},{8,7},{9,10},{10,9},{11,... | collective-permute-start | bytes 491528 | tf_op jit(solution)/shard_map/ppermute | solution.py:434
  126.8 9.3 %collective-permute-start.21 = (bf16[128,1280]{1,0:T(8,128)(2,1)}, bf16[128,1280]{1,0:T(8,128)(2,1)}, u32[]{:S(2)}, u32[]{:S(2)}) collective-permute-start(bf16[128,1280]{1,0:T(8,128)(2,1)} %layer_out.5), channel_id=1, source_target_pairs={{0,16},{16,32},{32,48},{1,17},{17,33},{33,49},{2,18},{18,34},{34,5... | collective-permute-start | bytes 983048 | tf_op jit(solution)/shard_map/ppermute | solution.py:457
  138.5 9.5 %collective-permute-start.22 = (bf16[64,1280]{1,0:T(8,128)(2,1)S(1)}, bf16[64,1280]{1,0:T(8,128)(2,1)S(1)}, u32[]{:S(2)}, u32[]{:S(2)}) collective-permute-start(bf16[64,1280]{1,0:T(8,128)(2,1)S(1)} %get-tuple-element.60.a_ref), channel_id=1, source_target_pairs={{0,1},{1,0},{2,3},{3,2},{4,5},{5,4},{6,7},{7,6},{8,9},{9,8},{10,11... | collective-permute-start | bytes 491528 | tf_op jit(solution)/shard_map/ppermute | solution.py:433
  145.9 2.0 collective-permute-start.23
  150.3 9.9 %collective-permute-start.24 = (bf16[128,1280]{1,0:T(8,128)(2,1)}, bf16[128,1280]{1,0:T(8,128)(2,1)}, u32[]{:S(2)}, u32[]{:S(2)}) collective-permute-start(bf16[128,1280]{1,0:T(8,128)(2,1)} %layer_out.6), channel_id=1, source_target_pairs={{0,16},{16,32},{32,48},{1,17},{17,33},{33,49},{2,18},{18,34},{34,5... | collective-permute-start | bytes 983048 | tf_op jit(solution)/shard_map/ppermute | solution.py:457
  162.2 10.6 %collective-permute-start.25 = (bf16[64,1280]{1,0:T(8,128)(2,1)S(1)}, bf16[64,1280]{1,0:T(8,128)(2,1)S(1)}, u32[]{:S(2)}, u32[]{:S(2)}) collective-permute-start(bf16[64,1280]{1,0:T(8,128)(2,1)S(1)} %get-tuple-element.68.a_ref), channel_id=1, source_target_pairs={{0,1},{1,0},{2,3},{3,2},{4,5},{5,4},{6,7},{7,6},{8,9},{9,8},{10,11... | collective-permute-start | bytes 491528 | tf_op jit(solution)/shard_map/ppermute | solution.py:433
  170.8 2.0 collective-permute-start.26
  175.7 9.3 %collective-permute-start.27 = (bf16[128,1280]{1,0:T(8,128)(2,1)}, bf16[128,1280]{1,0:T(8,128)(2,1)}, u32[]{:S(2)}, u32[]{:S(2)}) collective-permute-start(bf16[128,1280]{1,0:T(8,128)(2,1)} %layer_out.7), channel_id=1, source_target_pairs={{0,16},{16,32},{32,48},{1,17},{17,33},{33,49},{2,18},{18,34},{34,5... | collective-permute-start | bytes 983048 | tf_op jit(solution)/shard_map/ppermute | solution.py:457
  186.9 12.5 %collective-permute-start.28 = (bf16[64,1280]{1,0:T(8,128)(2,1)S(1)}, bf16[64,1280]{1,0:T(8,128)(2,1)S(1)}, u32[]{:S(2)}, u32[]{:S(2)}) collective-permute-start(bf16[64,1280]{1,0:T(8,128)(2,1)S(1)} %get-tuple-element.77.a_ref), channel_id=1, source_target_pairs={{0,1},{1,0},{2,3},{3,2},{4,5},{5,4},{6,7},{7,6},{8,9},{9,8},{10,11... | collective-permute-start | bytes 491528 | tf_op jit(solution)/shard_map/ppermute | solution.py:433
  197.4 2.0 collective-permute-start.29
  202.3 9.2 %collective-permute-start.33 = (bf16[128,1280]{1,0:T(8,128)(2,1)}, bf16[128,1280]{1,0:T(8,128)(2,1)S(1)}, u32[]{:S(2)}, u32[]{:S(2)}) collective-permute-start(bf16[128,1280]{1,0:T(8,128)(2,1)} %layer_out.8.refs_0_), channel_id=1, source_target_pairs={{0,16},{16,32},{32,48},{1,17},{17,33},{33,49},{2,18},{18,34},{34,5... | collective-permute-start | bytes 983048 | tf_op jit(solution)/shard_map/ppermute | solution.py:457
  204.2 23.1 %collective-permute-start.30 = (bf16[128,1280]{1,0:T(8,128)(2,1)}, bf16[128,1280]{1,0:T(8,128)(2,1)S(1)}, u32[]{:S(2)}, u32[]{:S(2)}) collective-permute-start(bf16[128,1280]{1,0:T(8,128)(2,1)} %layer_out.8.refs_0_), channel_id=1, source_target_pairs={{48,0},{49,1},{50,2},{51,3},{52,4},{53,5},{54,6},{55,7},{56,8},{57... | collective-permute-start | bytes 983048 | tf_op jit(solution)/shard_map/ppermute | solution.py:455
  212.8 11.4 %collective-permute-start.34 = (bf16[64,1280]{1,0:T(8,128)(2,1)S(1)}, bf16[64,1280]{1,0:T(8,128)(2,1)S(1)}, u32[]{:S(2)}, u32[]{:S(2)}) collective-permute-start(bf16[64,1280]{1,0:T(8,128)(2,1)S(1)} %get-tuple-element.84.a_ref), channel_id=1, source_target_pairs={{0,1},{1,0},{2,3},{3,2},{4,5},{5,4},{6,7},{7,6},{8,9},{9,8},{10,11... | collective-permute-start | bytes 491528 | tf_op jit(solution)/shard_map/ppermute | solution.py:433
  220.2 4.0 %collective-permute-start.35 = (bf16[64,1280]{1,0:T(8,128)(2,1)S(1)}, bf16[64,1280]{1,0:T(8,128)(2,1)S(1)}, u32[]{:S(2)}, u32[]{:S(2)}) collective-permute-start(bf16[64,1280]{1,0:T(8,128)(2,1)S(1)} %get-tuple-element.85.b_ref), channel_id=1, source_target_pairs={{1,2},{2,1},{3,4},{4,3},{5,6},{6,5},{7,8},{8,7},{9,10},{10,9},{11,... | collective-permute-start | bytes 491528 | tf_op jit(solution)/shard_map/ppermute | solution.py:434
  220.9 8.5 %collective-permute-start.31 = (bf16[128,1280]{1,0:T(8,128)(2,1)}, bf16[128,1280]{1,0:T(8,128)(2,1)S(1)}, u32[]{:S(2)}, u32[]{:S(2)}) collective-permute-start(bf16[128,1280]{1,0:T(8,128)(2,1)} %layer_out.8.refs_0_), channel_id=1, source_target_pairs={{48,16},{49,17},{50,18},{51,19},{52,20},{53,21},{54,22},{55,23},{5... | collective-permute-start | bytes 983048 | tf_op jit(solution)/shard_map/ppermute | solution.py:455
  221.6 13.4 %collective-permute-start.32 = (bf16[128,1280]{1,0:T(8,128)(2,1)}, bf16[128,1280]{1,0:T(8,128)(2,1)S(1)}, u32[]{:S(2)}, u32[]{:S(2)}) collective-permute-start(bf16[128,1280]{1,0:T(8,128)(2,1)} %layer_out.8.refs_0_), channel_id=1, source_target_pairs={{48,32},{49,33},{50,34},{51,35},{52,36},{53,37},{54,38},{55,39},{5... | collective-permute-start | bytes 983048 | tf_op jit(solution)/shard_map/ppermute | solution.py:455
  225.9 9.1 %collective-permute-start.36 = (bf16[128,1280]{1,0:T(8,128)(2,1)S(1)}, bf16[128,1280]{1,0:T(8,128)(2,1)S(1)}, u32[]{:S(2)}, u32[]{:S(2)}) collective-permute-start(bf16[128,1280]{1,0:T(8,128)(2,1)S(1)} %layer_out.9.refs_4_), channel_id=1, source_target_pairs={{48,0},{49,1},{50,2},{51,3},{52,4},{53,5},{54,6},{55,7},{56,8},{57... | collective-permute-start | bytes 983048 | tf_op jit(solution)/shard_map/ppermute | solution.py:455
  226.6 8.4 %collective-permute-start.37 = (bf16[128,1280]{1,0:T(8,128)(2,1)S(1)}, bf16[128,1280]{1,0:T(8,128)(2,1)S(1)}, u32[]{:S(2)}, u32[]{:S(2)}) collective-permute-start(bf16[128,1280]{1,0:T(8,128)(2,1)S(1)} %layer_out.9.refs_4_), channel_id=1, source_target_pairs={{48,16},{49,17},{50,18},{51,19},{52,20},{53,21},{54,22},{55,23},{5... | collective-permute-start | bytes 983048 | tf_op jit(solution)/shard_map/ppermute | solution.py:455
  228.0 21.0 %collective-permute-start.38 = (bf16[128,1280]{1,0:T(8,128)(2,1)S(1)}, bf16[128,1280]{1,0:T(8,128)(2,1)S(1)}, u32[]{:S(2)}, u32[]{:S(2)}) collective-permute-start(bf16[128,1280]{1,0:T(8,128)(2,1)S(1)} %layer_out.9.refs_4_), channel_id=1, source_target_pairs={{48,32},{49,33},{50,34},{51,35},{52,36},{53,37},{54,38},{55,39},{5... | collective-permute-start | bytes 983048 | tf_op jit(solution)/shard_map/ppermute | solution.py:455
  (29 other events, 190.6 us)
Sparse Core Ops, SparseCore 0:
  11.7 89.6 all-gather.6
  103.5 43.8 all-gather.4

commit v3 on v1

--- a/solution.py
+++ b/solution.py
@@ -16,8 +16,6 @@
 VMEM = pl.BlockSpec(memory_space=pltpu.VMEM)
 SMEM = pl.BlockSpec(memory_space=pltpu.SMEM)
 PARAMS = pltpu.CompilerParams(vmem_limit_bytes=16 * 1024 * 1024)
-JOIN_PARAMS = pltpu.CompilerParams()
-JOINED = VMEM
 
 
 def normed_rows(values):
@@ -57,10 +55,15 @@
         copy.wait()
 
 
-def kv_kernel(x_ref, w_ref, n_ref, first_ref, last_ref):
+def halves_product(n, near_ref, far_ref):
+    half = near_ref.shape[0]
+    return matmul(n[:, :half], near_ref[...]) + matmul(n[:, half:], far_ref[...])
+
+
+def kv_kernel(x_ref, near_ref, far_ref, n_ref, first_ref, last_ref):
     n = normed_rows(x_ref[...])
     n_ref[...] = n
-    kv = matmul(n, w_ref[...]).astype(BF16)
+    kv = halves_product(n, near_ref, far_ref).astype(BF16)
     first_ref[...] = kv[:BLK]
     last_ref[...] = kv[BLK:]
 
@@ -97,11 +100,11 @@
 
 
 def own_kernel(
-    moment, place_ref, mask_ref, n_ref, first_ref, last_ref, w_ref, q_ref, num_ref, den_ref
+    moment, place_ref, mask_ref, n_ref, first_ref, last_ref, near_ref, far_ref, q_ref, num_ref, den_ref
 ):
     width = q_ref.shape[1]
     allowed = allowed_of(moment, False, place_ref, mask_ref)
-    q = matmul(n_ref[...], w_ref[...]).astype(BF16)
+    q = halves_product(n_ref[...], near_ref, far_ref).astype(BF16)
     q_ref[...] = q
     for lane in range(0, width, 2 * HD):
         cols = slice(lane, lane + 2 * HD)
@@ -112,7 +115,7 @@
 
 
 def out_kernel(
-    moment, place_ref, mask_ref, q_ref, num_ref, den_ref, left_ref, right_ref, x_ref, w_ref,
+    moment, place_ref, mask_ref, q_ref, num_ref, den_ref, left_ref, right_ref, x_ref, near_ref, far_ref,
     o_ref, ctx_ref
 ):
     width = q_ref.shape[1]
@@ -124,8 +127,10 @@
         v = jnp.concatenate([left_ref[:, vcols], right_ref[:, vcols]], axis=0)
         num, den = pair_attention(q_ref[:, cols], k, v, allowed)
         ctx_ref[:, cols] = ((num + num_ref[:, cols]) / (den + den_ref[:, cols])).astype(BF16)
-    update = matmul_nt(ctx_ref[...], w_ref[...])
-    o_ref[...] = (x_ref[...].astype(F32) + update).astype(BF16)
+    half = near_ref.shape[0]
+    for cols, w_ref in ((slice(0, half), near_ref), (slice(half, 2 * half), far_ref)):
+        update = matmul_nt(ctx_ref[...], w_ref[...])
+        o_ref[:, cols] = (x_ref[:, cols].astype(F32) + update).astype(BF16)
 
 
 def order_kernel(order_ref, frames_ref, *out_refs):
@@ -310,12 +315,24 @@
             ring.append(moving)
             source.append((shard - step * (hop + 1)) % shards)
     swap = [(i, i ^ 1) for i in range(shards)]
-    pieces_w = ring + [lax.ppermute(value, "tm", swap) for value in ring]
     source = jnp.stack(source + [place ^ 1 for place in source])
     each = model // (groups * shards)
     slots = (group - jnp.array(steps)) % groups
     order = (slots[None, :, None] * shards + source[:, None, None]) * each + jnp.arange(each)
     order = order.reshape(-1).astype(jnp.int32)
+
+    half = model // 2
+    q_near, kv_near, out_near = pl.pallas_call(
+        join_kernel,
+        out_shape=(shape((half, width)), shape((half, 2 * width)), shape((half, width))),
+        in_specs=[pl.BlockSpec(memory_space=pl.ANY)] * len(ring),
+        out_specs=(VMEM,) * 3,
+        scratch_shapes=[pltpu.SemaphoreType.DMA((3, len(ring)))],
+        compiler_params=pltpu.CompilerParams(),
+        name="join",
+    )(*ring)
+    swap = [(i, i ^ 1) for i in range(shards)]
+    kv_far, q_far, out_far = (lax.ppermute(w, "tm", swap) for w in (kv_near, q_near, out_near))
 
     cross = jnp.concatenate([pad_lanes(w) for w in (cross_key, cross_value, cross_query)], axis=1)
     cross = lax.all_gather(cross, ("dp", "tm"), axis=0, tiled=True)
@@ -350,16 +367,9 @@
     tokens = dec_states.shape[0] // MB
     carried = inputs[0]
     memory = []
-    w_q, w_kv, w_out = pl.pallas_call(
-        join_kernel,
-        out_shape=(shape((model, width)), shape((model, 2 * width)), shape((model, width))),
-        in_specs=[pl.BlockSpec(memory_space=pl.ANY)] * len(pieces_w),
-        out_specs=(JOINED,) * 3,
-        scratch_shapes=[pltpu.SemaphoreType.DMA((3, len(pieces_w)))],
-        compiler_params=JOIN_PARAMS,
-        name="join",
-    )(*pieces_w)
     for moment in range(MB + sections - 1):
+        if moment == 1:
+            carried, cross = lax.optimization_barrier((carried, cross))
         if 0 < moment < MB:
             carried = jnp.where(section == 0, inputs[moment], carried)
         if moment == 2:
@@ -412,34 +422,40 @@
         n, first, last = pl.pallas_call(
             kv_kernel,
             out_shape=(shape((rows, model)), shape((BLK, 2 * width)), shape((BLK, 2 * width))),
-            in_specs=[VMEM, VMEM],
+            in_specs=[VMEM] * 3,
             out_specs=(VMEM, VMEM, VMEM),
             compiler_params=PARAMS,
             name="keys_values",
-        )(carried, w_kv)
+        )(carried, kv_near, kv_far)
         left = lax.ppermute(last, "tm", up)
         right = lax.ppermute(first, "tm", down)
         q, num, den = pl.pallas_call(
             functools.partial(own_kernel, moment),
             out_shape=(shape((rows, width)), shape((rows, width), F32), shape((rows, width), F32)),
-            in_specs=[SMEM, SMEM] + [VMEM] * 4,
+            in_specs=[SMEM, SMEM] + [VMEM] * 5,
             out_specs=(VMEM, VMEM, VMEM),
             compiler_params=PARAMS,
             name="own_blocks",
-        )(place, mask, n, first, last, w_q)
+        )(place, mask, n, first, last, q_near, q_far)
+        if moment == sections:
+            q, relayed = lax.optimization_barrier((q, relayed))
+            memory.append(lax.ppermute(relayed, "section", [(0, 1)]))
         finished = pl.pallas_call(
             functools.partial(out_kernel, moment),
             out_shape=shape((rows, model)),
-            in_specs=[SMEM, SMEM] + [VMEM] * 7,
+            in_specs=[SMEM, SMEM] + [VMEM] * 8,
             out_specs=VMEM,
             scratch_shapes=[pltpu.VMEM((rows, width), BF16)],
             compiler_params=PARAMS,
             name="layer_out",
-        )(place, mask, q, num, den, left, right, carried, w_out)
+        )(place, mask, q, num, den, left, right, carried, out_near, out_far)
         if moment >= sections - 1:
-            memory.append(finished)
-            for target in (0, 1, 2):
-                memory.append(lax.ppermute(finished, "section", [(sections - 1, target)]))
+            sent = [lax.ppermute(finished, "section", [(sections - 1, t)]) for t in (0, 2)]
+            if moment == sections - 1:
+                relayed = sent[0]
+            else:
+                sent.append(lax.ppermute(finished, "section", [(sections - 1, 1)]))
+            memory += [finished] + sent
         if moment < MB + sections - 2:
             carried = lax.ppermute(finished, "section", onward)
 

time: 305 us -> 299 us (0.980)
  starting transfers between devices: 122 us -> 108 us
  waiting for transfers between devices: 51.6 us -> 63.4 us
  blocking collectives: 41.5 us -> 36.7 us
  Pallas kernels: 42.2 us -> 45.7 us
    ppermute x14, waiting for transfers between devices: 22 us -> 33.2 us  [around(): lax.ppermute(value, axis, [(i, (i + step) % size) for i in range(size)])]
    ppermute x14 -> x9, starting transfers between devices: 21.8 us -> 12.4 us  [the longest x3 6.25 us: per_device(): lax.ppermute(w, 'tm', swap)]
    unnamed x71 -> x80, local copies, waits for them, and re-layouts: 21 us -> 14.3 us
    ppermute x5, starting transfers between devices: 29.3 us -> 22.6 us  [per_device(): left = lax.ppermute(last, 'tm', up)]
    optimization_barrier x0 -> x1, local copies, waits for them, and re-layouts: none -> 4.99 us  [per_device(): carried, cross = lax.optimization_barrier((carried, cross))]
    ppermute x4, waiting for transfers between devices: 10.8 us -> 6.18 us  [per_device(): carried = lax.ppermute(finished, 'section', onward)]
    ppermute x5, waiting for transfers between devices: 0.01 us -> 4.47 us  [per_device(): right = lax.ppermute(first, 'tm', down)]
    pallas_call x5, Pallas kernels: 6.41 us -> 10.3 us  [per_device(): pl.pallas_call(functools.partial(own_kernel, moment), out_shape=(shape((r...]
  transfers between devices with their start and end apart: 44 -> 39, of which waited for: 13 -> 16; matrix products, arithmetic and copies ran while one was open for 4% -> 4% of each run, Pallas kernels for 11% -> 12%
where the time goes in v3:
time: 299 us; the launch traced here: 297 us
  starting transfers between devices  108 us (36%)
  waiting for transfers between devices  63.4 us (21%)
  Pallas kernels  45.7 us (15%)
  blocking collectives  36.7 us (12%)
  local copies, waits for them, and re-layouts  22.9 us (8%)
  between operations  15 us (5%)
  other arithmetic  5.14 us (2%)
    ppermute x14, starting transfers between devices, around(): lax.ppermute(value, axis, [(i, (i + step) % size) for i in range(size)])  52.9 us
    ppermute x14, waiting for transfers between devices, around(): lax.ppermute(value, axis, [(i, (i + step) % size) for i in range(size)])  33.2 us
    all_gather x1, blocking collectives, per_device(): everyone = lax.all_gather(pieces, 'tm', axis=0)  24.1 us
    ppermute x5, starting transfers between devices, per_device(): left = lax.ppermute(last, 'tm', up)  22.6 us
    unnamed x80, local copies, waits for them, and re-layouts  14.3 us
    ppermute x1, waiting for transfers between devices, per_device(): sent.append(lax.ppermute(finished, 'section', [(sections - 1, 1)]))  14 us
    ppermute x4, starting transfers between devices, per_device(): carried = lax.ppermute(finished, 'section', onward)  13.4 us
    all_to_all x1, blocking collectives, per_device(): grad = lax.all_to_all(grad, 'dp', 0, 0, tiled=True)  12.6 us
  transfers between devices with their start and end apart: 39, of which 16 were waited for; matrix products, arithmetic and copies ran while one was open for 4% of the time, Pallas kernels for 12%

profile of v3, /device:TPU:2, one launch (start us, length us, event | category | flops | bytes accessed | tf_op | source)
XLA Modules:
  0.0 296.8 jit_solution(2355534150662601002)
XLA Ops:
  11.3 4.3 %collective-permute-start = (bf16[10,2560]{1,0:T(8,128)(2,1)S(1)}, bf16[10,2560]{1,0:T(8,128)(2,1)S(1)}, u32[]{:S(2)}, u32[]{:S(2)}) collective-permute-start(bf16[10,2560]{1,0:T(8,128)(2,1)S(1)} %pad_maximum_fusion.1), channel_id=1, source_target_pairs={{0,64},{64,128},{128,192},{192,256},{256,320},{320,384},{384,448},... | collective-permute-start | bytes 153608 | tf_op jit(solution)/shard_map/ppermute | solution.py:297
  15.5 8.6 %collective-permute-start.4 = (bf16[10,2560]{1,0:T(8,128)(2,1)S(1)}, bf16[10,2560]{1,0:T(8,128)(2,1)S(1)}, u32[]{:S(2)}, u32[]{:S(2)}) collective-permute-start(bf16[10,2560]{1,0:T(8,128)(2,1)S(1)} %pad_maximum_fusion.1), channel_id=1, source_target_pairs={{0,448},{64,0},{128,64},{192,128},{256,192},{320,256},{384,320},{4... | collective-permute-start | bytes 153608 | tf_op jit(solution)/shard_map/ppermute | solution.py:297
  26.6 5.1 %collective-permute-start.5 = (bf16[10,2560]{1,0:T(8,128)(2,1)S(1)}, bf16[10,2560]{1,0:T(8,128)(2,1)S(1)}, u32[]{:S(2)}, u32[]{:S(2)}) collective-permute-start(bf16[10,2560]{1,0:T(8,128)(2,1)S(1)} %collective-permute-done.4), channel_id=1, source_target_pairs={{0,448},{64,0},{128,64},{192,128},{256,192},{320,256},{384,320},{4... | collective-permute-start | bytes 153608 | tf_op jit(solution)/shard_map/ppermute | solution.py:297
  34.1 5.2 %collective-permute-start.6 = (bf16[10,2560]{1,0:T(8,128)(2,1)S(1)}, bf16[10,2560]{1,0:T(8,128)(2,1)S(1)}, u32[]{:S(2)}, u32[]{:S(2)}) collective-permute-start(bf16[10,2560]{1,0:T(8,128)(2,1)S(1)} %collective-permute-done.5), channel_id=1, source_target_pairs={{0,448},{64,0},{128,64},{192,128},{256,192},{320,256},{384,320},{4... | collective-permute-start | bytes 153608 | tf_op jit(solution)/shard_map/ppermute | solution.py:297
  41.6 5.6 %collective-permute-done.3 = bf16[10,2560]{1,0:T(8,128)(2,1)S(1)} collective-permute-done((bf16[10,2560]{1,0:T(8,128)(2,1)S(1)}, bf16[10,2560]{1,0:T(8,128)(2,1)S(1)}, u32[]{:S(2)}, u32[]{:S(2)}) %collective-permute-start.3) | collective-permute-done | bytes 51232 | tf_op jit(solution)/shard_map/ppermute | solution.py:297
  48.5 3.7 %collective-permute-start.7 = (bf16[80,2560]{1,0:T(8,128)(2,1)S(1)}, bf16[80,2560]{1,0:T(8,128)(2,1)S(1)}, u32[]{:S(2)}, u32[]{:S(2)}) collective-permute-start(bf16[80,2560]{1,0:T(8,128)(2,1)S(1)} %concatenate.13.refs_0_), channel_id=1, source_target_pairs={{0,2},{1,3},{2,4},{3,5},{4,6},{5,7},{6,8},{7,9},{8,10},{9,11},{10,... | collective-permute-start | bytes 1228808 | tf_op jit(solution)/shard_map/ppermute | solution.py:297
  52.2 3.9 %collective-permute-start.11 = (bf16[80,2560]{1,0:T(8,128)(2,1)S(1)}, bf16[80,2560]{1,0:T(8,128)(2,1)S(1)}, u32[]{:S(2)}, u32[]{:S(2)}) collective-permute-start(bf16[80,2560]{1,0:T(8,128)(2,1)S(1)} %concatenate.13.refs_0_), channel_id=1, source_target_pairs={{0,14},{1,15},{2,0},{3,1},{4,2},{5,3},{6,4},{7,5},{8,6},{9,7},{10,... | collective-permute-start | bytes 1228808 | tf_op jit(solution)/shard_map/ppermute | solution.py:297
  56.1 4.4 %collective-permute-done.7.refs_1_ = bf16[80,2560]{1,0:T(8,128)(2,1)S(1)} collective-permute-done((bf16[80,2560]{1,0:T(8,128)(2,1)S(1)}, bf16[80,2560]{1,0:T(8,128)(2,1)S(1)}, u32[]{:S(2)}, u32[]{:S(2)}) %collective-permute-start.7) | collective-permute-done | bytes 409632 | tf_op jit(solution)/shard_map/ppermute | solution.py:297
  62.5 5.1 %collective-permute-start.12 = (bf16[80,2560]{1,0:T(8,128)(2,1)S(1)}, bf16[80,2560]{1,0:T(8,128)(2,1)S(1)}, u32[]{:S(2)}, u32[]{:S(2)}) collective-permute-start(bf16[80,2560]{1,0:T(8,128)(2,1)S(1)} %collective-permute-done.11.refs_5_), channel_id=1, source_target_pairs={{0,14},{1,15},{2,0},{3,1},{4,2},{5,3},{6,4},{7,5},{8,6},{9,7},{10,... | collective-permute-start | bytes 1228808 | tf_op jit(solution)/shard_map/ppermute | solution.py:297
  67.6 4.0 %collective-permute-done.8.refs_2_ = bf16[80,2560]{1,0:T(8,128)(2,1)S(1)} collective-permute-done((bf16[80,2560]{1,0:T(8,128)(2,1)S(1)}, bf16[80,2560]{1,0:T(8,128)(2,1)S(1)}, u32[]{:S(2)}, u32[]{:S(2)}) %collective-permute-start.8) | collective-permute-done | bytes 409632 | tf_op jit(solution)/shard_map/ppermute | solution.py:297
  74.9 5.6 %collective-permute-start.13 = (bf16[80,2560]{1,0:T(8,128)(2,1)S(1)}, bf16[80,2560]{1,0:T(8,128)(2,1)S(1)}, u32[]{:S(2)}, u32[]{:S(2)}) collective-permute-start(bf16[80,2560]{1,0:T(8,128)(2,1)S(1)} %collective-permute-done.12.refs_6_), channel_id=1, source_target_pairs={{0,14},{1,15},{2,0},{3,1},{4,2},{5,3},{6,4},{7,5},{8,6},{9,7},{10,... | collective-permute-start | bytes 1228808 | tf_op jit(solution)/shard_map/ppermute | solution.py:297
  80.5 5.9 %collective-permute-done.9.refs_3_ = bf16[80,2560]{1,0:T(8,128)(2,1)S(1)} collective-permute-done((bf16[80,2560]{1,0:T(8,128)(2,1)S(1)}, bf16[80,2560]{1,0:T(8,128)(2,1)S(1)}, u32[]{:S(2)}, u32[]{:S(2)}) %collective-permute-start.9) | collective-permute-done | bytes 409632 | tf_op jit(solution)/shard_map/ppermute | solution.py:297
  88.3 10.6 %collective-permute-done.10.refs_4_ = bf16[80,2560]{1,0:T(8,128)(2,1)} collective-permute-done((bf16[80,2560]{1,0:T(8,128)(2,1)S(1)}, bf16[80,2560]{1,0:T(8,128)(2,1)}, u32[]{:S(2)}, u32[]{:S(2)}) %collective-permute-start.10) | collective-permute-done | bytes 409632 | tf_op jit(solution)/shard_map/ppermute | solution.py:297
  98.9 4.0 %join.1 = (bf16[640,640]{1,0:T(8,128)(2,1)}, bf16[640,1280]{1,0:T(8,128)(2,1)}, bf16[640,640]{1,0:T(8,128)(2,1)}) custom-call(bf16[80,2560]{1,0:T(8,128)(2,1)} %copy-done.28, bf16[80,2560]{1,0:T(8,128)(2,1)} %copy-done.29, bf16[80,2560]{1,0:T(8,128)(2,1)} %copy-done.31, bf16[80,2560]{1,0:T(8,128)(2,1)} %copy-done.33, ...), custom_call_target="tpu_custom_call" | custom-call | tf_op jit(solution)/shard_map/join/pallas_call | solution.py:325
  102.9 1.9 collective-permute-start.14
  105.0 2.4 collective-permute-start.15
  107.4 1.9 collective-permute-start.18
  115.3 2.5 collective-permute-start.16
  121.4 2.2 own_blocks.5
  123.7 2.9 layer_out.5
  126.7 3.4 %collective-permute-start.19 = (bf16[128,1280]{1,0:T(8,128)(2,1)}, bf16[128,1280]{1,0:T(8,128)(2,1)}, u32[]{:S(2)}, u32[]{:S(2)}) collective-permute-start(bf16[128,1280]{1,0:T(8,128)(2,1)} %layer_out.5), channel_id=1, source_target_pairs={{0,16},{16,32},{32,48},{1,17},{17,33},{33,49},{2,18},{18,34},{34,5... | collective-permute-start | bytes 983048 | tf_op jit(solution)/shard_map/ppermute | solution.py:460
  130.1 5.0 %reshape.97.w_ref = bf16[1280,768]{1,0:T(8,128)(2,1)} reshape(bf16[128,10,768]{2,1,0:T(8,128)(2,1)} %all-gather.7.cloned.1.call-done) | data formatting | bytes 3932160 | tf_op jit(solution)/shard_map/optimization_barrier | solution.py:372
  135.1 2.3 collective-permute-done.19
  139.3 4.3 %collective-permute-start.20 = (bf16[64,1280]{1,0:T(8,128)(2,1)S(1)}, bf16[64,1280]{1,0:T(8,128)(2,1)S(1)}, u32[]{:S(2)}, u32[]{:S(2)}) collective-permute-start(bf16[64,1280]{1,0:T(8,128)(2,1)S(1)} %get-tuple-element.63.last_ref), channel_id=1, source_target_pairs={{0,1},{1,2},{2,3},{3,4},{4,5},{5,6},{6,7},{7,8},{8,9},{9,10},{10,1... | collective-permute-start | bytes 491528 | tf_op jit(solution)/shard_map/ppermute | solution.py:430
  144.9 2.0 own_blocks.6
  148.5 2.4 layer_out.6
  150.9 3.6 %collective-permute-start.22 = (bf16[128,1280]{1,0:T(8,128)(2,1)}, bf16[128,1280]{1,0:T(8,128)(2,1)}, u32[]{:S(2)}, u32[]{:S(2)}) collective-permute-start(bf16[128,1280]{1,0:T(8,128)(2,1)} %layer_out.6), channel_id=1, source_target_pairs={{0,16},{16,32},{32,48},{1,17},{17,33},{33,49},{2,18},{18,34},{34,5... | collective-permute-start | bytes 983048 | tf_op jit(solution)/shard_map/ppermute | solution.py:460
  161.1 1.9 keys_values.7
  163.1 5.6 %collective-permute-start.23 = (bf16[64,1280]{1,0:T(8,128)(2,1)S(1)}, bf16[64,1280]{1,0:T(8,128)(2,1)S(1)}, u32[]{:S(2)}, u32[]{:S(2)}) collective-permute-start(bf16[64,1280]{1,0:T(8,128)(2,1)S(1)} %get-tuple-element.71.last_ref), channel_id=1, source_target_pairs={{0,1},{1,2},{2,3},{3,4},{4,5},{5,6},{6,7},{7,8},{8,9},{9,10},{10,1... | collective-permute-start | bytes 491528 | tf_op jit(solution)/shard_map/ppermute | solution.py:430
  170.0 2.0 own_blocks.7
  173.8 2.8 layer_out.7
  176.6 3.4 %collective-permute-start.25 = (bf16[128,1280]{1,0:T(8,128)(2,1)}, bf16[128,1280]{1,0:T(8,128)(2,1)}, u32[]{:S(2)}, u32[]{:S(2)}) collective-permute-start(bf16[128,1280]{1,0:T(8,128)(2,1)} %layer_out.7), channel_id=1, source_target_pairs={{0,16},{16,32},{32,48},{1,17},{17,33},{33,49},{2,18},{18,34},{34,5... | collective-permute-start | bytes 983048 | tf_op jit(solution)/shard_map/ppermute | solution.py:460
  180.1 2.5 copy-done.2
  184.1 2.2 queries.1.q_ref
  187.0 2.0 keys_values.8
  189.1 5.6 %collective-permute-start.26 = (bf16[64,1280]{1,0:T(8,128)(2,1)S(1)}, bf16[64,1280]{1,0:T(8,128)(2,1)S(1)}, u32[]{:S(2)}, u32[]{:S(2)}) collective-permute-start(bf16[64,1280]{1,0:T(8,128)(2,1)S(1)} %get-tuple-element.80.last_ref), channel_id=1, source_target_pairs={{0,1},{1,2},{2,3},{3,4},{4,5},{5,6},{6,7},{7,8},{8,9},{9,10},{10,1... | collective-permute-start | bytes 491528 | tf_op jit(solution)/shard_map/ppermute | solution.py:430
  196.0 2.0 own_blocks.8
  199.3 2.8 layer_out.8.refs_0_
  202.1 3.1 %collective-permute-start.30 = (bf16[128,1280]{1,0:T(8,128)(2,1)}, bf16[128,1280]{1,0:T(8,128)(2,1)S(1)}, u32[]{:S(2)}, u32[]{:S(2)}) collective-permute-start(bf16[128,1280]{1,0:T(8,128)(2,1)} %layer_out.8.refs_0_), channel_id=1, source_target_pairs={{0,16},{16,32},{32,48},{1,17},{17,33},{33,49},{2,18},{18,34},{34,5... | collective-permute-start | bytes 983048 | tf_op jit(solution)/shard_map/ppermute | solution.py:460
  208.0 3.9 %collective-permute-done.30.x_ref = bf16[128,1280]{1,0:T(8,128)(2,1)S(1)} collective-permute-done((bf16[128,1280]{1,0:T(8,128)(2,1)}, bf16[128,1280]{1,0:T(8,128)(2,1)S(1)}, u32[]{:S(2)}, u32[]{:S(2)}) %collective-permute-start.30) | collective-permute-done | bytes 327712 | tf_op jit(solution)/shard_map/ppermute | solution.py:460
  212.8 4.6 %collective-permute-start.32 = (bf16[64,1280]{1,0:T(8,128)(2,1)S(1)}, bf16[64,1280]{1,0:T(8,128)(2,1)S(1)}, u32[]{:S(2)}, u32[]{:S(2)}) collective-permute-start(bf16[64,1280]{1,0:T(8,128)(2,1)S(1)} %get-tuple-element.87.last_ref), channel_id=1, source_target_pairs={{0,1},{1,2},{2,3},{3,4},{4,5},{5,6},{6,7},{7,8},{8,9},{9,10},{10,1... | collective-permute-start | bytes 491528 | tf_op jit(solution)/shard_map/ppermute | solution.py:430
  219.4 2.0 own_blocks.9
  227.3 5.5 %collective-permute-done.31.refs_3_ = bf16[128,1280]{1,0:T(8,128)(2,1)S(1)} collective-permute-done((bf16[128,1280]{1,0:T(8,128)(2,1)}, bf16[128,1280]{1,0:T(8,128)(2,1)S(1)}, u32[]{:S(2)}, u32[]{:S(2)}) %collective-permute-start.31) | collective-permute-done | bytes 327712 | tf_op jit(solution)/shard_map/ppermute | solution.py:442
  232.7 14.0 %collective-permute-done.36.refs_7_ = bf16[128,1280]{1,0:T(8,128)(2,1)S(1)} collective-permute-done((bf16[128,1280]{1,0:T(8,128)(2,1)S(1)}, bf16[128,1280]{1,0:T(8,128)(2,1)S(1)}, u32[]{:S(2)}, u32[]{:S(2)}) %collective-permute-start.36) | collective-permute-done | bytes 327712 | tf_op jit(solution)/shard_map/ppermute | solution.py:457
  247.6 2.3 cross.1
  250.0 24.1 %all-gather = bf16[3584,128]{1,0:T(8,128)(2,1)S(1)} all-gather(bf16[224,128]{1,0:T(8,128)(2,1)S(1)} %cross.1), channel_id=2, replica_groups=mesh['dp'=8,'section'=4,'tm'=16] {'tm'}, dimensions={0}, use_global_device_ids=true | all-gather | bytes 974848 | tf_op jit(solution)/shard_map/all_gather | solution.py:470
  274.0 2.7 combine.1
  276.7 12.6 %all_to_all.5 = bf16[8,16,256]{2,1,0:T(8,128)(2,1)S(1)} all-to-all(bf16[8,16,256]{2,1,0:T(8,128)(2,1)S(1)} %get-tuple-element.95), channel_id=1, replica_groups=mesh['dp'=8,'section'=4,'tm'=16] {'dp'}, dimensions={0} | all-to-all | bytes 131072 | tf_op jit(solution)/shard_map/all_to_all | solution.py:484
  (156 shorter events, 61.4 us)
Async XLA Ops:
  7.2 122.9 %all-gather.7.cloned.1.call-start = ((), (), s32[]{:S(2)}) async-start(), calls=%async_computation.2 | async-start | bytes 3170304 | tf_op jit(solution)/shard_map/all_gather | solution.py:338
  8.6 171.5 %all-gather.5.cloned.1.call-start = ((), (), s32[]{:S(2)}) async-start(), calls=%async_computation.1 | async-start | bytes 5570560 | tf_op jit(solution)/shard_map/all_gather | solution.py:339
  11.3 13.4 %collective-permute-start = (bf16[10,2560]{1,0:T(8,128)(2,1)S(1)}, bf16[10,2560]{1,0:T(8,128)(2,1)S(1)}, u32[]{:S(2)}, u32[]{:S(2)}) collective-permute-start(bf16[10,2560]{1,0:T(8,128)(2,1)S(1)} %pad_maximum_fusion.1), channel_id=1, source_target_pairs={{0,64},{64,128},{128,192},{192,256},{256,320},{320,384},{384,448},... | collective-permute-start | bytes 153608 | tf_op jit(solution)/shard_map/ppermute | solution.py:297
  15.5 11.0 %collective-permute-start.4 = (bf16[10,2560]{1,0:T(8,128)(2,1)S(1)}, bf16[10,2560]{1,0:T(8,128)(2,1)S(1)}, u32[]{:S(2)}, u32[]{:S(2)}) collective-permute-start(bf16[10,2560]{1,0:T(8,128)(2,1)S(1)} %pad_maximum_fusion.1), channel_id=1, source_target_pairs={{0,448},{64,0},{128,64},{192,128},{256,192},{320,256},{384,320},{4... | collective-permute-start | bytes 153608 | tf_op jit(solution)/shard_map/ppermute | solution.py:297
  24.6 7.5 %collective-permute-start.1 = (bf16[10,2560]{1,0:T(8,128)(2,1)S(1)}, bf16[10,2560]{1,0:T(8,128)(2,1)S(1)}, u32[]{:S(2)}, u32[]{:S(2)}) collective-permute-start(bf16[10,2560]{1,0:T(8,128)(2,1)S(1)} %collective-permute-done), channel_id=1, source_target_pairs={{0,64},{64,128},{128,192},{192,256},{256,320},{320,384},{384,448},... | collective-permute-start | bytes 153608 | tf_op jit(solution)/shard_map/ppermute | solution.py:297
  26.6 7.5 %collective-permute-start.5 = (bf16[10,2560]{1,0:T(8,128)(2,1)S(1)}, bf16[10,2560]{1,0:T(8,128)(2,1)S(1)}, u32[]{:S(2)}, u32[]{:S(2)}) collective-permute-start(bf16[10,2560]{1,0:T(8,128)(2,1)S(1)} %collective-permute-done.4), channel_id=1, source_target_pairs={{0,448},{64,0},{128,64},{192,128},{256,192},{320,256},{384,320},{4... | collective-permute-start | bytes 153608 | tf_op jit(solution)/shard_map/ppermute | solution.py:297
  32.2 7.5 %collective-permute-start.2 = (bf16[10,2560]{1,0:T(8,128)(2,1)S(1)}, bf16[10,2560]{1,0:T(8,128)(2,1)S(1)}, u32[]{:S(2)}, u32[]{:S(2)}) collective-permute-start(bf16[10,2560]{1,0:T(8,128)(2,1)S(1)} %collective-permute-done.1), channel_id=1, source_target_pairs={{0,64},{64,128},{128,192},{192,256},{256,320},{320,384},{384,448},... | collective-permute-start | bytes 153608 | tf_op jit(solution)/shard_map/ppermute | solution.py:297
  34.1 7.5 %collective-permute-start.6 = (bf16[10,2560]{1,0:T(8,128)(2,1)S(1)}, bf16[10,2560]{1,0:T(8,128)(2,1)S(1)}, u32[]{:S(2)}, u32[]{:S(2)}) collective-permute-start(bf16[10,2560]{1,0:T(8,128)(2,1)S(1)} %collective-permute-done.5), channel_id=1, source_target_pairs={{0,448},{64,0},{128,64},{192,128},{256,192},{320,256},{384,320},{4... | collective-permute-start | bytes 153608 | tf_op jit(solution)/shard_map/ppermute | solution.py:297
  39.7 7.5 %collective-permute-start.3 = (bf16[10,2560]{1,0:T(8,128)(2,1)S(1)}, bf16[10,2560]{1,0:T(8,128)(2,1)S(1)}, u32[]{:S(2)}, u32[]{:S(2)}) collective-permute-start(bf16[10,2560]{1,0:T(8,128)(2,1)S(1)} %collective-permute-done.2), channel_id=1, source_target_pairs={{0,64},{64,128},{128,192},{192,256},{256,320},{320,384},{384,448},... | collective-permute-start | bytes 153608 | tf_op jit(solution)/shard_map/ppermute | solution.py:297
  48.5 50.4 %copy-start.28 = (bf16[80,2560]{1,0:T(8,128)(2,1)}, bf16[80,2560]{1,0:T(8,128)(2,1)S(1)}, u32[]{:S(2)}) copy-start(bf16[80,2560]{1,0:T(8,128)(2,1)S(1)} %concatenate.13.refs_0_) | copy-start | bytes 1228804
  48.5 60.9 %copy-start.37 = (s32[8]{0:T(128)S(1)}, s32[8]{0:T(128)}, u32[]{:S(2)}) copy-start(s32[8]{0:T(128)} %constant.125) | copy-start | bytes 100
  48.5 61.2 %copy-start.22 = (bf16[2,128,1280]{2,1,0:T(8,128)(2,1)S(1)}, bf16[2,128,1280]{2,1,0:T(8,128)(2,1)}, u32[]{:S(2)}) copy-start(bf16[2,128,1280]{2,1,0:T(8,128)(2,1)} %frames_ref.1) | copy-start | bytes 1966084
  48.5 12.0 %collective-permute-start.7 = (bf16[80,2560]{1,0:T(8,128)(2,1)S(1)}, bf16[80,2560]{1,0:T(8,128)(2,1)S(1)}, u32[]{:S(2)}, u32[]{:S(2)}) collective-permute-start(bf16[80,2560]{1,0:T(8,128)(2,1)S(1)} %concatenate.13.refs_0_), channel_id=1, source_target_pairs={{0,2},{1,3},{2,4},{3,5},{4,6},{5,7},{6,8},{7,9},{8,10},{9,11},{10,... | collective-permute-start | bytes 1228808 | tf_op jit(solution)/shard_map/ppermute | solution.py:297
  52.2 10.3 %collective-permute-start.11 = (bf16[80,2560]{1,0:T(8,128)(2,1)S(1)}, bf16[80,2560]{1,0:T(8,128)(2,1)S(1)}, u32[]{:S(2)}, u32[]{:S(2)}) collective-permute-start(bf16[80,2560]{1,0:T(8,128)(2,1)S(1)} %concatenate.13.refs_0_), channel_id=1, source_target_pairs={{0,14},{1,15},{2,0},{3,1},{4,2},{5,3},{6,4},{7,5},{8,6},{9,7},{10,... | collective-permute-start | bytes 1228808 | tf_op jit(solution)/shard_map/ppermute | solution.py:297
  60.6 38.3 %copy-start.29 = (bf16[80,2560]{1,0:T(8,128)(2,1)}, bf16[80,2560]{1,0:T(8,128)(2,1)S(1)}, u32[]{:S(2)}) copy-start(bf16[80,2560]{1,0:T(8,128)(2,1)S(1)} %collective-permute-done.7.refs_1_) | copy-start | bytes 1228804
  60.6 11.0 %collective-permute-start.8 = (bf16[80,2560]{1,0:T(8,128)(2,1)S(1)}, bf16[80,2560]{1,0:T(8,128)(2,1)S(1)}, u32[]{:S(2)}, u32[]{:S(2)}) collective-permute-start(bf16[80,2560]{1,0:T(8,128)(2,1)S(1)} %collective-permute-done.7.refs_1_), channel_id=1, source_target_pairs={{0,2},{1,3},{2,4},{3,5},{4,6},{5,7},{6,8},{7,9},{8,10},{9,11},{10,... | collective-permute-start | bytes 1228808 | tf_op jit(solution)/shard_map/ppermute | solution.py:297
  62.5 36.4 %copy-start.30 = (bf16[80,2560]{1,0:T(8,128)(2,1)}, bf16[80,2560]{1,0:T(8,128)(2,1)S(1)}, u32[]{:S(2)}) copy-start(bf16[80,2560]{1,0:T(8,128)(2,1)S(1)} %collective-permute-done.11.refs_5_) | copy-start | bytes 1228804
  62.5 12.4 %collective-permute-start.12 = (bf16[80,2560]{1,0:T(8,128)(2,1)S(1)}, bf16[80,2560]{1,0:T(8,128)(2,1)S(1)}, u32[]{:S(2)}, u32[]{:S(2)}) collective-permute-start(bf16[80,2560]{1,0:T(8,128)(2,1)S(1)} %collective-permute-done.11.refs_5_), channel_id=1, source_target_pairs={{0,14},{1,15},{2,0},{3,1},{4,2},{5,3},{6,4},{7,5},{8,6},{9,7},{10,... | collective-permute-start | bytes 1228808 | tf_op jit(solution)/shard_map/ppermute | solution.py:297
  71.6 27.3 %copy-start.31 = (bf16[80,2560]{1,0:T(8,128)(2,1)}, bf16[80,2560]{1,0:T(8,128)(2,1)S(1)}, u32[]{:S(2)}) copy-start(bf16[80,2560]{1,0:T(8,128)(2,1)S(1)} %collective-permute-done.8.refs_2_) | copy-start | bytes 1228804
  71.6 14.7 %collective-permute-start.9 = (bf16[80,2560]{1,0:T(8,128)(2,1)S(1)}, bf16[80,2560]{1,0:T(8,128)(2,1)S(1)}, u32[]{:S(2)}, u32[]{:S(2)}) collective-permute-start(bf16[80,2560]{1,0:T(8,128)(2,1)S(1)} %collective-permute-done.8.refs_2_), channel_id=1, source_target_pairs={{0,2},{1,3},{2,4},{3,5},{4,6},{5,7},{6,8},{7,9},{8,10},{9,11},{10,... | collective-permute-start | bytes 1228808 | tf_op jit(solution)/shard_map/ppermute | solution.py:297
  74.9 24.0 %copy-start.32 = (bf16[80,2560]{1,0:T(8,128)(2,1)}, bf16[80,2560]{1,0:T(8,128)(2,1)S(1)}, u32[]{:S(2)}) copy-start(bf16[80,2560]{1,0:T(8,128)(2,1)S(1)} %collective-permute-done.12.refs_6_) | copy-start | bytes 1228804
  74.9 13.4 %collective-permute-start.13 = (bf16[80,2560]{1,0:T(8,128)(2,1)S(1)}, bf16[80,2560]{1,0:T(8,128)(2,1)S(1)}, u32[]{:S(2)}, u32[]{:S(2)}) collective-permute-start(bf16[80,2560]{1,0:T(8,128)(2,1)S(1)} %collective-permute-done.12.refs_6_), channel_id=1, source_target_pairs={{0,14},{1,15},{2,0},{3,1},{4,2},{5,3},{6,4},{7,5},{8,6},{9,7},{10,... | collective-permute-start | bytes 1228808 | tf_op jit(solution)/shard_map/ppermute | solution.py:297
  86.4 12.5 %collective-permute-start.10 = (bf16[80,2560]{1,0:T(8,128)(2,1)S(1)}, bf16[80,2560]{1,0:T(8,128)(2,1)}, u32[]{:S(2)}, u32[]{:S(2)}) collective-permute-start(bf16[80,2560]{1,0:T(8,128)(2,1)S(1)} %collective-permute-done.9.refs_3_), channel_id=1, source_target_pairs={{0,2},{1,3},{2,4},{3,5},{4,6},{5,7},{6,8},{7,9},{8,10},{9,11},{10,... | collective-permute-start | bytes 1228808 | tf_op jit(solution)/shard_map/ppermute | solution.py:297
  102.9 7.9 %collective-permute-start.14 = (bf16[640,1280]{1,0:T(8,128)(2,1)}, bf16[640,1280]{1,0:T(8,128)(2,1)S(1)}, u32[]{:S(2)}, u32[]{:S(2)}) collective-permute-start(bf16[640,1280]{1,0:T(8,128)(2,1)} %get-tuple-element.51.near_ref), channel_id=1, source_target_pairs={{0,1},{1,0},{2,3},{3,2},{4,5},{5,4},{6,7},{7,6},{8,9},{9,8},{10,11... | collective-permute-start | bytes 4915208 | tf_op jit(solution)/shard_map/ppermute | solution.py:335
  105.0 14.3 %collective-permute-start.15 = (bf16[640,640]{1,0:T(8,128)(2,1)}, bf16[640,640]{1,0:T(8,128)(2,1)}, u32[]{:S(2)}, u32[]{:S(2)}) collective-permute-start(bf16[640,640]{1,0:T(8,128)(2,1)} %get-tuple-element.55.near_ref), channel_id=1, source_target_pairs={{0,1},{1,0},{2,3},{3,2},{4,5},{5,4},{6,7},{7,6},{8,9},{9,8},{10,11... | collective-permute-start | bytes 2457608 | tf_op jit(solution)/shard_map/ppermute | solution.py:335
  107.4 16.2 %collective-permute-start.18 = (bf16[640,640]{1,0:T(8,128)(2,1)}, bf16[640,640]{1,0:T(8,128)(2,1)S(1)}, u32[]{:S(2)}, u32[]{:S(2)}) collective-permute-start(bf16[640,640]{1,0:T(8,128)(2,1)} %get-tuple-element.59.near_ref), channel_id=1, source_target_pairs={{0,1},{1,0},{2,3},{3,2},{4,5},{5,4},{6,7},{7,6},{8,9},{9,8},{10,11... | collective-permute-start | bytes 2457608 | tf_op jit(solution)/shard_map/ppermute | solution.py:335
  115.3 8.4 %collective-permute-start.16 = (bf16[64,1280]{1,0:T(8,128)(2,1)}, bf16[64,1280]{1,0:T(8,128)(2,1)S(1)}, u32[]{:S(2)}, u32[]{:S(2)}) collective-permute-start(bf16[64,1280]{1,0:T(8,128)(2,1)} %get-tuple-element.54.last_ref), channel_id=1, source_target_pairs={{0,1},{1,2},{2,3},{3,4},{4,5},{5,6},{6,7},{7,8},{8,9},{9,10},{10,1... | collective-permute-start | bytes 491528 | tf_op jit(solution)/shard_map/ppermute | solution.py:430
  117.8 5.9 %collective-permute-start.17 = (bf16[64,1280]{1,0:T(8,128)(2,1)}, bf16[64,1280]{1,0:T(8,128)(2,1)}, u32[]{:S(2)}, u32[]{:S(2)}) collective-permute-start(bf16[64,1280]{1,0:T(8,128)(2,1)} %get-tuple-element.53.first_ref), channel_id=1, source_target_pairs={{1,0},{2,1},{3,2},{4,3},{5,4},{6,5},{7,6},{8,7},{9,8},{10,9},{11,1... | collective-permute-start | bytes 491528 | tf_op jit(solution)/shard_map/ppermute | solution.py:431
  126.7 10.7 %collective-permute-start.19 = (bf16[128,1280]{1,0:T(8,128)(2,1)}, bf16[128,1280]{1,0:T(8,128)(2,1)}, u32[]{:S(2)}, u32[]{:S(2)}) collective-permute-start(bf16[128,1280]{1,0:T(8,128)(2,1)} %layer_out.5), channel_id=1, source_target_pairs={{0,16},{16,32},{32,48},{1,17},{17,33},{33,49},{2,18},{18,34},{34,5... | collective-permute-start | bytes 983048 | tf_op jit(solution)/shard_map/ppermute | solution.py:460
  139.3 7.6 %collective-permute-start.20 = (bf16[64,1280]{1,0:T(8,128)(2,1)S(1)}, bf16[64,1280]{1,0:T(8,128)(2,1)S(1)}, u32[]{:S(2)}, u32[]{:S(2)}) collective-permute-start(bf16[64,1280]{1,0:T(8,128)(2,1)S(1)} %get-tuple-element.63.last_ref), channel_id=1, source_target_pairs={{0,1},{1,2},{2,3},{3,4},{4,5},{5,6},{6,7},{7,8},{8,9},{9,10},{10,1... | collective-permute-start | bytes 491528 | tf_op jit(solution)/shard_map/ppermute | solution.py:430
  143.6 4.9 %collective-permute-start.21 = (bf16[64,1280]{1,0:T(8,128)(2,1)S(1)}, bf16[64,1280]{1,0:T(8,128)(2,1)S(1)}, u32[]{:S(2)}, u32[]{:S(2)}) collective-permute-start(bf16[64,1280]{1,0:T(8,128)(2,1)S(1)} %get-tuple-element.62.first_ref), channel_id=1, source_target_pairs={{1,0},{2,1},{3,2},{4,3},{5,4},{6,5},{7,6},{8,7},{9,8},{10,9},{11,1... | collective-permute-start | bytes 491528 | tf_op jit(solution)/shard_map/ppermute | solution.py:431
  150.9 10.2 %collective-permute-start.22 = (bf16[128,1280]{1,0:T(8,128)(2,1)}, bf16[128,1280]{1,0:T(8,128)(2,1)}, u32[]{:S(2)}, u32[]{:S(2)}) collective-permute-start(bf16[128,1280]{1,0:T(8,128)(2,1)} %layer_out.6), channel_id=1, source_target_pairs={{0,16},{16,32},{32,48},{1,17},{17,33},{33,49},{2,18},{18,34},{34,5... | collective-permute-start | bytes 983048 | tf_op jit(solution)/shard_map/ppermute | solution.py:460
  163.1 9.0 %collective-permute-start.23 = (bf16[64,1280]{1,0:T(8,128)(2,1)S(1)}, bf16[64,1280]{1,0:T(8,128)(2,1)S(1)}, u32[]{:S(2)}, u32[]{:S(2)}) collective-permute-start(bf16[64,1280]{1,0:T(8,128)(2,1)S(1)} %get-tuple-element.71.last_ref), channel_id=1, source_target_pairs={{0,1},{1,2},{2,3},{3,4},{4,5},{5,6},{6,7},{7,8},{8,9},{9,10},{10,1... | collective-permute-start | bytes 491528 | tf_op jit(solution)/shard_map/ppermute | solution.py:430
  168.7 5.0 %collective-permute-start.24 = (bf16[64,1280]{1,0:T(8,128)(2,1)S(1)}, bf16[64,1280]{1,0:T(8,128)(2,1)S(1)}, u32[]{:S(2)}, u32[]{:S(2)}) collective-permute-start(bf16[64,1280]{1,0:T(8,128)(2,1)S(1)} %get-tuple-element.70.first_ref), channel_id=1, source_target_pairs={{1,0},{2,1},{3,2},{4,3},{5,4},{6,5},{7,6},{8,7},{9,8},{10,9},{11,1... | collective-permute-start | bytes 491528 | tf_op jit(solution)/shard_map/ppermute | solution.py:431
  176.6 10.5 %collective-permute-start.25 = (bf16[128,1280]{1,0:T(8,128)(2,1)}, bf16[128,1280]{1,0:T(8,128)(2,1)}, u32[]{:S(2)}, u32[]{:S(2)}) collective-permute-start(bf16[128,1280]{1,0:T(8,128)(2,1)} %layer_out.7), channel_id=1, source_target_pairs={{0,16},{16,32},{32,48},{1,17},{17,33},{33,49},{2,18},{18,34},{34,5... | collective-permute-start | bytes 983048 | tf_op jit(solution)/shard_map/ppermute | solution.py:460
  184.1 22.4 %slice-start = ((s8[5242880]{0:T(1024)(128)(4,1)}), s8[1048576]{0:T(1024)(128)(4,1)S(1)}, s32[]{:S(2)}) async-start(s8[5242880]{0:T(1024)(128)(4,1)} %bitcast.26), calls=%async_computation.3 | async-start | bytes 2097152
  189.1 9.0 %collective-permute-start.26 = (bf16[64,1280]{1,0:T(8,128)(2,1)S(1)}, bf16[64,1280]{1,0:T(8,128)(2,1)S(1)}, u32[]{:S(2)}, u32[]{:S(2)}) collective-permute-start(bf16[64,1280]{1,0:T(8,128)(2,1)S(1)} %get-tuple-element.80.last_ref), channel_id=1, source_target_pairs={{0,1},{1,2},{2,3},{3,4},{4,5},{5,6},{6,7},{7,8},{8,9},{9,10},{10,1... | collective-permute-start | bytes 491528 | tf_op jit(solution)/shard_map/ppermute | solution.py:430
  194.7 4.6 %collective-permute-start.27 = (bf16[64,1280]{1,0:T(8,128)(2,1)S(1)}, bf16[64,1280]{1,0:T(8,128)(2,1)S(1)}, u32[]{:S(2)}, u32[]{:S(2)}) collective-permute-start(bf16[64,1280]{1,0:T(8,128)(2,1)S(1)} %get-tuple-element.79.first_ref), channel_id=1, source_target_pairs={{1,0},{2,1},{3,2},{4,3},{5,4},{6,5},{7,6},{8,7},{9,8},{10,9},{11,1... | collective-permute-start | bytes 491528 | tf_op jit(solution)/shard_map/ppermute | solution.py:431
  202.1 9.8 %collective-permute-start.30 = (bf16[128,1280]{1,0:T(8,128)(2,1)}, bf16[128,1280]{1,0:T(8,128)(2,1)S(1)}, u32[]{:S(2)}, u32[]{:S(2)}) collective-permute-start(bf16[128,1280]{1,0:T(8,128)(2,1)} %layer_out.8.refs_0_), channel_id=1, source_target_pairs={{0,16},{16,32},{32,48},{1,17},{17,33},{33,49},{2,18},{18,34},{34,5... | collective-permute-start | bytes 983048 | tf_op jit(solution)/shard_map/ppermute | solution.py:460
  205.1 16.3 %collective-permute-start.28 = (bf16[128,1280]{1,0:T(8,128)(2,1)}, bf16[128,1280]{1,0:T(8,128)(2,1)}, u32[]{:S(2)}, u32[]{:S(2)}) collective-permute-start(bf16[128,1280]{1,0:T(8,128)(2,1)} %layer_out.8.refs_0_), channel_id=1, source_target_pairs={{48,0},{49,1},{50,2},{51,3},{52,4},{53,5},{54,6},{55,7},{56,8},{57... | collective-permute-start | bytes 983048 | tf_op jit(solution)/shard_map/ppermute | solution.py:453
  212.8 10.1 %collective-permute-start.32 = (bf16[64,1280]{1,0:T(8,128)(2,1)S(1)}, bf16[64,1280]{1,0:T(8,128)(2,1)S(1)}, u32[]{:S(2)}, u32[]{:S(2)}) collective-permute-start(bf16[64,1280]{1,0:T(8,128)(2,1)S(1)} %get-tuple-element.87.last_ref), channel_id=1, source_target_pairs={{0,1},{1,2},{2,3},{3,4},{4,5},{5,6},{6,7},{7,8},{8,9},{9,10},{10,1... | collective-permute-start | bytes 491528 | tf_op jit(solution)/shard_map/ppermute | solution.py:430
  217.4 5.5 %collective-permute-start.33 = (bf16[64,1280]{1,0:T(8,128)(2,1)S(1)}, bf16[64,1280]{1,0:T(8,128)(2,1)S(1)}, u32[]{:S(2)}, u32[]{:S(2)}) collective-permute-start(bf16[64,1280]{1,0:T(8,128)(2,1)S(1)} %get-tuple-element.86.first_ref), channel_id=1, source_target_pairs={{1,0},{2,1},{3,2},{4,3},{5,4},{6,5},{7,6},{8,7},{9,8},{10,9},{11,1... | collective-permute-start | bytes 491528 | tf_op jit(solution)/shard_map/ppermute | solution.py:431
  218.7 8.6 %collective-permute-start.29 = (bf16[128,1280]{1,0:T(8,128)(2,1)}, bf16[128,1280]{1,0:T(8,128)(2,1)S(1)}, u32[]{:S(2)}, u32[]{:S(2)}) collective-permute-start(bf16[128,1280]{1,0:T(8,128)(2,1)} %layer_out.8.refs_0_), channel_id=1, source_target_pairs={{48,32},{49,33},{50,34},{51,35},{52,36},{53,37},{54,38},{55,39},{5... | collective-permute-start | bytes 983048 | tf_op jit(solution)/shard_map/ppermute | solution.py:453
  221.4 25.4 %copy-start.18 = (bf16[1280,512]{1,0:T(8,128)(2,1)S(1)}, bf16[1280,512]{1,0:T(8,128)(2,1)}, u32[]{:S(2)}) copy-start(bf16[1280,512]{1,0:T(8,128)(2,1)} %copy-done.17) | copy-start | bytes 3932164
  221.4 11.3 %collective-permute-start.31 = (bf16[128,1280]{1,0:T(8,128)(2,1)}, bf16[128,1280]{1,0:T(8,128)(2,1)S(1)}, u32[]{:S(2)}, u32[]{:S(2)}) collective-permute-start(bf16[128,1280]{1,0:T(8,128)(2,1)} %collective-permute-done.28.refs_1_), channel_id=1, source_target_pairs={{0,16},{1,17},{2,18},{3,19},{4,20},{5,21},{6,22},{7,23},{8,24},{9,... | collective-permute-start | bytes 983048 | tf_op jit(solution)/shard_map/ppermute | solution.py:442
  224.5 8.2 %collective-permute-start.34 = (bf16[128,1280]{1,0:T(8,128)(2,1)S(1)}, bf16[128,1280]{1,0:T(8,128)(2,1)S(1)}, u32[]{:S(2)}, u32[]{:S(2)}) collective-permute-start(bf16[128,1280]{1,0:T(8,128)(2,1)S(1)} %layer_out.9.refs_4_), channel_id=1, source_target_pairs={{48,0},{49,1},{50,2},{51,3},{52,4},{53,5},{54,6},{55,7},{56,8},{57... | collective-permute-start | bytes 983048 | tf_op jit(solution)/shard_map/ppermute | solution.py:453
  225.2 7.6 %collective-permute-start.35 = (bf16[128,1280]{1,0:T(8,128)(2,1)S(1)}, bf16[128,1280]{1,0:T(8,128)(2,1)S(1)}, u32[]{:S(2)}, u32[]{:S(2)}) collective-permute-start(bf16[128,1280]{1,0:T(8,128)(2,1)S(1)} %layer_out.9.refs_4_), channel_id=1, source_target_pairs={{48,32},{49,33},{50,34},{51,35},{52,36},{53,37},{54,38},{55,39},{5... | collective-permute-start | bytes 983048 | tf_op jit(solution)/shard_map/ppermute | solution.py:453
  225.9 20.9 %collective-permute-start.36 = (bf16[128,1280]{1,0:T(8,128)(2,1)S(1)}, bf16[128,1280]{1,0:T(8,128)(2,1)S(1)}, u32[]{:S(2)}, u32[]{:S(2)}) collective-permute-start(bf16[128,1280]{1,0:T(8,128)(2,1)S(1)} %layer_out.9.refs_4_), channel_id=1, source_target_pairs={{48,16},{49,17},{50,18},{51,19},{52,20},{53,21},{54,22},{55,23},{5... | collective-permute-start | bytes 983048 | tf_op jit(solution)/shard_map/ppermute | solution.py:457
  (31 other events, 190.9 us)
Sparse Core Ops, SparseCore 0:
  11.7 89.3 all-gather.6
  103.2 43.9 all-gather.4

commit v4 on v3

--- a/solution.py
+++ b/solution.py
@@ -40,15 +40,17 @@
     for index, out_ref in enumerate(outs):
         cols = slice(start, start + out_ref.shape[1])
         start += out_ref.shape[1]
+        row = 0
         for slot, piece in enumerate(pieces):
             height = piece.shape[0]
             copies.append(
                 pltpu.make_async_copy(
                     piece.at[:, cols],
-                    out_ref.at[pl.ds(slot * height, height), :],
+                    out_ref.at[pl.ds(row, height), :],
                     sems.at[index, slot],
                 )
             )
+            row += height
     for copy in copies:
         copy.start()
     for copy in copies:
@@ -296,28 +298,28 @@
     def around(value, axis, size, step):
         return lax.ppermute(value, axis, [(i, (i + step) % size) for i in range(size)])
 
-    group = lax.axis_index("dp")
     own = jnp.concatenate([enc_qkv[0], enc_out[0].T], axis=1)
-    blocks, steps = [own], [0]
-    for step, count in ((1, groups // 2), (-1, (groups - 1) // 2)):
-        moving = own
-        for hop in range(count):
-            moving = around(moving, "dp", groups, step)
-            blocks.append(moving)
-            steps.append(step * (hop + 1))
-    block = jnp.concatenate(blocks, axis=0)
+    lanes = own.reshape(-1, 128)
+    block = lax.all_to_all(
+        jnp.broadcast_to(lanes[None], (groups,) + lanes.shape), "dp", 0, 0, tiled=True
+    ).reshape(groups * own.shape[0], own.shape[1])
     chips = shards // 2
     ring, source = [block], [shard]
-    for step, count in ((2, chips // 2), (-2, (chips - 1) // 2)):
+    ends = []
+    for step in (2, -2):
         moving = block
-        for hop in range(count):
+        for hop in range(chips // 2 - 1):
             moving = around(moving, "tm", shards, step)
             ring.append(moving)
             source.append((shard - step * (hop + 1)) % shards)
-    swap = [(i, i ^ 1) for i in range(shards)]
+        ends.append(moving)
+    cut = block.shape[0] * 3 // 5
+    ring.append(around(ends[0][:cut], "tm", shards, 2))
+    ring.append(around(ends[1][cut:], "tm", shards, -2))
+    source.append((shard + chips) % shards)
     source = jnp.stack(source + [place ^ 1 for place in source])
     each = model // (groups * shards)
-    slots = (group - jnp.array(steps)) % groups
+    slots = jnp.arange(groups)
     order = (slots[None, :, None] * shards + source[:, None, None]) * each + jnp.arange(each)
     order = order.reshape(-1).astype(jnp.int32)
 

time: 299 us -> 290 us (0.970)
  blocking collectives: 36.7 us -> 64.1 us
  starting transfers between devices: 108 us -> 84 us
  waiting for transfers between devices: 63.4 us -> 51.6 us
    all_to_all x0 -> x1, blocking collectives: none -> 25.1 us  [per_device(): lax.all_to_all(jnp.broadcast_to(lanes[None], (groups,) + lanes.shape), 'd...]
    ppermute x14 -> x8, starting transfers between devices: 52.9 us -> 29 us  [around(): lax.ppermute(value, axis, [(i, (i + step) % size) for i in range(size)])]
    ppermute x14 -> x8, waiting for transfers between devices: 33.2 us -> 20.6 us  [around(): lax.ppermute(value, axis, [(i, (i + step) % size) for i in range(size)])]
    unnamed x80 -> x78, local copies, waits for them, and re-layouts: 14.3 us -> 14.5 us
  transfers between devices with their start and end apart: 39 -> 33, of which waited for: 16 -> 12; matrix products, arithmetic and copies ran while one was open for 4% -> 4% of each run, Pallas kernels for 12% -> 12%
where the time goes in v4:
time: 290 us; the launch traced here: 288 us
  starting transfers between devices  84 us (29%)
  blocking collectives  64.1 us (22%)
  waiting for transfers between devices  51.6 us (18%)
  Pallas kernels  45.6 us (16%)
  local copies, waits for them, and re-layouts  22.4 us (8%)
  between operations  14.9 us (5%)
  other arithmetic  5.15 us (2%)
    ppermute x8, starting transfers between devices, around(): lax.ppermute(value, axis, [(i, (i + step) % size) for i in range(size)])  29 us
    all_to_all x1, blocking collectives, per_device(): lax.all_to_all(jnp.broadcast_to(lanes[None], (groups,) + lanes.shape), 'd...  25.1 us
    all_gather x1, blocking collectives, per_device(): everyone = lax.all_gather(pieces, 'tm', axis=0)  24.1 us
    ppermute x5, starting transfers between devices, per_device(): left = lax.ppermute(last, 'tm', up)  23.2 us
    ppermute x8, waiting for transfers between devices, around(): lax.ppermute(value, axis, [(i, (i + step) % size) for i in range(size)])  20.6 us
    all_to_all x1, blocking collectives, per_device(): grad = lax.all_to_all(grad, 'dp', 0, 0, tiled=True)  14.9 us
    unnamed x78, local copies, waits for them, and re-layouts  14.5 us
    ppermute x1, waiting for transfers between devices, per_device(): sent.append(lax.ppermute(finished, 'section', [(sections - 1, 1)]))  14 us
  transfers between devices with their start and end apart: 33, of which 12 were waited for; matrix products, arithmetic and copies ran while one was open for 4% of the time, Pallas kernels for 12%

profile of v4, /device:TPU:2, one launch (start us, length us, event | category | flops | bytes accessed | tf_op | source)
XLA Modules:
  0.0 287.7 jit_solution(7301500974451913059)
XLA Ops:
  11.4 25.1 %all_to_all.10 = bf16[8,200,128]{2,1,0:T(8,128)(2,1)S(1)} all-to-all(bf16[8,200,128]{2,1,0:T(8,128)(2,1)S(1)} %broadcast_in_dim.5), channel_id=1, replica_groups=mesh['dp'=8,'section'=4,'tm'=16] {'dp'}, dimensions={0} | all-to-all | bytes 819200 | tf_op jit(solution)/shard_map/all_to_all | solution.py:303
  37.1 3.5 %collective-permute-start = (bf16[80,2560]{1,0:T(8,128)(2,1)S(1)}, bf16[80,2560]{1,0:T(8,128)(2,1)S(1)}, u32[]{:S(2)}, u32[]{:S(2)}) collective-permute-start(bf16[80,2560]{1,0:T(8,128)(2,1)S(1)} %reshape.103.refs_0_), channel_id=1, source_target_pairs={{0,2},{1,3},{2,4},{3,5},{4,6},{5,7},{6,8},{7,9},{8,10},{9,11},{10,... | collective-permute-start | bytes 1228808 | tf_op jit(solution)/shard_map/ppermute | solution.py:299
  40.6 3.8 %collective-permute-start.3 = (bf16[80,2560]{1,0:T(8,128)(2,1)S(1)}, bf16[80,2560]{1,0:T(8,128)(2,1)S(1)}, u32[]{:S(2)}, u32[]{:S(2)}) collective-permute-start(bf16[80,2560]{1,0:T(8,128)(2,1)S(1)} %reshape.103.refs_0_), channel_id=1, source_target_pairs={{0,14},{1,15},{2,0},{3,1},{4,2},{5,3},{6,4},{7,5},{8,6},{9,7},{10,... | collective-permute-start | bytes 1228808 | tf_op jit(solution)/shard_map/ppermute | solution.py:299
  44.4 6.3 %collective-permute-done.refs_1_ = bf16[80,2560]{1,0:T(8,128)(2,1)S(1)} collective-permute-done((bf16[80,2560]{1,0:T(8,128)(2,1)S(1)}, bf16[80,2560]{1,0:T(8,128)(2,1)S(1)}, u32[]{:S(2)}, u32[]{:S(2)}) %collective-permute-start) | collective-permute-done | bytes 409632 | tf_op jit(solution)/shard_map/ppermute | solution.py:299
  50.7 1.9 collective-permute-start.1
  52.6 5.1 %collective-permute-start.4 = (bf16[80,2560]{1,0:T(8,128)(2,1)S(1)}, bf16[80,2560]{1,0:T(8,128)(2,1)S(1)}, u32[]{:S(2)}, u32[]{:S(2)}) collective-permute-start(bf16[80,2560]{1,0:T(8,128)(2,1)S(1)} %collective-permute-done.3.refs_4_), channel_id=1, source_target_pairs={{0,14},{1,15},{2,0},{3,1},{4,2},{5,3},{6,4},{7,5},{8,6},{9,7},{10,... | collective-permute-start | bytes 1228808 | tf_op jit(solution)/shard_map/ppermute | solution.py:299
  57.7 5.2 %collective-permute-done.1.refs_2_ = bf16[80,2560]{1,0:T(8,128)(2,1)S(1)} collective-permute-done((bf16[80,2560]{1,0:T(8,128)(2,1)S(1)}, bf16[80,2560]{1,0:T(8,128)(2,1)S(1)}, u32[]{:S(2)}, u32[]{:S(2)}) %collective-permute-start.1) | collective-permute-done | bytes 409632 | tf_op jit(solution)/shard_map/ppermute | solution.py:299
  62.9 1.9 collective-permute-start.2
  64.8 5.1 %collective-permute-start.5 = (bf16[80,2560]{1,0:T(8,128)(2,1)S(1)}, bf16[80,2560]{1,0:T(8,128)(2,1)S(1)}, u32[]{:S(2)}, u32[]{:S(2)}) collective-permute-start(bf16[80,2560]{1,0:T(8,128)(2,1)S(1)} %collective-permute-done.4.refs_5_), channel_id=1, source_target_pairs={{0,14},{1,15},{2,0},{3,1},{4,2},{5,3},{6,4},{7,5},{8,6},{9,7},{10,... | collective-permute-start | bytes 1228808 | tf_op jit(solution)/shard_map/ppermute | solution.py:299
  70.0 5.3 %collective-permute-done.2.refs_3_ = bf16[80,2560]{1,0:T(8,128)(2,1)S(1)} collective-permute-done((bf16[80,2560]{1,0:T(8,128)(2,1)S(1)}, bf16[80,2560]{1,0:T(8,128)(2,1)S(1)}, u32[]{:S(2)}, u32[]{:S(2)}) %collective-permute-start.2) | collective-permute-done | bytes 409632 | tf_op jit(solution)/shard_map/ppermute | solution.py:299
  75.3 2.1 collective-permute-start.6
  77.4 5.5 %collective-permute-start.7 = (bf16[32,2560]{1,0:T(8,128)(2,1)S(1)}, bf16[32,2560]{1,0:T(8,128)(2,1)}, u32[]{:S(2)}, u32[]{:S(2)}) collective-permute-start(bf16[32,2560]{1,0:T(8,128)(2,1)S(1)} %slice.13), channel_id=1, source_target_pairs={{0,14},{1,15},{2,0},{3,1},{4,2},{5,3},{6,4},{7,5},{8,6},{9,7},{10,... | collective-permute-start | bytes 491528 | tf_op jit(solution)/shard_map/ppermute | solution.py:299
  83.0 3.8 %collective-permute-done.7.refs_8_ = bf16[32,2560]{1,0:T(8,128)(2,1)} collective-permute-done((bf16[32,2560]{1,0:T(8,128)(2,1)S(1)}, bf16[32,2560]{1,0:T(8,128)(2,1)}, u32[]{:S(2)}, u32[]{:S(2)}) %collective-permute-start.7) | collective-permute-done | bytes 163872 | tf_op jit(solution)/shard_map/ppermute | solution.py:299
  86.9 4.0 %join.1 = (bf16[640,640]{1,0:T(8,128)(2,1)}, bf16[640,1280]{1,0:T(8,128)(2,1)}, bf16[640,640]{1,0:T(8,128)(2,1)}) custom-call(bf16[80,2560]{1,0:T(8,128)(2,1)} %copy-done.28, bf16[80,2560]{1,0:T(8,128)(2,1)} %copy-done.31, bf16[80,2560]{1,0:T(8,128)(2,1)} %copy-done.33, bf16[80,2560]{1,0:T(8,128)(2,1)} %copy-done.29, bf16[80,2560]{1,0:T(8,128)(2,1)} %copy-done.32, ...), custom_call_target="tpu_custom_call" | custom-call | tf_op jit(solution)/shard_map/join/pallas_call | solution.py:327
  90.9 1.9 collective-permute-start.8
  92.9 2.4 collective-permute-start.9
  95.3 1.9 collective-permute-start.12
  103.4 2.5 collective-permute-start.10
  109.6 2.2 own_blocks.5
  111.8 2.9 %layer_out.5 = bf16[128,1280]{1,0:T(8,128)(2,1)} custom-call(s32[6]{0:T(128)S(1)} %stack.60.place_ref, s32[8]{0:T(128)S(1)} %reshape.102.mask_ref, bf16[128,640]{1,0:T(8,128)(2,1)S(1)} %get-tuple-element.56.q_ref, f32[128,640]{1,0:T(8,128)S(1)} %get-tuple-element.57.num_ref, f32[128,640]{1,0:T(8,128)S(1)} %get-tuple-element.58.den_ref, ...), custom_call_target="tpu_custom_call" | custom-call | tf_op jit(solution)/shard_map/layer_out/pallas_call | solution.py:445
  114.8 3.4 %collective-permute-start.13 = (bf16[128,1280]{1,0:T(8,128)(2,1)}, bf16[128,1280]{1,0:T(8,128)(2,1)}, u32[]{:S(2)}, u32[]{:S(2)}) collective-permute-start(bf16[128,1280]{1,0:T(8,128)(2,1)} %layer_out.5), channel_id=1, source_target_pairs={{0,16},{16,32},{32,48},{1,17},{17,33},{33,49},{2,18},{18,34},{34,5... | collective-permute-start | bytes 983048 | tf_op jit(solution)/shard_map/ppermute | solution.py:462
  118.2 5.0 %reshape.107.w_ref = bf16[1280,768]{1,0:T(8,128)(2,1)} reshape(bf16[128,10,768]{2,1,0:T(8,128)(2,1)} %all-gather.7.cloned.1.call-done) | data formatting | bytes 3932160 | tf_op jit(solution)/shard_map/optimization_barrier | solution.py:374
  123.3 4.1 %collective-permute-done.13 = bf16[128,1280]{1,0:T(8,128)(2,1)} collective-permute-done((bf16[128,1280]{1,0:T(8,128)(2,1)}, bf16[128,1280]{1,0:T(8,128)(2,1)}, u32[]{:S(2)}, u32[]{:S(2)}) %collective-permute-start.13) | collective-permute-done | bytes 327712 | tf_op jit(solution)/shard_map/ppermute | solution.py:462
  129.3 2.3 collective-permute-start.14
  133.0 2.0 own_blocks.6
  136.7 2.4 layer_out.6
  139.1 3.4 %collective-permute-start.16 = (bf16[128,1280]{1,0:T(8,128)(2,1)}, bf16[128,1280]{1,0:T(8,128)(2,1)}, u32[]{:S(2)}, u32[]{:S(2)}) collective-permute-start(bf16[128,1280]{1,0:T(8,128)(2,1)} %layer_out.6), channel_id=1, source_target_pairs={{0,16},{16,32},{32,48},{1,17},{17,33},{33,49},{2,18},{18,34},{34,5... | collective-permute-start | bytes 983048 | tf_op jit(solution)/shard_map/ppermute | solution.py:462
  149.2 1.9 keys_values.7
  151.2 8.1 %collective-permute-start.17 = (bf16[64,1280]{1,0:T(8,128)(2,1)S(1)}, bf16[64,1280]{1,0:T(8,128)(2,1)S(1)}, u32[]{:S(2)}, u32[]{:S(2)}) collective-permute-start(bf16[64,1280]{1,0:T(8,128)(2,1)S(1)} %get-tuple-element.71.last_ref), channel_id=1, source_target_pairs={{0,1},{1,2},{2,3},{3,4},{4,5},{5,6},{6,7},{7,8},{8,9},{9,10},{10,1... | collective-permute-start | bytes 491528 | tf_op jit(solution)/shard_map/ppermute | solution.py:432
  160.5 2.0 own_blocks.7
  164.0 2.8 layer_out.7
  166.8 2.9 %collective-permute-start.19 = (bf16[128,1280]{1,0:T(8,128)(2,1)}, bf16[128,1280]{1,0:T(8,128)(2,1)}, u32[]{:S(2)}, u32[]{:S(2)}) collective-permute-start(bf16[128,1280]{1,0:T(8,128)(2,1)} %layer_out.7), channel_id=1, source_target_pairs={{0,16},{16,32},{32,48},{1,17},{17,33},{33,49},{2,18},{18,34},{34,5... | collective-permute-start | bytes 983048 | tf_op jit(solution)/shard_map/ppermute | solution.py:462
  169.9 2.5 copy-done.2
  173.9 2.2 queries.1.q_ref
  176.8 2.0 keys_values.8
  178.9 5.6 %collective-permute-start.20 = (bf16[64,1280]{1,0:T(8,128)(2,1)S(1)}, bf16[64,1280]{1,0:T(8,128)(2,1)S(1)}, u32[]{:S(2)}, u32[]{:S(2)}) collective-permute-start(bf16[64,1280]{1,0:T(8,128)(2,1)S(1)} %get-tuple-element.80.last_ref), channel_id=1, source_target_pairs={{0,1},{1,2},{2,3},{3,4},{4,5},{5,6},{6,7},{7,8},{8,9},{9,10},{10,1... | collective-permute-start | bytes 491528 | tf_op jit(solution)/shard_map/ppermute | solution.py:432
  185.8 2.0 own_blocks.8
  189.7 2.8 layer_out.8.refs_0_
  192.5 3.1 %collective-permute-start.24 = (bf16[128,1280]{1,0:T(8,128)(2,1)}, bf16[128,1280]{1,0:T(8,128)(2,1)S(1)}, u32[]{:S(2)}, u32[]{:S(2)}) collective-permute-start(bf16[128,1280]{1,0:T(8,128)(2,1)} %layer_out.8.refs_0_), channel_id=1, source_target_pairs={{0,16},{16,32},{32,48},{1,17},{17,33},{33,49},{2,18},{18,34},{34,5... | collective-permute-start | bytes 983048 | tf_op jit(solution)/shard_map/ppermute | solution.py:462
  198.4 3.9 %collective-permute-done.24.x_ref = bf16[128,1280]{1,0:T(8,128)(2,1)S(1)} collective-permute-done((bf16[128,1280]{1,0:T(8,128)(2,1)}, bf16[128,1280]{1,0:T(8,128)(2,1)S(1)}, u32[]{:S(2)}, u32[]{:S(2)}) %collective-permute-start.24) | collective-permute-done | bytes 327712 | tf_op jit(solution)/shard_map/ppermute | solution.py:462
  203.2 4.6 %collective-permute-start.26 = (bf16[64,1280]{1,0:T(8,128)(2,1)S(1)}, bf16[64,1280]{1,0:T(8,128)(2,1)S(1)}, u32[]{:S(2)}, u32[]{:S(2)}) collective-permute-start(bf16[64,1280]{1,0:T(8,128)(2,1)S(1)} %get-tuple-element.87.last_ref), channel_id=1, source_target_pairs={{0,1},{1,2},{2,3},{3,4},{4,5},{5,6},{6,7},{7,8},{8,9},{9,10},{10,1... | collective-permute-start | bytes 491528 | tf_op jit(solution)/shard_map/ppermute | solution.py:432
  209.8 2.0 own_blocks.9
  218.5 3.0 %collective-permute-done.25.refs_3_ = bf16[128,1280]{1,0:T(8,128)(2,1)S(1)} collective-permute-done((bf16[128,1280]{1,0:T(8,128)(2,1)}, bf16[128,1280]{1,0:T(8,128)(2,1)S(1)}, u32[]{:S(2)}, u32[]{:S(2)}) %collective-permute-start.25) | collective-permute-done | bytes 327712 | tf_op jit(solution)/shard_map/ppermute | solution.py:444
  221.5 14.0 %collective-permute-done.30.refs_7_ = bf16[128,1280]{1,0:T(8,128)(2,1)S(1)} collective-permute-done((bf16[128,1280]{1,0:T(8,128)(2,1)S(1)}, bf16[128,1280]{1,0:T(8,128)(2,1)S(1)}, u32[]{:S(2)}, u32[]{:S(2)}) %collective-permute-start.30) | collective-permute-done | bytes 327712 | tf_op jit(solution)/shard_map/ppermute | solution.py:459
  236.4 2.3 cross.1
  238.7 24.1 %all-gather = bf16[3584,128]{1,0:T(8,128)(2,1)S(1)} all-gather(bf16[224,128]{1,0:T(8,128)(2,1)S(1)} %cross.1), channel_id=2, replica_groups=mesh['dp'=8,'section'=4,'tm'=16] {'tm'}, dimensions={0}, use_global_device_ids=true | all-gather | bytes 974848 | tf_op jit(solution)/shard_map/all_gather | solution.py:472
  262.8 2.6 combine.1
  265.4 14.9 %all_to_all.11 = bf16[8,16,256]{2,1,0:T(8,128)(2,1)S(1)} all-to-all(bf16[8,16,256]{2,1,0:T(8,128)(2,1)S(1)} %get-tuple-element.95), channel_id=1, replica_groups=mesh['dp'=8,'section'=4,'tm'=16] {'dp'}, dimensions={0} | all-to-all | bytes 131072 | tf_op jit(solution)/shard_map/all_to_all | solution.py:486
  (147 shorter events, 48.1 us)
Async XLA Ops:
  7.2 111.1 %all-gather.7.cloned.1.call-start = ((), (), s32[]{:S(2)}) async-start(), calls=%async_computation.3 | async-start | bytes 3170304 | tf_op jit(solution)/shard_map/all_gather | solution.py:340
  8.6 161.3 %all-gather.5.cloned.1.call-start = ((), (), s32[]{:S(2)}) async-start(), calls=%async_computation.2 | async-start | bytes 5570560 | tf_op jit(solution)/shard_map/all_gather | solution.py:341
  37.1 49.8 %copy-start.28 = (bf16[80,2560]{1,0:T(8,128)(2,1)}, bf16[80,2560]{1,0:T(8,128)(2,1)S(1)}, u32[]{:S(2)}) copy-start(bf16[80,2560]{1,0:T(8,128)(2,1)S(1)} %reshape.103.refs_0_) | copy-start | bytes 1228804
  37.1 13.6 %collective-permute-start = (bf16[80,2560]{1,0:T(8,128)(2,1)S(1)}, bf16[80,2560]{1,0:T(8,128)(2,1)S(1)}, u32[]{:S(2)}, u32[]{:S(2)}) collective-permute-start(bf16[80,2560]{1,0:T(8,128)(2,1)S(1)} %reshape.103.refs_0_), channel_id=1, source_target_pairs={{0,2},{1,3},{2,4},{3,5},{4,6},{5,7},{6,8},{7,9},{8,10},{9,11},{10,... | collective-permute-start | bytes 1228808 | tf_op jit(solution)/shard_map/ppermute | solution.py:299
  40.6 12.0 %collective-permute-start.3 = (bf16[80,2560]{1,0:T(8,128)(2,1)S(1)}, bf16[80,2560]{1,0:T(8,128)(2,1)S(1)}, u32[]{:S(2)}, u32[]{:S(2)}) collective-permute-start(bf16[80,2560]{1,0:T(8,128)(2,1)S(1)} %reshape.103.refs_0_), channel_id=1, source_target_pairs={{0,14},{1,15},{2,0},{3,1},{4,2},{5,3},{6,4},{7,5},{8,6},{9,7},{10,... | collective-permute-start | bytes 1228808 | tf_op jit(solution)/shard_map/ppermute | solution.py:299
  50.7 36.2 %copy-start.31 = (bf16[80,2560]{1,0:T(8,128)(2,1)}, bf16[80,2560]{1,0:T(8,128)(2,1)S(1)}, u32[]{:S(2)}) copy-start(bf16[80,2560]{1,0:T(8,128)(2,1)S(1)} %collective-permute-done.refs_1_) | copy-start | bytes 1228804
  50.7 12.2 %collective-permute-start.1 = (bf16[80,2560]{1,0:T(8,128)(2,1)S(1)}, bf16[80,2560]{1,0:T(8,128)(2,1)S(1)}, u32[]{:S(2)}, u32[]{:S(2)}) collective-permute-start(bf16[80,2560]{1,0:T(8,128)(2,1)S(1)} %collective-permute-done.refs_1_), channel_id=1, source_target_pairs={{0,2},{1,3},{2,4},{3,5},{4,6},{5,7},{6,8},{7,9},{8,10},{9,11},{10,... | collective-permute-start | bytes 1228808 | tf_op jit(solution)/shard_map/ppermute | solution.py:299
  52.6 34.2 %copy-start.32 = (bf16[80,2560]{1,0:T(8,128)(2,1)}, bf16[80,2560]{1,0:T(8,128)(2,1)S(1)}, u32[]{:S(2)}) copy-start(bf16[80,2560]{1,0:T(8,128)(2,1)S(1)} %collective-permute-done.3.refs_4_) | copy-start | bytes 1228804
  52.6 12.2 %collective-permute-start.4 = (bf16[80,2560]{1,0:T(8,128)(2,1)S(1)}, bf16[80,2560]{1,0:T(8,128)(2,1)S(1)}, u32[]{:S(2)}, u32[]{:S(2)}) collective-permute-start(bf16[80,2560]{1,0:T(8,128)(2,1)S(1)} %collective-permute-done.3.refs_4_), channel_id=1, source_target_pairs={{0,14},{1,15},{2,0},{3,1},{4,2},{5,3},{6,4},{7,5},{8,6},{9,7},{10,... | collective-permute-start | bytes 1228808 | tf_op jit(solution)/shard_map/ppermute | solution.py:299
  62.9 23.9 %copy-start.33 = (bf16[80,2560]{1,0:T(8,128)(2,1)}, bf16[80,2560]{1,0:T(8,128)(2,1)S(1)}, u32[]{:S(2)}) copy-start(bf16[80,2560]{1,0:T(8,128)(2,1)S(1)} %collective-permute-done.1.refs_2_) | copy-start | bytes 1228804
  62.9 12.4 %collective-permute-start.2 = (bf16[80,2560]{1,0:T(8,128)(2,1)S(1)}, bf16[80,2560]{1,0:T(8,128)(2,1)S(1)}, u32[]{:S(2)}, u32[]{:S(2)}) collective-permute-start(bf16[80,2560]{1,0:T(8,128)(2,1)S(1)} %collective-permute-done.1.refs_2_), channel_id=1, source_target_pairs={{0,2},{1,3},{2,4},{3,5},{4,6},{5,7},{6,8},{7,9},{8,10},{9,11},{10,... | collective-permute-start | bytes 1228808 | tf_op jit(solution)/shard_map/ppermute | solution.py:299
  64.8 22.0 %copy-start.34 = (bf16[80,2560]{1,0:T(8,128)(2,1)}, bf16[80,2560]{1,0:T(8,128)(2,1)S(1)}, u32[]{:S(2)}) copy-start(bf16[80,2560]{1,0:T(8,128)(2,1)S(1)} %collective-permute-done.4.refs_5_) | copy-start | bytes 1228804
  64.8 12.5 %collective-permute-start.5 = (bf16[80,2560]{1,0:T(8,128)(2,1)S(1)}, bf16[80,2560]{1,0:T(8,128)(2,1)S(1)}, u32[]{:S(2)}, u32[]{:S(2)}) collective-permute-start(bf16[80,2560]{1,0:T(8,128)(2,1)S(1)} %collective-permute-done.4.refs_5_), channel_id=1, source_target_pairs={{0,14},{1,15},{2,0},{3,1},{4,2},{5,3},{6,4},{7,5},{8,6},{9,7},{10,... | collective-permute-start | bytes 1228808 | tf_op jit(solution)/shard_map/ppermute | solution.py:299
  75.3 11.6 %copy-start.29 = (bf16[80,2560]{1,0:T(8,128)(2,1)}, bf16[80,2560]{1,0:T(8,128)(2,1)S(1)}, u32[]{:S(2)}) copy-start(bf16[80,2560]{1,0:T(8,128)(2,1)S(1)} %collective-permute-done.2.refs_3_) | copy-start | bytes 1228804
  75.3 22.4 %copy-start.22 = (bf16[2,128,1280]{2,1,0:T(8,128)(2,1)S(1)}, bf16[2,128,1280]{2,1,0:T(8,128)(2,1)}, u32[]{:S(2)}) copy-start(bf16[2,128,1280]{2,1,0:T(8,128)(2,1)} %frames_ref.1) | copy-start | bytes 1966084
  75.3 11.5 %collective-permute-start.6 = (bf16[48,2560]{1,0:T(8,128)(2,1)S(1)}, bf16[48,2560]{1,0:T(8,128)(2,1)}, u32[]{:S(2)}, u32[]{:S(2)}) collective-permute-start(bf16[48,2560]{1,0:T(8,128)(2,1)S(1)} %slice.12), channel_id=1, source_target_pairs={{0,2},{1,3},{2,4},{3,5},{4,6},{5,7},{6,8},{7,9},{8,10},{9,11},{10,... | collective-permute-start | bytes 737288 | tf_op jit(solution)/shard_map/ppermute | solution.py:299
  77.4 9.4 %collective-permute-start.7 = (bf16[32,2560]{1,0:T(8,128)(2,1)S(1)}, bf16[32,2560]{1,0:T(8,128)(2,1)}, u32[]{:S(2)}, u32[]{:S(2)}) collective-permute-start(bf16[32,2560]{1,0:T(8,128)(2,1)S(1)} %slice.13), channel_id=1, source_target_pairs={{0,14},{1,15},{2,0},{3,1},{4,2},{5,3},{6,4},{7,5},{8,6},{9,7},{10,... | collective-permute-start | bytes 491528 | tf_op jit(solution)/shard_map/ppermute | solution.py:299
  90.9 8.6 %collective-permute-start.8 = (bf16[640,1280]{1,0:T(8,128)(2,1)}, bf16[640,1280]{1,0:T(8,128)(2,1)S(1)}, u32[]{:S(2)}, u32[]{:S(2)}) collective-permute-start(bf16[640,1280]{1,0:T(8,128)(2,1)} %get-tuple-element.51.near_ref), channel_id=1, source_target_pairs={{0,1},{1,0},{2,3},{3,2},{4,5},{5,4},{6,7},{7,6},{8,9},{9,8},{10,11... | collective-permute-start | bytes 4915208 | tf_op jit(solution)/shard_map/ppermute | solution.py:337
  92.9 14.6 %collective-permute-start.9 = (bf16[640,640]{1,0:T(8,128)(2,1)}, bf16[640,640]{1,0:T(8,128)(2,1)}, u32[]{:S(2)}, u32[]{:S(2)}) collective-permute-start(bf16[640,640]{1,0:T(8,128)(2,1)} %get-tuple-element.55.near_ref), channel_id=1, source_target_pairs={{0,1},{1,0},{2,3},{3,2},{4,5},{5,4},{6,7},{7,6},{8,9},{9,8},{10,11... | collective-permute-start | bytes 2457608 | tf_op jit(solution)/shard_map/ppermute | solution.py:337
  95.3 16.5 %collective-permute-start.12 = (bf16[640,640]{1,0:T(8,128)(2,1)}, bf16[640,640]{1,0:T(8,128)(2,1)S(1)}, u32[]{:S(2)}, u32[]{:S(2)}) collective-permute-start(bf16[640,640]{1,0:T(8,128)(2,1)} %get-tuple-element.59.near_ref), channel_id=1, source_target_pairs={{0,1},{1,0},{2,3},{3,2},{4,5},{5,4},{6,7},{7,6},{8,9},{9,8},{10,11... | collective-permute-start | bytes 2457608 | tf_op jit(solution)/shard_map/ppermute | solution.py:337
  103.4 8.4 %collective-permute-start.10 = (bf16[64,1280]{1,0:T(8,128)(2,1)}, bf16[64,1280]{1,0:T(8,128)(2,1)S(1)}, u32[]{:S(2)}, u32[]{:S(2)}) collective-permute-start(bf16[64,1280]{1,0:T(8,128)(2,1)} %get-tuple-element.54.last_ref), channel_id=1, source_target_pairs={{0,1},{1,2},{2,3},{3,4},{4,5},{5,6},{6,7},{7,8},{8,9},{9,10},{10,1... | collective-permute-start | bytes 491528 | tf_op jit(solution)/shard_map/ppermute | solution.py:432
  106.0 5.9 %collective-permute-start.11 = (bf16[64,1280]{1,0:T(8,128)(2,1)}, bf16[64,1280]{1,0:T(8,128)(2,1)}, u32[]{:S(2)}, u32[]{:S(2)}) collective-permute-start(bf16[64,1280]{1,0:T(8,128)(2,1)} %get-tuple-element.53.first_ref), channel_id=1, source_target_pairs={{1,0},{2,1},{3,2},{4,3},{5,4},{6,5},{7,6},{8,7},{9,8},{10,9},{11,1... | collective-permute-start | bytes 491528 | tf_op jit(solution)/shard_map/ppermute | solution.py:433
  114.8 12.6 %collective-permute-start.13 = (bf16[128,1280]{1,0:T(8,128)(2,1)}, bf16[128,1280]{1,0:T(8,128)(2,1)}, u32[]{:S(2)}, u32[]{:S(2)}) collective-permute-start(bf16[128,1280]{1,0:T(8,128)(2,1)} %layer_out.5), channel_id=1, source_target_pairs={{0,16},{16,32},{32,48},{1,17},{17,33},{33,49},{2,18},{18,34},{34,5... | collective-permute-start | bytes 983048 | tf_op jit(solution)/shard_map/ppermute | solution.py:462
  129.3 5.7 %collective-permute-start.14 = (bf16[64,1280]{1,0:T(8,128)(2,1)S(1)}, bf16[64,1280]{1,0:T(8,128)(2,1)S(1)}, u32[]{:S(2)}, u32[]{:S(2)}) collective-permute-start(bf16[64,1280]{1,0:T(8,128)(2,1)S(1)} %get-tuple-element.63.last_ref), channel_id=1, source_target_pairs={{0,1},{1,2},{2,3},{3,4},{4,5},{5,6},{6,7},{7,8},{8,9},{9,10},{10,1... | collective-permute-start | bytes 491528 | tf_op jit(solution)/shard_map/ppermute | solution.py:432
  131.7 5.0 %collective-permute-start.15 = (bf16[64,1280]{1,0:T(8,128)(2,1)S(1)}, bf16[64,1280]{1,0:T(8,128)(2,1)S(1)}, u32[]{:S(2)}, u32[]{:S(2)}) collective-permute-start(bf16[64,1280]{1,0:T(8,128)(2,1)S(1)} %get-tuple-element.62.first_ref), channel_id=1, source_target_pairs={{1,0},{2,1},{3,2},{4,3},{5,4},{6,5},{7,6},{8,7},{9,8},{10,9},{11,1... | collective-permute-start | bytes 491528 | tf_op jit(solution)/shard_map/ppermute | solution.py:433
  139.1 10.1 %collective-permute-start.16 = (bf16[128,1280]{1,0:T(8,128)(2,1)}, bf16[128,1280]{1,0:T(8,128)(2,1)}, u32[]{:S(2)}, u32[]{:S(2)}) collective-permute-start(bf16[128,1280]{1,0:T(8,128)(2,1)} %layer_out.6), channel_id=1, source_target_pairs={{0,16},{16,32},{32,48},{1,17},{17,33},{33,49},{2,18},{18,34},{34,5... | collective-permute-start | bytes 983048 | tf_op jit(solution)/shard_map/ppermute | solution.py:462
  149.2 11.3 %copy-start.13 = (bf16[640,640]{1,0:T(8,128)(2,1)S(1)}, bf16[640,640]{1,0:T(8,128)(2,1)}, u32[]{:S(2)}) copy-start(bf16[640,640]{1,0:T(8,128)(2,1)} %get-tuple-element.55.near_ref) | copy-start | bytes 2457604
  151.1 12.9 %copy-start.5 = (bf16[640,640]{1,0:T(8,128)(2,1)S(1)}, bf16[640,640]{1,0:T(8,128)(2,1)}, u32[]{:S(2)}) copy-start(bf16[640,640]{1,0:T(8,128)(2,1)} %get-tuple-element.59.near_ref) | copy-start | bytes 2457604
  151.2 12.9 %copy-start.9 = (bf16[640,640]{1,0:T(8,128)(2,1)S(1)}, bf16[640,640]{1,0:T(8,128)(2,1)}, u32[]{:S(2)}) copy-start(bf16[640,640]{1,0:T(8,128)(2,1)} %copy-done.7) | copy-start | bytes 2457604
  151.2 11.4 %collective-permute-start.17 = (bf16[64,1280]{1,0:T(8,128)(2,1)S(1)}, bf16[64,1280]{1,0:T(8,128)(2,1)S(1)}, u32[]{:S(2)}, u32[]{:S(2)}) collective-permute-start(bf16[64,1280]{1,0:T(8,128)(2,1)S(1)} %get-tuple-element.71.last_ref), channel_id=1, source_target_pairs={{0,1},{1,2},{2,3},{3,4},{4,5},{5,6},{6,7},{7,8},{8,9},{9,10},{10,1... | collective-permute-start | bytes 491528 | tf_op jit(solution)/shard_map/ppermute | solution.py:432
  159.2 4.8 %collective-permute-start.18 = (bf16[64,1280]{1,0:T(8,128)(2,1)S(1)}, bf16[64,1280]{1,0:T(8,128)(2,1)S(1)}, u32[]{:S(2)}, u32[]{:S(2)}) collective-permute-start(bf16[64,1280]{1,0:T(8,128)(2,1)S(1)} %get-tuple-element.70.first_ref), channel_id=1, source_target_pairs={{1,0},{2,1},{3,2},{4,3},{5,4},{6,5},{7,6},{8,7},{9,8},{10,9},{11,1... | collective-permute-start | bytes 491528 | tf_op jit(solution)/shard_map/ppermute | solution.py:433
  166.8 10.0 %collective-permute-start.19 = (bf16[128,1280]{1,0:T(8,128)(2,1)}, bf16[128,1280]{1,0:T(8,128)(2,1)}, u32[]{:S(2)}, u32[]{:S(2)}) collective-permute-start(bf16[128,1280]{1,0:T(8,128)(2,1)} %layer_out.7), channel_id=1, source_target_pairs={{0,16},{16,32},{32,48},{1,17},{17,33},{33,49},{2,18},{18,34},{34,5... | collective-permute-start | bytes 983048 | tf_op jit(solution)/shard_map/ppermute | solution.py:462
  173.9 11.9 %copy-start.14 = (bf16[640,640]{1,0:T(8,128)(2,1)S(1)}, bf16[640,640]{1,0:T(8,128)(2,1)}, u32[]{:S(2)}) copy-start(bf16[640,640]{1,0:T(8,128)(2,1)} %get-tuple-element.55.near_ref) | copy-start | bytes 2457604
  173.9 23.0 %slice-start = ((s8[5242880]{0:T(1024)(128)(4,1)}), s8[1048576]{0:T(1024)(128)(4,1)S(1)}, s32[]{:S(2)}) async-start(s8[5242880]{0:T(1024)(128)(4,1)} %bitcast.26), calls=%async_computation.4 | async-start | bytes 2097152
  176.8 20.2 %slice-start.1 = ((s8[5242880]{0:T(1024)(128)(4,1)}), s8[4194304]{0:T(1024)(128)(4,1)S(1)}, s32[]{:S(2)}) async-start(s8[5242880]{0:T(1024)(128)(4,1)} %bitcast.26), calls=%async_computation.5 | async-start | bytes 8388608
  178.8 10.9 %copy-start.6 = (bf16[640,640]{1,0:T(8,128)(2,1)S(1)}, bf16[640,640]{1,0:T(8,128)(2,1)}, u32[]{:S(2)}) copy-start(bf16[640,640]{1,0:T(8,128)(2,1)} %get-tuple-element.59.near_ref) | copy-start | bytes 2457604
  178.9 8.9 %collective-permute-start.20 = (bf16[64,1280]{1,0:T(8,128)(2,1)S(1)}, bf16[64,1280]{1,0:T(8,128)(2,1)S(1)}, u32[]{:S(2)}, u32[]{:S(2)}) collective-permute-start(bf16[64,1280]{1,0:T(8,128)(2,1)S(1)} %get-tuple-element.80.last_ref), channel_id=1, source_target_pairs={{0,1},{1,2},{2,3},{3,4},{4,5},{5,6},{6,7},{7,8},{8,9},{9,10},{10,1... | collective-permute-start | bytes 491528 | tf_op jit(solution)/shard_map/ppermute | solution.py:432
  184.5 5.2 %collective-permute-start.21 = (bf16[64,1280]{1,0:T(8,128)(2,1)S(1)}, bf16[64,1280]{1,0:T(8,128)(2,1)S(1)}, u32[]{:S(2)}, u32[]{:S(2)}) collective-permute-start(bf16[64,1280]{1,0:T(8,128)(2,1)S(1)} %get-tuple-element.79.first_ref), channel_id=1, source_target_pairs={{1,0},{2,1},{3,2},{4,3},{5,4},{6,5},{7,6},{8,7},{9,8},{10,9},{11,1... | collective-permute-start | bytes 491528 | tf_op jit(solution)/shard_map/ppermute | solution.py:433
  192.5 9.8 %collective-permute-start.24 = (bf16[128,1280]{1,0:T(8,128)(2,1)}, bf16[128,1280]{1,0:T(8,128)(2,1)S(1)}, u32[]{:S(2)}, u32[]{:S(2)}) collective-permute-start(bf16[128,1280]{1,0:T(8,128)(2,1)} %layer_out.8.refs_0_), channel_id=1, source_target_pairs={{0,16},{16,32},{32,48},{1,17},{17,33},{33,49},{2,18},{18,34},{34,5... | collective-permute-start | bytes 983048 | tf_op jit(solution)/shard_map/ppermute | solution.py:462
  195.6 16.3 %collective-permute-start.22 = (bf16[128,1280]{1,0:T(8,128)(2,1)}, bf16[128,1280]{1,0:T(8,128)(2,1)}, u32[]{:S(2)}, u32[]{:S(2)}) collective-permute-start(bf16[128,1280]{1,0:T(8,128)(2,1)} %layer_out.8.refs_0_), channel_id=1, source_target_pairs={{48,0},{49,1},{50,2},{51,3},{52,4},{53,5},{54,6},{55,7},{56,8},{57... | collective-permute-start | bytes 983048 | tf_op jit(solution)/shard_map/ppermute | solution.py:455
  203.2 10.1 %collective-permute-start.26 = (bf16[64,1280]{1,0:T(8,128)(2,1)S(1)}, bf16[64,1280]{1,0:T(8,128)(2,1)S(1)}, u32[]{:S(2)}, u32[]{:S(2)}) collective-permute-start(bf16[64,1280]{1,0:T(8,128)(2,1)S(1)} %get-tuple-element.87.last_ref), channel_id=1, source_target_pairs={{0,1},{1,2},{2,3},{3,4},{4,5},{5,6},{6,7},{7,8},{8,9},{9,10},{10,1... | collective-permute-start | bytes 491528 | tf_op jit(solution)/shard_map/ppermute | solution.py:432
  207.8 6.3 %collective-permute-start.27 = (bf16[64,1280]{1,0:T(8,128)(2,1)S(1)}, bf16[64,1280]{1,0:T(8,128)(2,1)S(1)}, u32[]{:S(2)}, u32[]{:S(2)}) collective-permute-start(bf16[64,1280]{1,0:T(8,128)(2,1)S(1)} %get-tuple-element.86.first_ref), channel_id=1, source_target_pairs={{1,0},{2,1},{3,2},{4,3},{5,4},{6,5},{7,6},{8,7},{9,8},{10,9},{11,1... | collective-permute-start | bytes 491528 | tf_op jit(solution)/shard_map/ppermute | solution.py:433
  209.1 9.4 %collective-permute-start.23 = (bf16[128,1280]{1,0:T(8,128)(2,1)}, bf16[128,1280]{1,0:T(8,128)(2,1)S(1)}, u32[]{:S(2)}, u32[]{:S(2)}) collective-permute-start(bf16[128,1280]{1,0:T(8,128)(2,1)} %layer_out.8.refs_0_), channel_id=1, source_target_pairs={{48,32},{49,33},{50,34},{51,35},{52,36},{53,37},{54,38},{55,39},{5... | collective-permute-start | bytes 983048 | tf_op jit(solution)/shard_map/ppermute | solution.py:455
  211.8 23.7 %copy-start.18 = (bf16[1280,512]{1,0:T(8,128)(2,1)S(1)}, bf16[1280,512]{1,0:T(8,128)(2,1)}, u32[]{:S(2)}) copy-start(bf16[1280,512]{1,0:T(8,128)(2,1)} %copy-done.17) | copy-start | bytes 3932164
  211.8 9.6 %collective-permute-start.25 = (bf16[128,1280]{1,0:T(8,128)(2,1)}, bf16[128,1280]{1,0:T(8,128)(2,1)S(1)}, u32[]{:S(2)}, u32[]{:S(2)}) collective-permute-start(bf16[128,1280]{1,0:T(8,128)(2,1)} %collective-permute-done.22.refs_1_), channel_id=1, source_target_pairs={{0,16},{1,17},{2,18},{3,19},{4,20},{5,21},{6,22},{7,23},{8,24},{9,... | collective-permute-start | bytes 983048 | tf_op jit(solution)/shard_map/ppermute | solution.py:444
  215.7 5.8 %collective-permute-start.28 = (bf16[128,1280]{1,0:T(8,128)(2,1)S(1)}, bf16[128,1280]{1,0:T(8,128)(2,1)S(1)}, u32[]{:S(2)}, u32[]{:S(2)}) collective-permute-start(bf16[128,1280]{1,0:T(8,128)(2,1)S(1)} %layer_out.9.refs_4_), channel_id=1, source_target_pairs={{48,0},{49,1},{50,2},{51,3},{52,4},{53,5},{54,6},{55,7},{56,8},{57... | collective-permute-start | bytes 983048 | tf_op jit(solution)/shard_map/ppermute | solution.py:455
  216.4 5.1 %collective-permute-start.29 = (bf16[128,1280]{1,0:T(8,128)(2,1)S(1)}, bf16[128,1280]{1,0:T(8,128)(2,1)S(1)}, u32[]{:S(2)}, u32[]{:S(2)}) collective-permute-start(bf16[128,1280]{1,0:T(8,128)(2,1)S(1)} %layer_out.9.refs_4_), channel_id=1, source_target_pairs={{48,32},{49,33},{50,34},{51,35},{52,36},{53,37},{54,38},{55,39},{5... | collective-permute-start | bytes 983048 | tf_op jit(solution)/shard_map/ppermute | solution.py:455
  217.1 18.4 %collective-permute-start.30 = (bf16[128,1280]{1,0:T(8,128)(2,1)S(1)}, bf16[128,1280]{1,0:T(8,128)(2,1)S(1)}, u32[]{:S(2)}, u32[]{:S(2)}) collective-permute-start(bf16[128,1280]{1,0:T(8,128)(2,1)S(1)} %layer_out.9.refs_4_), channel_id=1, source_target_pairs={{48,16},{49,17},{50,18},{51,19},{52,20},{53,21},{54,22},{55,23},{5... | collective-permute-start | bytes 983048 | tf_op jit(solution)/shard_map/ppermute | solution.py:459
  (24 other events, 101.3 us)
Sparse Core Ops, SparseCore 0:
  11.7 88.7 all-gather.6
  102.6 43.3 all-gather.4

commit v5 on v4

--- a/solution.py
+++ b/solution.py
@@ -323,6 +323,16 @@
     order = (slots[None, :, None] * shards + source[:, None, None]) * each + jnp.arange(each)
     order = order.reshape(-1).astype(jnp.int32)
 
+    inputs = pl.pallas_call(
+        order_kernel,
+        out_shape=(shape(frames.shape[1:]),) * MB,
+        in_specs=[VMEM, VMEM],
+        out_specs=(VMEM,) * MB,
+        compiler_params=PARAMS,
+        name="order",
+    )(order.reshape(1, -1), frames)
+
+    ring[-1], *inputs = lax.optimization_barrier((ring[-1], *inputs))
     half = model // 2
     q_near, kv_near, out_near = pl.pallas_call(
         join_kernel,
@@ -353,15 +363,6 @@
         ]
     ).astype(jnp.int32)
     mask = block_mask.reshape(-1)
-    inputs = pl.pallas_call(
-        order_kernel,
-        out_shape=(shape(frames.shape[1:]),) * MB,
-        in_specs=[VMEM, VMEM],
-        out_specs=(VMEM,) * MB,
-        compiler_params=PARAMS,
-        name="order",
-    )(order.reshape(1, -1), frames)
-
     up = [(i, i + 1) for i in range(shards - 1)]
     down = [(i + 1, i) for i in range(shards - 1)]
     onward = [(i, i + 1) for i in range(sections - 1)]

time: 290 us -> 289 us (level)
  waiting for transfers between devices: 51.6 us -> 48.2 us
    ppermute x5, waiting for transfers between devices: 5.84 us -> 1.9 us  [per_device(): right = lax.ppermute(first, 'tm', down)]
  transfers between devices with their start and end apart: 33 -> 33, of which waited for: 12 -> 11; matrix products, arithmetic and copies ran while one was open for 4% -> 4% of each run, Pallas kernels for 12% -> 12%
where the time goes in v5:
time: 289 us; the launch traced here: 287 us
  starting transfers between devices  85.4 us (30%)
  blocking collectives  63.7 us (22%)
  waiting for transfers between devices  48.2 us (17%)
  Pallas kernels  45.6 us (16%)
  local copies, waits for them, and re-layouts  23.7 us (8%)
  between operations  15 us (5%)
  other arithmetic  5.2 us (2%)
    ppermute x8, starting transfers between devices, around(): lax.ppermute(value, axis, [(i, (i + step) % size) for i in range(size)])  28.6 us
    all_to_all x1, blocking collectives, per_device(): lax.all_to_all(jnp.broadcast_to(lanes[None], (groups,) + lanes.shape), 'd...  25.1 us
    all_gather x1, blocking collectives, per_device(): everyone = lax.all_gather(pieces, 'tm', axis=0)  24.3 us
    ppermute x5, starting transfers between devices, per_device(): left = lax.ppermute(last, 'tm', up)  24.1 us
    ppermute x8, waiting for transfers between devices, around(): lax.ppermute(value, axis, [(i, (i + step) % size) for i in range(size)])  19.1 us
    unnamed x78, local copies, waits for them, and re-layouts  14.3 us
    all_to_all x1, blocking collectives, per_device(): grad = lax.all_to_all(grad, 'dp', 0, 0, tiled=True)  14.2 us
    ppermute x1, waiting for transfers between devices, per_device(): sent.append(lax.ppermute(finished, 'section', [(sections - 1, 1)]))  13.9 us
  transfers between devices with their start and end apart: 33, of which 11 were waited for; matrix products, arithmetic and copies ran while one was open for 4% of the time, Pallas kernels for 12%

profile of v5, /device:TPU:2, one launch (start us, length us, event | category | flops | bytes accessed | tf_op | source)
XLA Modules:
  0.0 286.9 jit_solution(16407926730737843697)
XLA Ops:
  11.5 25.1 %all_to_all.10 = bf16[8,200,128]{2,1,0:T(8,128)(2,1)S(1)} all-to-all(bf16[8,200,128]{2,1,0:T(8,128)(2,1)S(1)} %broadcast_in_dim.5), channel_id=1, replica_groups=mesh['dp'=8,'section'=4,'tm'=16] {'dp'}, dimensions={0} | all-to-all | bytes 819200 | tf_op jit(solution)/shard_map/all_to_all | solution.py:303
  37.1 3.5 %collective-permute-start.4 = (bf16[80,2560]{1,0:T(8,128)(2,1)S(1)}, bf16[80,2560]{1,0:T(8,128)(2,1)S(1)}, u32[]{:S(2)}, u32[]{:S(2)}) collective-permute-start(bf16[80,2560]{1,0:T(8,128)(2,1)S(1)} %reshape.103.refs_0_), channel_id=1, source_target_pairs={{0,2},{1,3},{2,4},{3,5},{4,6},{5,7},{6,8},{7,9},{8,10},{9,11},{10,... | collective-permute-start | bytes 1228808 | tf_op jit(solution)/shard_map/ppermute | solution.py:299
  40.6 3.8 %collective-permute-start = (bf16[80,2560]{1,0:T(8,128)(2,1)S(1)}, bf16[80,2560]{1,0:T(8,128)(2,1)S(1)}, u32[]{:S(2)}, u32[]{:S(2)}) collective-permute-start(bf16[80,2560]{1,0:T(8,128)(2,1)S(1)} %reshape.103.refs_0_), channel_id=1, source_target_pairs={{0,14},{1,15},{2,0},{3,1},{4,2},{5,3},{6,4},{7,5},{8,6},{9,7},{10,... | collective-permute-start | bytes 1228808 | tf_op jit(solution)/shard_map/ppermute | solution.py:299
  44.5 6.3 %collective-permute-done.4.refs_1_ = bf16[80,2560]{1,0:T(8,128)(2,1)S(1)} collective-permute-done((bf16[80,2560]{1,0:T(8,128)(2,1)S(1)}, bf16[80,2560]{1,0:T(8,128)(2,1)S(1)}, u32[]{:S(2)}, u32[]{:S(2)}) %collective-permute-start.4) | collective-permute-done | bytes 409632 | tf_op jit(solution)/shard_map/ppermute | solution.py:299
  50.7 1.9 collective-permute-start.5
  52.7 5.1 %collective-permute-start.1 = (bf16[80,2560]{1,0:T(8,128)(2,1)S(1)}, bf16[80,2560]{1,0:T(8,128)(2,1)}, u32[]{:S(2)}, u32[]{:S(2)}) collective-permute-start(bf16[80,2560]{1,0:T(8,128)(2,1)S(1)} %collective-permute-done.refs_4_), channel_id=1, source_target_pairs={{0,14},{1,15},{2,0},{3,1},{4,2},{5,3},{6,4},{7,5},{8,6},{9,7},{10,... | collective-permute-start | bytes 1228808 | tf_op jit(solution)/shard_map/ppermute | solution.py:299
  57.8 5.2 %collective-permute-done.5.refs_2_ = bf16[80,2560]{1,0:T(8,128)(2,1)S(1)} collective-permute-done((bf16[80,2560]{1,0:T(8,128)(2,1)S(1)}, bf16[80,2560]{1,0:T(8,128)(2,1)S(1)}, u32[]{:S(2)}, u32[]{:S(2)}) %collective-permute-start.5) | collective-permute-done | bytes 409632 | tf_op jit(solution)/shard_map/ppermute | solution.py:299
  63.0 1.9 collective-permute-start.6
  64.9 5.1 %collective-permute-start.2 = (bf16[80,2560]{1,0:T(8,128)(2,1)}, bf16[80,2560]{1,0:T(8,128)(2,1)S(1)}, u32[]{:S(2)}, u32[]{:S(2)}) collective-permute-start(bf16[80,2560]{1,0:T(8,128)(2,1)} %collective-permute-done.1.refs_5_), channel_id=1, source_target_pairs={{0,14},{1,15},{2,0},{3,1},{4,2},{5,3},{6,4},{7,5},{8,6},{9,7},{10,... | collective-permute-start | bytes 1228808 | tf_op jit(solution)/shard_map/ppermute | solution.py:299
  70.2 5.1 %collective-permute-done.6.refs_3_ = bf16[80,2560]{1,0:T(8,128)(2,1)S(1)} collective-permute-done((bf16[80,2560]{1,0:T(8,128)(2,1)S(1)}, bf16[80,2560]{1,0:T(8,128)(2,1)S(1)}, u32[]{:S(2)}, u32[]{:S(2)}) %collective-permute-start.6) | collective-permute-done | bytes 409632 | tf_op jit(solution)/shard_map/ppermute | solution.py:299
  76.1 1.9 collective-permute-start.7
  78.8 5.3 %collective-permute-start.3 = (bf16[32,2560]{1,0:T(8,128)(2,1)}, bf16[32,2560]{1,0:T(8,128)(2,1)}, u32[]{:S(2)}, u32[]{:S(2)}) collective-permute-start(bf16[32,2560]{1,0:T(8,128)(2,1)} %slice.12), channel_id=1, source_target_pairs={{0,14},{1,15},{2,0},{3,1},{4,2},{5,3},{6,4},{7,5},{8,6},{9,7},{10,... | collective-permute-start | bytes 491528 | tf_op jit(solution)/shard_map/ppermute | solution.py:299
  85.5 2.6 collective-permute-done.3.refs_8_
  88.8 4.0 %join.1 = (bf16[640,640]{1,0:T(8,128)(2,1)}, bf16[640,1280]{1,0:T(8,128)(2,1)}, bf16[640,640]{1,0:T(8,128)(2,1)}) custom-call(bf16[80,2560]{1,0:T(8,128)(2,1)} %copy-done.28, bf16[80,2560]{1,0:T(8,128)(2,1)} %copy-done.31, bf16[80,2560]{1,0:T(8,128)(2,1)} %copy-done.33, bf16[80,2560]{1,0:T(8,128)(2,1)} %copy-done.29, bf16[80,2560]{1,0:T(8,128)(2,1)} %copy-done.32, ...), custom_call_target="tpu_custom_call" | custom-call | tf_op jit(solution)/shard_map/join/pallas_call | solution.py:337
  92.8 1.9 collective-permute-start.8
  94.7 2.4 collective-permute-start.9
  97.1 1.9 collective-permute-start.12
  102.9 2.5 collective-permute-start.10
  109.0 2.2 own_blocks.5
  111.3 2.9 %layer_out.5 = bf16[128,1280]{1,0:T(8,128)(2,1)} custom-call(s32[6]{0:T(128)S(1)} %stack.60.place_ref, s32[8]{0:T(128)S(1)} %reshape.102.mask_ref, bf16[128,640]{1,0:T(8,128)(2,1)S(1)} %get-tuple-element.62.q_ref, f32[128,640]{1,0:T(8,128)S(1)} %get-tuple-element.63.num_ref, f32[128,640]{1,0:T(8,128)S(1)} %get-tuple-element.64.den_ref, ...), custom_call_target="tpu_custom_call" | custom-call | tf_op jit(solution)/shard_map/layer_out/pallas_call | solution.py:446
  114.3 3.3 %collective-permute-start.13 = (bf16[128,1280]{1,0:T(8,128)(2,1)}, bf16[128,1280]{1,0:T(8,128)(2,1)}, u32[]{:S(2)}, u32[]{:S(2)}) collective-permute-start(bf16[128,1280]{1,0:T(8,128)(2,1)} %layer_out.5), channel_id=1, source_target_pairs={{0,16},{16,32},{32,48},{1,17},{17,33},{33,49},{2,18},{18,34},{34,5... | collective-permute-start | bytes 983048 | tf_op jit(solution)/shard_map/ppermute | solution.py:463
  117.7 5.0 %reshape.107.w_ref = bf16[1280,768]{1,0:T(8,128)(2,1)} reshape(bf16[128,10,768]{2,1,0:T(8,128)(2,1)} %all-gather.7.cloned.1.call-done) | data formatting | bytes 3932160 | tf_op jit(solution)/shard_map/optimization_barrier | solution.py:375
  122.7 4.2 %collective-permute-done.13 = bf16[128,1280]{1,0:T(8,128)(2,1)} collective-permute-done((bf16[128,1280]{1,0:T(8,128)(2,1)}, bf16[128,1280]{1,0:T(8,128)(2,1)}, u32[]{:S(2)}, u32[]{:S(2)}) %collective-permute-start.13) | collective-permute-done | bytes 327712 | tf_op jit(solution)/shard_map/ppermute | solution.py:463
  128.9 2.3 collective-permute-start.14
  132.5 2.0 own_blocks.6
  135.3 2.4 layer_out.6
  137.7 3.2 %collective-permute-start.16 = (bf16[128,1280]{1,0:T(8,128)(2,1)}, bf16[128,1280]{1,0:T(8,128)(2,1)}, u32[]{:S(2)}, u32[]{:S(2)}) collective-permute-start(bf16[128,1280]{1,0:T(8,128)(2,1)} %layer_out.6), channel_id=1, source_target_pairs={{0,16},{16,32},{32,48},{1,17},{17,33},{33,49},{2,18},{18,34},{34,5... | collective-permute-start | bytes 983048 | tf_op jit(solution)/shard_map/ppermute | solution.py:463
  147.6 2.0 keys_values.7
  149.6 9.0 %collective-permute-start.17 = (bf16[64,1280]{1,0:T(8,128)(2,1)S(1)}, bf16[64,1280]{1,0:T(8,128)(2,1)S(1)}, u32[]{:S(2)}, u32[]{:S(2)}) collective-permute-start(bf16[64,1280]{1,0:T(8,128)(2,1)S(1)} %get-tuple-element.77.last_ref), channel_id=1, source_target_pairs={{0,1},{1,2},{2,3},{3,4},{4,5},{5,6},{6,7},{7,8},{8,9},{9,10},{10,1... | collective-permute-start | bytes 491528 | tf_op jit(solution)/shard_map/ppermute | solution.py:433
  160.1 2.0 own_blocks.7
  162.6 2.8 layer_out.7
  165.3 3.4 %collective-permute-start.19 = (bf16[128,1280]{1,0:T(8,128)(2,1)}, bf16[128,1280]{1,0:T(8,128)(2,1)}, u32[]{:S(2)}, u32[]{:S(2)}) collective-permute-start(bf16[128,1280]{1,0:T(8,128)(2,1)} %layer_out.7), channel_id=1, source_target_pairs={{0,16},{16,32},{32,48},{1,17},{17,33},{33,49},{2,18},{18,34},{34,5... | collective-permute-start | bytes 983048 | tf_op jit(solution)/shard_map/ppermute | solution.py:463
  168.9 2.5 copy-done.2
  172.9 2.2 queries.1.q_ref
  175.8 2.0 keys_values.8
  177.9 5.6 %collective-permute-start.20 = (bf16[64,1280]{1,0:T(8,128)(2,1)S(1)}, bf16[64,1280]{1,0:T(8,128)(2,1)S(1)}, u32[]{:S(2)}, u32[]{:S(2)}) collective-permute-start(bf16[64,1280]{1,0:T(8,128)(2,1)S(1)} %get-tuple-element.86.last_ref), channel_id=1, source_target_pairs={{0,1},{1,2},{2,3},{3,4},{4,5},{5,6},{6,7},{7,8},{8,9},{9,10},{10,1... | collective-permute-start | bytes 491528 | tf_op jit(solution)/shard_map/ppermute | solution.py:433
  184.8 2.0 own_blocks.8
  187.5 2.8 layer_out.8.refs_0_
  190.3 3.7 %collective-permute-start.24 = (bf16[128,1280]{1,0:T(8,128)(2,1)}, bf16[128,1280]{1,0:T(8,128)(2,1)S(1)}, u32[]{:S(2)}, u32[]{:S(2)}) collective-permute-start(bf16[128,1280]{1,0:T(8,128)(2,1)} %layer_out.8.refs_0_), channel_id=1, source_target_pairs={{0,16},{16,32},{32,48},{1,17},{17,33},{33,49},{2,18},{18,34},{34,5... | collective-permute-start | bytes 983048 | tf_op jit(solution)/shard_map/ppermute | solution.py:463
  196.8 3.3 %collective-permute-done.24.x_ref = bf16[128,1280]{1,0:T(8,128)(2,1)S(1)} collective-permute-done((bf16[128,1280]{1,0:T(8,128)(2,1)}, bf16[128,1280]{1,0:T(8,128)(2,1)S(1)}, u32[]{:S(2)}, u32[]{:S(2)}) %collective-permute-start.24) | collective-permute-done | bytes 327712 | tf_op jit(solution)/shard_map/ppermute | solution.py:463
  201.0 4.6 %collective-permute-start.26 = (bf16[64,1280]{1,0:T(8,128)(2,1)S(1)}, bf16[64,1280]{1,0:T(8,128)(2,1)S(1)}, u32[]{:S(2)}, u32[]{:S(2)}) collective-permute-start(bf16[64,1280]{1,0:T(8,128)(2,1)S(1)} %get-tuple-element.93.last_ref), channel_id=1, source_target_pairs={{0,1},{1,2},{2,3},{3,4},{4,5},{5,6},{6,7},{7,8},{8,9},{9,10},{10,1... | collective-permute-start | bytes 491528 | tf_op jit(solution)/shard_map/ppermute | solution.py:433
  207.6 2.0 own_blocks.9
  215.5 5.7 %collective-permute-done.25.refs_3_ = bf16[128,1280]{1,0:T(8,128)(2,1)S(1)} collective-permute-done((bf16[128,1280]{1,0:T(8,128)(2,1)}, bf16[128,1280]{1,0:T(8,128)(2,1)S(1)}, u32[]{:S(2)}, u32[]{:S(2)}) %collective-permute-start.25) | collective-permute-done | bytes 327712 | tf_op jit(solution)/shard_map/ppermute | solution.py:445
  221.2 13.9 %collective-permute-done.30.refs_7_ = bf16[128,1280]{1,0:T(8,128)(2,1)S(1)} collective-permute-done((bf16[128,1280]{1,0:T(8,128)(2,1)S(1)}, bf16[128,1280]{1,0:T(8,128)(2,1)S(1)}, u32[]{:S(2)}, u32[]{:S(2)}) %collective-permute-start.30) | collective-permute-done | bytes 327712 | tf_op jit(solution)/shard_map/ppermute | solution.py:460
  235.9 2.3 cross.1
  238.3 24.3 %all-gather = bf16[3584,128]{1,0:T(8,128)(2,1)S(1)} all-gather(bf16[224,128]{1,0:T(8,128)(2,1)S(1)} %cross.1), channel_id=2, replica_groups=mesh['dp'=8,'section'=4,'tm'=16] {'tm'}, dimensions={0}, use_global_device_ids=true | all-gather | bytes 974848 | tf_op jit(solution)/shard_map/all_gather | solution.py:473
  262.5 2.7 combine.1
  265.2 14.2 %all_to_all.11 = bf16[8,16,256]{2,1,0:T(8,128)(2,1)S(1)} all-to-all(bf16[8,16,256]{2,1,0:T(8,128)(2,1)S(1)} %get-tuple-element.101), channel_id=1, replica_groups=mesh['dp'=8,'section'=4,'tm'=16] {'dp'}, dimensions={0} | all-to-all | bytes 131072 | tf_op jit(solution)/shard_map/all_to_all | solution.py:487
  (147 shorter events, 45.7 us)
Async XLA Ops:
  7.2 110.5 %all-gather.7.cloned.1.call-start = ((), (), s32[]{:S(2)}) async-start(), calls=%async_computation.3 | async-start | bytes 3170304 | tf_op jit(solution)/shard_map/all_gather | solution.py:350
  8.6 160.3 %all-gather.5.cloned.1.call-start = ((), (), s32[]{:S(2)}) async-start(), calls=%async_computation.2 | async-start | bytes 5570560 | tf_op jit(solution)/shard_map/all_gather | solution.py:351
  10.4 74.0 %copy-start.22 = (bf16[2,128,1280]{2,1,0:T(8,128)(2,1)S(1)}, bf16[2,128,1280]{2,1,0:T(8,128)(2,1)}, u32[]{:S(2)}) copy-start(bf16[2,128,1280]{2,1,0:T(8,128)(2,1)} %frames_ref.1) | copy-start | bytes 1966084
  37.1 50.9 %copy-start.28 = (bf16[80,2560]{1,0:T(8,128)(2,1)}, bf16[80,2560]{1,0:T(8,128)(2,1)S(1)}, u32[]{:S(2)}) copy-start(bf16[80,2560]{1,0:T(8,128)(2,1)S(1)} %reshape.103.refs_0_) | copy-start | bytes 1228804
  37.1 13.6 %collective-permute-start.4 = (bf16[80,2560]{1,0:T(8,128)(2,1)S(1)}, bf16[80,2560]{1,0:T(8,128)(2,1)S(1)}, u32[]{:S(2)}, u32[]{:S(2)}) collective-permute-start(bf16[80,2560]{1,0:T(8,128)(2,1)S(1)} %reshape.103.refs_0_), channel_id=1, source_target_pairs={{0,2},{1,3},{2,4},{3,5},{4,6},{5,7},{6,8},{7,9},{8,10},{9,11},{10,... | collective-permute-start | bytes 1228808 | tf_op jit(solution)/shard_map/ppermute | solution.py:299
  40.6 12.0 %collective-permute-start = (bf16[80,2560]{1,0:T(8,128)(2,1)S(1)}, bf16[80,2560]{1,0:T(8,128)(2,1)S(1)}, u32[]{:S(2)}, u32[]{:S(2)}) collective-permute-start(bf16[80,2560]{1,0:T(8,128)(2,1)S(1)} %reshape.103.refs_0_), channel_id=1, source_target_pairs={{0,14},{1,15},{2,0},{3,1},{4,2},{5,3},{6,4},{7,5},{8,6},{9,7},{10,... | collective-permute-start | bytes 1228808 | tf_op jit(solution)/shard_map/ppermute | solution.py:299
  50.7 37.3 %copy-start.31 = (bf16[80,2560]{1,0:T(8,128)(2,1)}, bf16[80,2560]{1,0:T(8,128)(2,1)S(1)}, u32[]{:S(2)}) copy-start(bf16[80,2560]{1,0:T(8,128)(2,1)S(1)} %collective-permute-done.4.refs_1_) | copy-start | bytes 1228804
  50.7 12.2 %collective-permute-start.5 = (bf16[80,2560]{1,0:T(8,128)(2,1)S(1)}, bf16[80,2560]{1,0:T(8,128)(2,1)S(1)}, u32[]{:S(2)}, u32[]{:S(2)}) collective-permute-start(bf16[80,2560]{1,0:T(8,128)(2,1)S(1)} %collective-permute-done.4.refs_1_), channel_id=1, source_target_pairs={{0,2},{1,3},{2,4},{3,5},{4,6},{5,7},{6,8},{7,9},{8,10},{9,11},{10,... | collective-permute-start | bytes 1228808 | tf_op jit(solution)/shard_map/ppermute | solution.py:299
  52.6 12.2 %copy-start.32 = (bf16[80,2560]{1,0:T(8,128)(2,1)}, bf16[80,2560]{1,0:T(8,128)(2,1)S(1)}, u32[]{:S(2)}) copy-start(bf16[80,2560]{1,0:T(8,128)(2,1)S(1)} %collective-permute-done.refs_4_) | copy-start | bytes 1228804
  52.7 12.2 %collective-permute-start.1 = (bf16[80,2560]{1,0:T(8,128)(2,1)S(1)}, bf16[80,2560]{1,0:T(8,128)(2,1)}, u32[]{:S(2)}, u32[]{:S(2)}) collective-permute-start(bf16[80,2560]{1,0:T(8,128)(2,1)S(1)} %collective-permute-done.refs_4_), channel_id=1, source_target_pairs={{0,14},{1,15},{2,0},{3,1},{4,2},{5,3},{6,4},{7,5},{8,6},{9,7},{10,... | collective-permute-start | bytes 1228808 | tf_op jit(solution)/shard_map/ppermute | solution.py:299
  63.0 21.3 %copy-start.33 = (bf16[80,2560]{1,0:T(8,128)(2,1)}, bf16[80,2560]{1,0:T(8,128)(2,1)S(1)}, u32[]{:S(2)}) copy-start(bf16[80,2560]{1,0:T(8,128)(2,1)S(1)} %collective-permute-done.5.refs_2_) | copy-start | bytes 1228804
  63.0 12.4 %collective-permute-start.6 = (bf16[80,2560]{1,0:T(8,128)(2,1)S(1)}, bf16[80,2560]{1,0:T(8,128)(2,1)S(1)}, u32[]{:S(2)}, u32[]{:S(2)}) collective-permute-start(bf16[80,2560]{1,0:T(8,128)(2,1)S(1)} %collective-permute-done.5.refs_2_), channel_id=1, source_target_pairs={{0,2},{1,3},{2,4},{3,5},{4,6},{5,7},{6,8},{7,9},{8,10},{9,11},{10,... | collective-permute-start | bytes 1228808 | tf_op jit(solution)/shard_map/ppermute | solution.py:299
  64.9 13.2 %collective-permute-start.2 = (bf16[80,2560]{1,0:T(8,128)(2,1)}, bf16[80,2560]{1,0:T(8,128)(2,1)S(1)}, u32[]{:S(2)}, u32[]{:S(2)}) collective-permute-start(bf16[80,2560]{1,0:T(8,128)(2,1)} %collective-permute-done.1.refs_5_), channel_id=1, source_target_pairs={{0,14},{1,15},{2,0},{3,1},{4,2},{5,3},{6,4},{7,5},{8,6},{9,7},{10,... | collective-permute-start | bytes 1228808 | tf_op jit(solution)/shard_map/ppermute | solution.py:299
  75.3 12.7 %copy-start.29 = (bf16[80,2560]{1,0:T(8,128)(2,1)}, bf16[80,2560]{1,0:T(8,128)(2,1)S(1)}, u32[]{:S(2)}) copy-start(bf16[80,2560]{1,0:T(8,128)(2,1)S(1)} %collective-permute-done.6.refs_3_) | copy-start | bytes 1228804
  76.1 11.9 %collective-permute-start.7 = (bf16[48,2560]{1,0:T(8,128)(2,1)}, bf16[48,2560]{1,0:T(8,128)(2,1)S(1)}, u32[]{:S(2)}, u32[]{:S(2)}) collective-permute-start(bf16[48,2560]{1,0:T(8,128)(2,1)} %slice.13), channel_id=1, source_target_pairs={{0,2},{1,3},{2,4},{3,5},{4,6},{5,7},{6,8},{7,9},{8,10},{9,11},{10,... | collective-permute-start | bytes 737288 | tf_op jit(solution)/shard_map/ppermute | solution.py:299
  78.8 9.2 %collective-permute-start.3 = (bf16[32,2560]{1,0:T(8,128)(2,1)}, bf16[32,2560]{1,0:T(8,128)(2,1)}, u32[]{:S(2)}, u32[]{:S(2)}) collective-permute-start(bf16[32,2560]{1,0:T(8,128)(2,1)} %slice.12), channel_id=1, source_target_pairs={{0,14},{1,15},{2,0},{3,1},{4,2},{5,3},{6,4},{7,5},{8,6},{9,7},{10,... | collective-permute-start | bytes 491528 | tf_op jit(solution)/shard_map/ppermute | solution.py:299
  85.4 13.6 %copy-start.20 = (bf16[128,1280]{1,0:T(8,128)(2,1)}, bf16[128,1280]{1,0:T(8,128)(2,1)S(1)}, u32[]{:S(2)}) copy-start(bf16[128,1280]{1,0:T(8,128)(2,1)S(1)} %get-tuple-element.55.x_ref) | copy-start | bytes 983044
  92.8 13.9 %copy-start.35 = (s32[2,2,2]{2,1,0:T(2,128)S(1)}, s32[2,2,2]{2,1,0:T(2,128)}, u32[]{:S(2)}) copy-start(s32[2,2,2]{2,1,0:T(2,128)} %param.11) | copy-start | bytes 100
  92.8 6.3 %collective-permute-start.8 = (bf16[640,1280]{1,0:T(8,128)(2,1)}, bf16[640,1280]{1,0:T(8,128)(2,1)S(1)}, u32[]{:S(2)}, u32[]{:S(2)}) collective-permute-start(bf16[640,1280]{1,0:T(8,128)(2,1)} %get-tuple-element.57.near_ref), channel_id=1, source_target_pairs={{0,1},{1,0},{2,3},{3,2},{4,5},{5,4},{6,7},{7,6},{8,9},{9,8},{10,11... | collective-permute-start | bytes 4915208 | tf_op jit(solution)/shard_map/ppermute | solution.py:347
  94.7 12.2 %collective-permute-start.9 = (bf16[640,640]{1,0:T(8,128)(2,1)}, bf16[640,640]{1,0:T(8,128)(2,1)}, u32[]{:S(2)}, u32[]{:S(2)}) collective-permute-start(bf16[640,640]{1,0:T(8,128)(2,1)} %get-tuple-element.61.near_ref), channel_id=1, source_target_pairs={{0,1},{1,0},{2,3},{3,2},{4,5},{5,4},{6,7},{7,6},{8,9},{9,8},{10,11... | collective-permute-start | bytes 2457608 | tf_op jit(solution)/shard_map/ppermute | solution.py:347
  97.1 14.1 %collective-permute-start.12 = (bf16[640,640]{1,0:T(8,128)(2,1)}, bf16[640,640]{1,0:T(8,128)(2,1)S(1)}, u32[]{:S(2)}, u32[]{:S(2)}) collective-permute-start(bf16[640,640]{1,0:T(8,128)(2,1)} %get-tuple-element.65.near_ref), channel_id=1, source_target_pairs={{0,1},{1,0},{2,3},{3,2},{4,5},{5,4},{6,7},{7,6},{8,9},{9,8},{10,11... | collective-permute-start | bytes 2457608 | tf_op jit(solution)/shard_map/ppermute | solution.py:347
  102.9 8.4 %collective-permute-start.10 = (bf16[64,1280]{1,0:T(8,128)(2,1)}, bf16[64,1280]{1,0:T(8,128)(2,1)S(1)}, u32[]{:S(2)}, u32[]{:S(2)}) collective-permute-start(bf16[64,1280]{1,0:T(8,128)(2,1)} %get-tuple-element.60.last_ref), channel_id=1, source_target_pairs={{0,1},{1,2},{2,3},{3,4},{4,5},{5,6},{6,7},{7,8},{8,9},{9,10},{10,1... | collective-permute-start | bytes 491528 | tf_op jit(solution)/shard_map/ppermute | solution.py:433
  105.4 5.9 %collective-permute-start.11 = (bf16[64,1280]{1,0:T(8,128)(2,1)}, bf16[64,1280]{1,0:T(8,128)(2,1)}, u32[]{:S(2)}, u32[]{:S(2)}) collective-permute-start(bf16[64,1280]{1,0:T(8,128)(2,1)} %get-tuple-element.59.first_ref), channel_id=1, source_target_pairs={{1,0},{2,1},{3,2},{4,3},{5,4},{6,5},{7,6},{8,7},{9,8},{10,9},{11,1... | collective-permute-start | bytes 491528 | tf_op jit(solution)/shard_map/ppermute | solution.py:434
  114.3 12.6 %collective-permute-start.13 = (bf16[128,1280]{1,0:T(8,128)(2,1)}, bf16[128,1280]{1,0:T(8,128)(2,1)}, u32[]{:S(2)}, u32[]{:S(2)}) collective-permute-start(bf16[128,1280]{1,0:T(8,128)(2,1)} %layer_out.5), channel_id=1, source_target_pairs={{0,16},{16,32},{32,48},{1,17},{17,33},{33,49},{2,18},{18,34},{34,5... | collective-permute-start | bytes 983048 | tf_op jit(solution)/shard_map/ppermute | solution.py:463
  128.9 5.7 %collective-permute-start.14 = (bf16[64,1280]{1,0:T(8,128)(2,1)S(1)}, bf16[64,1280]{1,0:T(8,128)(2,1)S(1)}, u32[]{:S(2)}, u32[]{:S(2)}) collective-permute-start(bf16[64,1280]{1,0:T(8,128)(2,1)S(1)} %get-tuple-element.69.last_ref), channel_id=1, source_target_pairs={{0,1},{1,2},{2,3},{3,4},{4,5},{5,6},{6,7},{7,8},{8,9},{9,10},{10,1... | collective-permute-start | bytes 491528 | tf_op jit(solution)/shard_map/ppermute | solution.py:433
  131.2 4.1 %collective-permute-start.15 = (bf16[64,1280]{1,0:T(8,128)(2,1)S(1)}, bf16[64,1280]{1,0:T(8,128)(2,1)S(1)}, u32[]{:S(2)}, u32[]{:S(2)}) collective-permute-start(bf16[64,1280]{1,0:T(8,128)(2,1)S(1)} %get-tuple-element.68.first_ref), channel_id=1, source_target_pairs={{1,0},{2,1},{3,2},{4,3},{5,4},{6,5},{7,6},{8,7},{9,8},{10,9},{11,1... | collective-permute-start | bytes 491528 | tf_op jit(solution)/shard_map/ppermute | solution.py:434
  137.7 9.9 %collective-permute-start.16 = (bf16[128,1280]{1,0:T(8,128)(2,1)}, bf16[128,1280]{1,0:T(8,128)(2,1)}, u32[]{:S(2)}, u32[]{:S(2)}) collective-permute-start(bf16[128,1280]{1,0:T(8,128)(2,1)} %layer_out.6), channel_id=1, source_target_pairs={{0,16},{16,32},{32,48},{1,17},{17,33},{33,49},{2,18},{18,34},{34,5... | collective-permute-start | bytes 983048 | tf_op jit(solution)/shard_map/ppermute | solution.py:463
  147.6 12.5 %copy-start.13 = (bf16[640,640]{1,0:T(8,128)(2,1)S(1)}, bf16[640,640]{1,0:T(8,128)(2,1)}, u32[]{:S(2)}) copy-start(bf16[640,640]{1,0:T(8,128)(2,1)} %get-tuple-element.61.near_ref) | copy-start | bytes 2457604
  149.5 13.0 %copy-start.5 = (bf16[640,640]{1,0:T(8,128)(2,1)S(1)}, bf16[640,640]{1,0:T(8,128)(2,1)}, u32[]{:S(2)}) copy-start(bf16[640,640]{1,0:T(8,128)(2,1)} %get-tuple-element.65.near_ref) | copy-start | bytes 2457604
  149.6 13.0 %copy-start.9 = (bf16[640,640]{1,0:T(8,128)(2,1)S(1)}, bf16[640,640]{1,0:T(8,128)(2,1)}, u32[]{:S(2)}) copy-start(bf16[640,640]{1,0:T(8,128)(2,1)} %copy-done.7) | copy-start | bytes 2457604
  149.6 12.6 %collective-permute-start.17 = (bf16[64,1280]{1,0:T(8,128)(2,1)S(1)}, bf16[64,1280]{1,0:T(8,128)(2,1)S(1)}, u32[]{:S(2)}, u32[]{:S(2)}) collective-permute-start(bf16[64,1280]{1,0:T(8,128)(2,1)S(1)} %get-tuple-element.77.last_ref), channel_id=1, source_target_pairs={{0,1},{1,2},{2,3},{3,4},{4,5},{5,6},{6,7},{7,8},{8,9},{9,10},{10,1... | collective-permute-start | bytes 491528 | tf_op jit(solution)/shard_map/ppermute | solution.py:433
  158.6 4.0 %collective-permute-start.18 = (bf16[64,1280]{1,0:T(8,128)(2,1)S(1)}, bf16[64,1280]{1,0:T(8,128)(2,1)S(1)}, u32[]{:S(2)}, u32[]{:S(2)}) collective-permute-start(bf16[64,1280]{1,0:T(8,128)(2,1)S(1)} %get-tuple-element.76.first_ref), channel_id=1, source_target_pairs={{1,0},{2,1},{3,2},{4,3},{5,4},{6,5},{7,6},{8,7},{9,8},{10,9},{11,1... | collective-permute-start | bytes 491528 | tf_op jit(solution)/shard_map/ppermute | solution.py:434
  165.3 10.5 %collective-permute-start.19 = (bf16[128,1280]{1,0:T(8,128)(2,1)}, bf16[128,1280]{1,0:T(8,128)(2,1)}, u32[]{:S(2)}, u32[]{:S(2)}) collective-permute-start(bf16[128,1280]{1,0:T(8,128)(2,1)} %layer_out.7), channel_id=1, source_target_pairs={{0,16},{16,32},{32,48},{1,17},{17,33},{33,49},{2,18},{18,34},{34,5... | collective-permute-start | bytes 983048 | tf_op jit(solution)/shard_map/ppermute | solution.py:463
  172.9 11.9 %copy-start.14 = (bf16[640,640]{1,0:T(8,128)(2,1)S(1)}, bf16[640,640]{1,0:T(8,128)(2,1)}, u32[]{:S(2)}) copy-start(bf16[640,640]{1,0:T(8,128)(2,1)} %get-tuple-element.61.near_ref) | copy-start | bytes 2457604
  172.9 22.4 %slice-start = ((s8[5242880]{0:T(1024)(128)(4,1)}), s8[1048576]{0:T(1024)(128)(4,1)S(1)}, s32[]{:S(2)}) async-start(s8[5242880]{0:T(1024)(128)(4,1)} %bitcast.26), calls=%async_computation.4 | async-start | bytes 2097152
  175.8 19.6 %slice-start.1 = ((s8[5242880]{0:T(1024)(128)(4,1)}), s8[4194304]{0:T(1024)(128)(4,1)S(1)}, s32[]{:S(2)}) async-start(s8[5242880]{0:T(1024)(128)(4,1)} %bitcast.26), calls=%async_computation.5 | async-start | bytes 8388608
  177.9 8.9 %collective-permute-start.20 = (bf16[64,1280]{1,0:T(8,128)(2,1)S(1)}, bf16[64,1280]{1,0:T(8,128)(2,1)S(1)}, u32[]{:S(2)}, u32[]{:S(2)}) collective-permute-start(bf16[64,1280]{1,0:T(8,128)(2,1)S(1)} %get-tuple-element.86.last_ref), channel_id=1, source_target_pairs={{0,1},{1,2},{2,3},{3,4},{4,5},{5,6},{6,7},{7,8},{8,9},{9,10},{10,1... | collective-permute-start | bytes 491528 | tf_op jit(solution)/shard_map/ppermute | solution.py:433
  183.5 4.0 %collective-permute-start.21 = (bf16[64,1280]{1,0:T(8,128)(2,1)S(1)}, bf16[64,1280]{1,0:T(8,128)(2,1)S(1)}, u32[]{:S(2)}, u32[]{:S(2)}) collective-permute-start(bf16[64,1280]{1,0:T(8,128)(2,1)S(1)} %get-tuple-element.85.first_ref), channel_id=1, source_target_pairs={{1,0},{2,1},{3,2},{4,3},{5,4},{6,5},{7,6},{8,7},{9,8},{10,9},{11,1... | collective-permute-start | bytes 491528 | tf_op jit(solution)/shard_map/ppermute | solution.py:434
  190.3 9.8 %collective-permute-start.24 = (bf16[128,1280]{1,0:T(8,128)(2,1)}, bf16[128,1280]{1,0:T(8,128)(2,1)S(1)}, u32[]{:S(2)}, u32[]{:S(2)}) collective-permute-start(bf16[128,1280]{1,0:T(8,128)(2,1)} %layer_out.8.refs_0_), channel_id=1, source_target_pairs={{0,16},{16,32},{32,48},{1,17},{17,33},{33,49},{2,18},{18,34},{34,5... | collective-permute-start | bytes 983048 | tf_op jit(solution)/shard_map/ppermute | solution.py:463
  194.0 15.6 %collective-permute-start.22 = (bf16[128,1280]{1,0:T(8,128)(2,1)}, bf16[128,1280]{1,0:T(8,128)(2,1)}, u32[]{:S(2)}, u32[]{:S(2)}) collective-permute-start(bf16[128,1280]{1,0:T(8,128)(2,1)} %layer_out.8.refs_0_), channel_id=1, source_target_pairs={{48,0},{49,1},{50,2},{51,3},{52,4},{53,5},{54,6},{55,7},{56,8},{57... | collective-permute-start | bytes 983048 | tf_op jit(solution)/shard_map/ppermute | solution.py:456
  201.0 10.1 %collective-permute-start.26 = (bf16[64,1280]{1,0:T(8,128)(2,1)S(1)}, bf16[64,1280]{1,0:T(8,128)(2,1)S(1)}, u32[]{:S(2)}, u32[]{:S(2)}) collective-permute-start(bf16[64,1280]{1,0:T(8,128)(2,1)S(1)} %get-tuple-element.93.last_ref), channel_id=1, source_target_pairs={{0,1},{1,2},{2,3},{3,4},{4,5},{5,6},{6,7},{7,8},{8,9},{9,10},{10,1... | collective-permute-start | bytes 491528 | tf_op jit(solution)/shard_map/ppermute | solution.py:433
  205.6 5.5 %collective-permute-start.27 = (bf16[64,1280]{1,0:T(8,128)(2,1)S(1)}, bf16[64,1280]{1,0:T(8,128)(2,1)S(1)}, u32[]{:S(2)}, u32[]{:S(2)}) collective-permute-start(bf16[64,1280]{1,0:T(8,128)(2,1)S(1)} %get-tuple-element.92.first_ref), channel_id=1, source_target_pairs={{1,0},{2,1},{3,2},{4,3},{5,4},{6,5},{7,6},{8,7},{9,8},{10,9},{11,1... | collective-permute-start | bytes 491528 | tf_op jit(solution)/shard_map/ppermute | solution.py:434
  206.9 8.6 %collective-permute-start.23 = (bf16[128,1280]{1,0:T(8,128)(2,1)}, bf16[128,1280]{1,0:T(8,128)(2,1)S(1)}, u32[]{:S(2)}, u32[]{:S(2)}) collective-permute-start(bf16[128,1280]{1,0:T(8,128)(2,1)} %layer_out.8.refs_0_), channel_id=1, source_target_pairs={{48,32},{49,33},{50,34},{51,35},{52,36},{53,37},{54,38},{55,39},{5... | collective-permute-start | bytes 983048 | tf_op jit(solution)/shard_map/ppermute | solution.py:456
  209.6 25.5 %copy-start.18 = (bf16[1280,512]{1,0:T(8,128)(2,1)S(1)}, bf16[1280,512]{1,0:T(8,128)(2,1)}, u32[]{:S(2)}) copy-start(bf16[1280,512]{1,0:T(8,128)(2,1)} %copy-done.17) | copy-start | bytes 3932164
  209.6 11.5 %collective-permute-start.25 = (bf16[128,1280]{1,0:T(8,128)(2,1)}, bf16[128,1280]{1,0:T(8,128)(2,1)S(1)}, u32[]{:S(2)}, u32[]{:S(2)}) collective-permute-start(bf16[128,1280]{1,0:T(8,128)(2,1)} %collective-permute-done.22.refs_1_), channel_id=1, source_target_pairs={{0,16},{1,17},{2,18},{3,19},{4,20},{5,21},{6,22},{7,23},{8,24},{9,... | collective-permute-start | bytes 983048 | tf_op jit(solution)/shard_map/ppermute | solution.py:445
  212.7 8.4 %collective-permute-start.28 = (bf16[128,1280]{1,0:T(8,128)(2,1)S(1)}, bf16[128,1280]{1,0:T(8,128)(2,1)S(1)}, u32[]{:S(2)}, u32[]{:S(2)}) collective-permute-start(bf16[128,1280]{1,0:T(8,128)(2,1)S(1)} %layer_out.9.refs_4_), channel_id=1, source_target_pairs={{48,0},{49,1},{50,2},{51,3},{52,4},{53,5},{54,6},{55,7},{56,8},{57... | collective-permute-start | bytes 983048 | tf_op jit(solution)/shard_map/ppermute | solution.py:456
  213.4 7.8 %collective-permute-start.29 = (bf16[128,1280]{1,0:T(8,128)(2,1)S(1)}, bf16[128,1280]{1,0:T(8,128)(2,1)S(1)}, u32[]{:S(2)}, u32[]{:S(2)}) collective-permute-start(bf16[128,1280]{1,0:T(8,128)(2,1)S(1)} %layer_out.9.refs_4_), channel_id=1, source_target_pairs={{48,32},{49,33},{50,34},{51,35},{52,36},{53,37},{54,38},{55,39},{5... | collective-permute-start | bytes 983048 | tf_op jit(solution)/shard_map/ppermute | solution.py:456
  214.1 21.0 %collective-permute-start.30 = (bf16[128,1280]{1,0:T(8,128)(2,1)S(1)}, bf16[128,1280]{1,0:T(8,128)(2,1)S(1)}, u32[]{:S(2)}, u32[]{:S(2)}) collective-permute-start(bf16[128,1280]{1,0:T(8,128)(2,1)S(1)} %layer_out.9.refs_4_), channel_id=1, source_target_pairs={{48,16},{49,17},{50,18},{51,19},{52,20},{53,21},{54,22},{55,23},{5... | collective-permute-start | bytes 983048 | tf_op jit(solution)/shard_map/ppermute | solution.py:460
  (24 other events, 102.4 us)
Sparse Core Ops, SparseCore 0:
  11.7 88.6 all-gather.6
  102.5 43.5 all-gather.4

commit v6 on v5

--- a/solution.py
+++ b/solution.py
@@ -453,11 +453,10 @@
             name="layer_out",
         )(place, mask, q, num, den, left, right, carried, out_near, out_far)
         if moment >= sections - 1:
-            sent = [lax.ppermute(finished, "section", [(sections - 1, t)]) for t in (0, 2)]
+            targets = (0, 2) if moment == sections - 1 else (1, 2, 0)
+            sent = [lax.ppermute(finished, "section", [(sections - 1, t)]) for t in targets]
             if moment == sections - 1:
                 relayed = sent[0]
-            else:
-                sent.append(lax.ppermute(finished, "section", [(sections - 1, 1)]))
             memory += [finished] + sent
         if moment < MB + sections - 2:
             carried = lax.ppermute(finished, "section", onward)

time: 289 us -> 287 us (level)
  the two profiles are of different devices: /device:TPU:2 before, /device:TPU:4 now
where the time goes in v6:
time: 287 us; the launch traced here: 285 us
  starting transfers between devices  84.3 us (29%)
  blocking collectives  64.1 us (22%)
  waiting for transfers between devices  47.1 us (16%)
  Pallas kernels  45.6 us (16%)
  local copies, waits for them, and re-layouts  23.8 us (8%)
  between operations  15 us (5%)
  other arithmetic  5.2 us (2%)
    ppermute x8, starting transfers between devices, around(): lax.ppermute(value, axis, [(i, (i + step) % size) for i in range(size)])  28.6 us
    all_to_all x1, blocking collectives, per_device(): lax.all_to_all(jnp.broadcast_to(lanes[None], (groups,) + lanes.shape), 'd...  25.1 us
    all_gather x1, blocking collectives, per_device(): everyone = lax.all_gather(pieces, 'tm', axis=0)  24.7 us
    ppermute x5, starting transfers between devices, per_device(): left = lax.ppermute(last, 'tm', up)  24 us
    ppermute x8, waiting for transfers between devices, around(): lax.ppermute(value, axis, [(i, (i + step) % size) for i in range(size)])  19.1 us
    ppermute x5, waiting for transfers between devices, per_device(): lax.ppermute(finished, 'section', [(sections - 1, t)])  17 us
    unnamed x78, local copies, waits for them, and re-layouts  14.4 us
    all_to_all x1, blocking collectives, per_device(): grad = lax.all_to_all(grad, 'dp', 0, 0, tiled=True)  14.2 us
  transfers between devices with their start and end apart: 33, of which 11 were waited for; matrix products, arithmetic and copies ran while one was open for 4% of the time, Pallas kernels for 13%

profile of v6, /device:TPU:4, one launch (start us, length us, event | category | flops | bytes accessed | tf_op | source)
XLA Modules:
  0.0 285.0 jit_solution(2908092878753896479)
XLA Ops:
  11.5 25.1 %all_to_all.10 = bf16[8,200,128]{2,1,0:T(8,128)(2,1)S(1)} all-to-all(bf16[8,200,128]{2,1,0:T(8,128)(2,1)S(1)} %broadcast_in_dim.5), channel_id=1, replica_groups=mesh['dp'=8,'section'=4,'tm'=16] {'dp'}, dimensions={0} | all-to-all | bytes 819200 | tf_op jit(solution)/shard_map/all_to_all | solution.py:303
  37.1 3.5 %collective-permute-start.4 = (bf16[80,2560]{1,0:T(8,128)(2,1)S(1)}, bf16[80,2560]{1,0:T(8,128)(2,1)S(1)}, u32[]{:S(2)}, u32[]{:S(2)}) collective-permute-start(bf16[80,2560]{1,0:T(8,128)(2,1)S(1)} %reshape.103.refs_0_), channel_id=1, source_target_pairs={{0,2},{1,3},{2,4},{3,5},{4,6},{5,7},{6,8},{7,9},{8,10},{9,11},{10,... | collective-permute-start | bytes 1228808 | tf_op jit(solution)/shard_map/ppermute | solution.py:299
  40.6 3.8 %collective-permute-start = (bf16[80,2560]{1,0:T(8,128)(2,1)S(1)}, bf16[80,2560]{1,0:T(8,128)(2,1)S(1)}, u32[]{:S(2)}, u32[]{:S(2)}) collective-permute-start(bf16[80,2560]{1,0:T(8,128)(2,1)S(1)} %reshape.103.refs_0_), channel_id=1, source_target_pairs={{0,14},{1,15},{2,0},{3,1},{4,2},{5,3},{6,4},{7,5},{8,6},{9,7},{10,... | collective-permute-start | bytes 1228808 | tf_op jit(solution)/shard_map/ppermute | solution.py:299
  44.5 6.3 %collective-permute-done.4.refs_1_ = bf16[80,2560]{1,0:T(8,128)(2,1)S(1)} collective-permute-done((bf16[80,2560]{1,0:T(8,128)(2,1)S(1)}, bf16[80,2560]{1,0:T(8,128)(2,1)S(1)}, u32[]{:S(2)}, u32[]{:S(2)}) %collective-permute-start.4) | collective-permute-done | bytes 409632 | tf_op jit(solution)/shard_map/ppermute | solution.py:299
  50.7 1.9 collective-permute-start.5
  52.7 5.1 %collective-permute-start.1 = (bf16[80,2560]{1,0:T(8,128)(2,1)S(1)}, bf16[80,2560]{1,0:T(8,128)(2,1)}, u32[]{:S(2)}, u32[]{:S(2)}) collective-permute-start(bf16[80,2560]{1,0:T(8,128)(2,1)S(1)} %collective-permute-done.refs_4_), channel_id=1, source_target_pairs={{0,14},{1,15},{2,0},{3,1},{4,2},{5,3},{6,4},{7,5},{8,6},{9,7},{10,... | collective-permute-start | bytes 1228808 | tf_op jit(solution)/shard_map/ppermute | solution.py:299
  57.8 5.2 %collective-permute-done.5.refs_2_ = bf16[80,2560]{1,0:T(8,128)(2,1)S(1)} collective-permute-done((bf16[80,2560]{1,0:T(8,128)(2,1)S(1)}, bf16[80,2560]{1,0:T(8,128)(2,1)S(1)}, u32[]{:S(2)}, u32[]{:S(2)}) %collective-permute-start.5) | collective-permute-done | bytes 409632 | tf_op jit(solution)/shard_map/ppermute | solution.py:299
  63.0 1.9 collective-permute-start.6
  64.9 5.1 %collective-permute-start.2 = (bf16[80,2560]{1,0:T(8,128)(2,1)}, bf16[80,2560]{1,0:T(8,128)(2,1)S(1)}, u32[]{:S(2)}, u32[]{:S(2)}) collective-permute-start(bf16[80,2560]{1,0:T(8,128)(2,1)} %collective-permute-done.1.refs_5_), channel_id=1, source_target_pairs={{0,14},{1,15},{2,0},{3,1},{4,2},{5,3},{6,4},{7,5},{8,6},{9,7},{10,... | collective-permute-start | bytes 1228808 | tf_op jit(solution)/shard_map/ppermute | solution.py:299
  70.2 5.1 %collective-permute-done.6.refs_3_ = bf16[80,2560]{1,0:T(8,128)(2,1)S(1)} collective-permute-done((bf16[80,2560]{1,0:T(8,128)(2,1)S(1)}, bf16[80,2560]{1,0:T(8,128)(2,1)S(1)}, u32[]{:S(2)}, u32[]{:S(2)}) %collective-permute-start.6) | collective-permute-done | bytes 409632 | tf_op jit(solution)/shard_map/ppermute | solution.py:299
  76.1 1.9 collective-permute-start.7
  78.8 5.3 %collective-permute-start.3 = (bf16[32,2560]{1,0:T(8,128)(2,1)}, bf16[32,2560]{1,0:T(8,128)(2,1)}, u32[]{:S(2)}, u32[]{:S(2)}) collective-permute-start(bf16[32,2560]{1,0:T(8,128)(2,1)} %slice.12), channel_id=1, source_target_pairs={{0,14},{1,15},{2,0},{3,1},{4,2},{5,3},{6,4},{7,5},{8,6},{9,7},{10,... | collective-permute-start | bytes 491528 | tf_op jit(solution)/shard_map/ppermute | solution.py:299
  85.5 2.5 collective-permute-done.3.refs_8_
  88.7 4.0 %join.1 = (bf16[640,640]{1,0:T(8,128)(2,1)}, bf16[640,1280]{1,0:T(8,128)(2,1)}, bf16[640,640]{1,0:T(8,128)(2,1)}) custom-call(bf16[80,2560]{1,0:T(8,128)(2,1)} %copy-done.28, bf16[80,2560]{1,0:T(8,128)(2,1)} %copy-done.31, bf16[80,2560]{1,0:T(8,128)(2,1)} %copy-done.33, bf16[80,2560]{1,0:T(8,128)(2,1)} %copy-done.29, bf16[80,2560]{1,0:T(8,128)(2,1)} %copy-done.32, ...), custom_call_target="tpu_custom_call" | custom-call | tf_op jit(solution)/shard_map/join/pallas_call | solution.py:337
  92.8 1.9 collective-permute-start.8
  94.7 2.4 collective-permute-start.9
  97.1 1.9 collective-permute-start.12
  102.9 2.5 collective-permute-start.10
  109.0 2.2 own_blocks.5
  111.3 2.9 %layer_out.5 = bf16[128,1280]{1,0:T(8,128)(2,1)} custom-call(s32[6]{0:T(128)S(1)} %stack.60.place_ref, s32[8]{0:T(128)S(1)} %reshape.102.mask_ref, bf16[128,640]{1,0:T(8,128)(2,1)S(1)} %get-tuple-element.62.q_ref, f32[128,640]{1,0:T(8,128)S(1)} %get-tuple-element.63.num_ref, f32[128,640]{1,0:T(8,128)S(1)} %get-tuple-element.64.den_ref, ...), custom_call_target="tpu_custom_call" | custom-call | tf_op jit(solution)/shard_map/layer_out/pallas_call | solution.py:446
  114.2 3.1 %collective-permute-start.13 = (bf16[128,1280]{1,0:T(8,128)(2,1)}, bf16[128,1280]{1,0:T(8,128)(2,1)}, u32[]{:S(2)}, u32[]{:S(2)}) collective-permute-start(bf16[128,1280]{1,0:T(8,128)(2,1)} %layer_out.5), channel_id=1, source_target_pairs={{0,16},{16,32},{32,48},{1,17},{17,33},{33,49},{2,18},{18,34},{34,5... | collective-permute-start | bytes 983048 | tf_op jit(solution)/shard_map/ppermute | solution.py:462
  117.4 5.0 %reshape.107.w_ref = bf16[1280,768]{1,0:T(8,128)(2,1)} reshape(bf16[128,10,768]{2,1,0:T(8,128)(2,1)} %all-gather.7.cloned.1.call-done) | data formatting | bytes 3932160 | tf_op jit(solution)/shard_map/optimization_barrier | solution.py:375
  122.3 4.5 %collective-permute-done.13 = bf16[128,1280]{1,0:T(8,128)(2,1)} collective-permute-done((bf16[128,1280]{1,0:T(8,128)(2,1)}, bf16[128,1280]{1,0:T(8,128)(2,1)}, u32[]{:S(2)}, u32[]{:S(2)}) %collective-permute-start.13) | collective-permute-done | bytes 327712 | tf_op jit(solution)/shard_map/ppermute | solution.py:462
  128.8 2.3 collective-permute-start.14
  132.4 2.0 own_blocks.6
  135.2 2.4 layer_out.6
  137.5 3.1 %collective-permute-start.16 = (bf16[128,1280]{1,0:T(8,128)(2,1)}, bf16[128,1280]{1,0:T(8,128)(2,1)}, u32[]{:S(2)}, u32[]{:S(2)}) collective-permute-start(bf16[128,1280]{1,0:T(8,128)(2,1)} %layer_out.6), channel_id=1, source_target_pairs={{0,16},{16,32},{32,48},{1,17},{17,33},{33,49},{2,18},{18,34},{34,5... | collective-permute-start | bytes 983048 | tf_op jit(solution)/shard_map/ppermute | solution.py:462
  147.3 2.0 keys_values.7
  149.3 9.0 %collective-permute-start.17 = (bf16[64,1280]{1,0:T(8,128)(2,1)S(1)}, bf16[64,1280]{1,0:T(8,128)(2,1)S(1)}, u32[]{:S(2)}, u32[]{:S(2)}) collective-permute-start(bf16[64,1280]{1,0:T(8,128)(2,1)S(1)} %get-tuple-element.77.last_ref), channel_id=1, source_target_pairs={{0,1},{1,2},{2,3},{3,4},{4,5},{5,6},{6,7},{7,8},{8,9},{9,10},{10,1... | collective-permute-start | bytes 491528 | tf_op jit(solution)/shard_map/ppermute | solution.py:433
  159.8 2.0 own_blocks.7
  162.6 2.8 layer_out.7
  165.3 3.0 %collective-permute-start.19 = (bf16[128,1280]{1,0:T(8,128)(2,1)}, bf16[128,1280]{1,0:T(8,128)(2,1)}, u32[]{:S(2)}, u32[]{:S(2)}) collective-permute-start(bf16[128,1280]{1,0:T(8,128)(2,1)} %layer_out.7), channel_id=1, source_target_pairs={{0,16},{16,32},{32,48},{1,17},{17,33},{33,49},{2,18},{18,34},{34,5... | collective-permute-start | bytes 983048 | tf_op jit(solution)/shard_map/ppermute | solution.py:462
  168.6 2.5 copy-done.2
  172.6 2.2 queries.1.q_ref
  175.5 2.0 keys_values.8
  177.5 5.6 %collective-permute-start.20 = (bf16[64,1280]{1,0:T(8,128)(2,1)S(1)}, bf16[64,1280]{1,0:T(8,128)(2,1)S(1)}, u32[]{:S(2)}, u32[]{:S(2)}) collective-permute-start(bf16[64,1280]{1,0:T(8,128)(2,1)S(1)} %get-tuple-element.86.last_ref), channel_id=1, source_target_pairs={{0,1},{1,2},{2,3},{3,4},{4,5},{5,6},{6,7},{7,8},{8,9},{9,10},{10,1... | collective-permute-start | bytes 491528 | tf_op jit(solution)/shard_map/ppermute | solution.py:433
  184.5 2.0 own_blocks.8
  187.8 2.8 layer_out.8.refs_0_
  190.6 3.3 %collective-permute-start.24 = (bf16[128,1280]{1,0:T(8,128)(2,1)}, bf16[128,1280]{1,0:T(8,128)(2,1)S(1)}, u32[]{:S(2)}, u32[]{:S(2)}) collective-permute-start(bf16[128,1280]{1,0:T(8,128)(2,1)} %layer_out.8.refs_0_), channel_id=1, source_target_pairs={{0,16},{16,32},{32,48},{1,17},{17,33},{33,49},{2,18},{18,34},{34,5... | collective-permute-start | bytes 983048 | tf_op jit(solution)/shard_map/ppermute | solution.py:462
  196.7 3.6 %collective-permute-done.24.x_ref = bf16[128,1280]{1,0:T(8,128)(2,1)S(1)} collective-permute-done((bf16[128,1280]{1,0:T(8,128)(2,1)}, bf16[128,1280]{1,0:T(8,128)(2,1)S(1)}, u32[]{:S(2)}, u32[]{:S(2)}) %collective-permute-start.24) | collective-permute-done | bytes 327712 | tf_op jit(solution)/shard_map/ppermute | solution.py:462
  201.3 4.6 %collective-permute-start.26 = (bf16[64,1280]{1,0:T(8,128)(2,1)S(1)}, bf16[64,1280]{1,0:T(8,128)(2,1)S(1)}, u32[]{:S(2)}, u32[]{:S(2)}) collective-permute-start(bf16[64,1280]{1,0:T(8,128)(2,1)S(1)} %get-tuple-element.93.last_ref), channel_id=1, source_target_pairs={{0,1},{1,2},{2,3},{3,4},{4,5},{5,6},{6,7},{7,8},{8,9},{9,10},{10,1... | collective-permute-start | bytes 491528 | tf_op jit(solution)/shard_map/ppermute | solution.py:433
  208.5 2.0 own_blocks.9
  215.8 2.0 collective-permute-done.23.refs_2_
  217.8 14.9 %collective-permute-done.29.refs_6_ = bf16[128,1280]{1,0:T(8,128)(2,1)S(1)} collective-permute-done((bf16[128,1280]{1,0:T(8,128)(2,1)S(1)}, bf16[128,1280]{1,0:T(8,128)(2,1)S(1)}, u32[]{:S(2)}, u32[]{:S(2)}) %collective-permute-start.29) | collective-permute-done | bytes 327712 | tf_op jit(solution)/shard_map/ppermute | solution.py:457
  233.6 2.4 cross.1
  236.0 24.7 %all-gather = bf16[3584,128]{1,0:T(8,128)(2,1)S(1)} all-gather(bf16[224,128]{1,0:T(8,128)(2,1)S(1)} %cross.1), channel_id=2, replica_groups=mesh['dp'=8,'section'=4,'tm'=16] {'tm'}, dimensions={0}, use_global_device_ids=true | all-gather | bytes 974848 | tf_op jit(solution)/shard_map/all_gather | solution.py:472
  260.6 2.7 combine.1
  263.3 14.2 %all_to_all.11 = bf16[8,16,256]{2,1,0:T(8,128)(2,1)S(1)} all-to-all(bf16[8,16,256]{2,1,0:T(8,128)(2,1)S(1)} %get-tuple-element.101), channel_id=1, replica_groups=mesh['dp'=8,'section'=4,'tm'=16] {'dp'}, dimensions={0} | all-to-all | bytes 131072 | tf_op jit(solution)/shard_map/all_to_all | solution.py:486
  (147 shorter events, 46.6 us)
Async XLA Ops:
  7.2 110.2 %all-gather.7.cloned.1.call-start = ((), (), s32[]{:S(2)}) async-start(), calls=%async_computation.3 | async-start | bytes 3170304 | tf_op jit(solution)/shard_map/all_gather | solution.py:350
  8.6 160.0 %all-gather.5.cloned.1.call-start = ((), (), s32[]{:S(2)}) async-start(), calls=%async_computation.2 | async-start | bytes 5570560 | tf_op jit(solution)/shard_map/all_gather | solution.py:351
  10.4 74.0 %copy-start.22 = (bf16[2,128,1280]{2,1,0:T(8,128)(2,1)S(1)}, bf16[2,128,1280]{2,1,0:T(8,128)(2,1)}, u32[]{:S(2)}) copy-start(bf16[2,128,1280]{2,1,0:T(8,128)(2,1)} %frames_ref.1) | copy-start | bytes 1966084
  37.1 50.9 %copy-start.28 = (bf16[80,2560]{1,0:T(8,128)(2,1)}, bf16[80,2560]{1,0:T(8,128)(2,1)S(1)}, u32[]{:S(2)}) copy-start(bf16[80,2560]{1,0:T(8,128)(2,1)S(1)} %reshape.103.refs_0_) | copy-start | bytes 1228804
  37.1 13.6 %collective-permute-start.4 = (bf16[80,2560]{1,0:T(8,128)(2,1)S(1)}, bf16[80,2560]{1,0:T(8,128)(2,1)S(1)}, u32[]{:S(2)}, u32[]{:S(2)}) collective-permute-start(bf16[80,2560]{1,0:T(8,128)(2,1)S(1)} %reshape.103.refs_0_), channel_id=1, source_target_pairs={{0,2},{1,3},{2,4},{3,5},{4,6},{5,7},{6,8},{7,9},{8,10},{9,11},{10,... | collective-permute-start | bytes 1228808 | tf_op jit(solution)/shard_map/ppermute | solution.py:299
  40.6 12.0 %collective-permute-start = (bf16[80,2560]{1,0:T(8,128)(2,1)S(1)}, bf16[80,2560]{1,0:T(8,128)(2,1)S(1)}, u32[]{:S(2)}, u32[]{:S(2)}) collective-permute-start(bf16[80,2560]{1,0:T(8,128)(2,1)S(1)} %reshape.103.refs_0_), channel_id=1, source_target_pairs={{0,14},{1,15},{2,0},{3,1},{4,2},{5,3},{6,4},{7,5},{8,6},{9,7},{10,... | collective-permute-start | bytes 1228808 | tf_op jit(solution)/shard_map/ppermute | solution.py:299
  50.7 37.3 %copy-start.31 = (bf16[80,2560]{1,0:T(8,128)(2,1)}, bf16[80,2560]{1,0:T(8,128)(2,1)S(1)}, u32[]{:S(2)}) copy-start(bf16[80,2560]{1,0:T(8,128)(2,1)S(1)} %collective-permute-done.4.refs_1_) | copy-start | bytes 1228804
  50.7 12.2 %collective-permute-start.5 = (bf16[80,2560]{1,0:T(8,128)(2,1)S(1)}, bf16[80,2560]{1,0:T(8,128)(2,1)S(1)}, u32[]{:S(2)}, u32[]{:S(2)}) collective-permute-start(bf16[80,2560]{1,0:T(8,128)(2,1)S(1)} %collective-permute-done.4.refs_1_), channel_id=1, source_target_pairs={{0,2},{1,3},{2,4},{3,5},{4,6},{5,7},{6,8},{7,9},{8,10},{9,11},{10,... | collective-permute-start | bytes 1228808 | tf_op jit(solution)/shard_map/ppermute | solution.py:299
  52.6 12.2 %copy-start.32 = (bf16[80,2560]{1,0:T(8,128)(2,1)}, bf16[80,2560]{1,0:T(8,128)(2,1)S(1)}, u32[]{:S(2)}) copy-start(bf16[80,2560]{1,0:T(8,128)(2,1)S(1)} %collective-permute-done.refs_4_) | copy-start | bytes 1228804
  52.7 12.2 %collective-permute-start.1 = (bf16[80,2560]{1,0:T(8,128)(2,1)S(1)}, bf16[80,2560]{1,0:T(8,128)(2,1)}, u32[]{:S(2)}, u32[]{:S(2)}) collective-permute-start(bf16[80,2560]{1,0:T(8,128)(2,1)S(1)} %collective-permute-done.refs_4_), channel_id=1, source_target_pairs={{0,14},{1,15},{2,0},{3,1},{4,2},{5,3},{6,4},{7,5},{8,6},{9,7},{10,... | collective-permute-start | bytes 1228808 | tf_op jit(solution)/shard_map/ppermute | solution.py:299
  63.0 21.3 %copy-start.33 = (bf16[80,2560]{1,0:T(8,128)(2,1)}, bf16[80,2560]{1,0:T(8,128)(2,1)S(1)}, u32[]{:S(2)}) copy-start(bf16[80,2560]{1,0:T(8,128)(2,1)S(1)} %collective-permute-done.5.refs_2_) | copy-start | bytes 1228804
  63.0 12.4 %collective-permute-start.6 = (bf16[80,2560]{1,0:T(8,128)(2,1)S(1)}, bf16[80,2560]{1,0:T(8,128)(2,1)S(1)}, u32[]{:S(2)}, u32[]{:S(2)}) collective-permute-start(bf16[80,2560]{1,0:T(8,128)(2,1)S(1)} %collective-permute-done.5.refs_2_), channel_id=1, source_target_pairs={{0,2},{1,3},{2,4},{3,5},{4,6},{5,7},{6,8},{7,9},{8,10},{9,11},{10,... | collective-permute-start | bytes 1228808 | tf_op jit(solution)/shard_map/ppermute | solution.py:299
  64.9 13.2 %collective-permute-start.2 = (bf16[80,2560]{1,0:T(8,128)(2,1)}, bf16[80,2560]{1,0:T(8,128)(2,1)S(1)}, u32[]{:S(2)}, u32[]{:S(2)}) collective-permute-start(bf16[80,2560]{1,0:T(8,128)(2,1)} %collective-permute-done.1.refs_5_), channel_id=1, source_target_pairs={{0,14},{1,15},{2,0},{3,1},{4,2},{5,3},{6,4},{7,5},{8,6},{9,7},{10,... | collective-permute-start | bytes 1228808 | tf_op jit(solution)/shard_map/ppermute | solution.py:299
  75.3 12.7 %copy-start.29 = (bf16[80,2560]{1,0:T(8,128)(2,1)}, bf16[80,2560]{1,0:T(8,128)(2,1)S(1)}, u32[]{:S(2)}) copy-start(bf16[80,2560]{1,0:T(8,128)(2,1)S(1)} %collective-permute-done.6.refs_3_) | copy-start | bytes 1228804
  76.1 11.9 %collective-permute-start.7 = (bf16[48,2560]{1,0:T(8,128)(2,1)}, bf16[48,2560]{1,0:T(8,128)(2,1)S(1)}, u32[]{:S(2)}, u32[]{:S(2)}) collective-permute-start(bf16[48,2560]{1,0:T(8,128)(2,1)} %slice.13), channel_id=1, source_target_pairs={{0,2},{1,3},{2,4},{3,5},{4,6},{5,7},{6,8},{7,9},{8,10},{9,11},{10,... | collective-permute-start | bytes 737288 | tf_op jit(solution)/shard_map/ppermute | solution.py:299
  78.8 9.2 %collective-permute-start.3 = (bf16[32,2560]{1,0:T(8,128)(2,1)}, bf16[32,2560]{1,0:T(8,128)(2,1)}, u32[]{:S(2)}, u32[]{:S(2)}) collective-permute-start(bf16[32,2560]{1,0:T(8,128)(2,1)} %slice.12), channel_id=1, source_target_pairs={{0,14},{1,15},{2,0},{3,1},{4,2},{5,3},{6,4},{7,5},{8,6},{9,7},{10,... | collective-permute-start | bytes 491528 | tf_op jit(solution)/shard_map/ppermute | solution.py:299
  85.4 13.6 %copy-start.20 = (bf16[128,1280]{1,0:T(8,128)(2,1)}, bf16[128,1280]{1,0:T(8,128)(2,1)S(1)}, u32[]{:S(2)}) copy-start(bf16[128,1280]{1,0:T(8,128)(2,1)S(1)} %get-tuple-element.55.x_ref) | copy-start | bytes 983044
  92.7 13.9 %copy-start.35 = (s32[2,2,2]{2,1,0:T(2,128)S(1)}, s32[2,2,2]{2,1,0:T(2,128)}, u32[]{:S(2)}) copy-start(s32[2,2,2]{2,1,0:T(2,128)} %param.11) | copy-start | bytes 100
  92.8 6.3 %collective-permute-start.8 = (bf16[640,1280]{1,0:T(8,128)(2,1)}, bf16[640,1280]{1,0:T(8,128)(2,1)S(1)}, u32[]{:S(2)}, u32[]{:S(2)}) collective-permute-start(bf16[640,1280]{1,0:T(8,128)(2,1)} %get-tuple-element.57.near_ref), channel_id=1, source_target_pairs={{0,1},{1,0},{2,3},{3,2},{4,5},{5,4},{6,7},{7,6},{8,9},{9,8},{10,11... | collective-permute-start | bytes 4915208 | tf_op jit(solution)/shard_map/ppermute | solution.py:347
  94.7 12.2 %collective-permute-start.9 = (bf16[640,640]{1,0:T(8,128)(2,1)}, bf16[640,640]{1,0:T(8,128)(2,1)}, u32[]{:S(2)}, u32[]{:S(2)}) collective-permute-start(bf16[640,640]{1,0:T(8,128)(2,1)} %get-tuple-element.61.near_ref), channel_id=1, source_target_pairs={{0,1},{1,0},{2,3},{3,2},{4,5},{5,4},{6,7},{7,6},{8,9},{9,8},{10,11... | collective-permute-start | bytes 2457608 | tf_op jit(solution)/shard_map/ppermute | solution.py:347
  97.1 14.1 %collective-permute-start.12 = (bf16[640,640]{1,0:T(8,128)(2,1)}, bf16[640,640]{1,0:T(8,128)(2,1)S(1)}, u32[]{:S(2)}, u32[]{:S(2)}) collective-permute-start(bf16[640,640]{1,0:T(8,128)(2,1)} %get-tuple-element.65.near_ref), channel_id=1, source_target_pairs={{0,1},{1,0},{2,3},{3,2},{4,5},{5,4},{6,7},{7,6},{8,9},{9,8},{10,11... | collective-permute-start | bytes 2457608 | tf_op jit(solution)/shard_map/ppermute | solution.py:347
  102.9 8.4 %collective-permute-start.10 = (bf16[64,1280]{1,0:T(8,128)(2,1)}, bf16[64,1280]{1,0:T(8,128)(2,1)S(1)}, u32[]{:S(2)}, u32[]{:S(2)}) collective-permute-start(bf16[64,1280]{1,0:T(8,128)(2,1)} %get-tuple-element.60.last_ref), channel_id=1, source_target_pairs={{0,1},{1,2},{2,3},{3,4},{4,5},{5,6},{6,7},{7,8},{8,9},{9,10},{10,1... | collective-permute-start | bytes 491528 | tf_op jit(solution)/shard_map/ppermute | solution.py:433
  105.4 5.9 %collective-permute-start.11 = (bf16[64,1280]{1,0:T(8,128)(2,1)}, bf16[64,1280]{1,0:T(8,128)(2,1)}, u32[]{:S(2)}, u32[]{:S(2)}) collective-permute-start(bf16[64,1280]{1,0:T(8,128)(2,1)} %get-tuple-element.59.first_ref), channel_id=1, source_target_pairs={{1,0},{2,1},{3,2},{4,3},{5,4},{6,5},{7,6},{8,7},{9,8},{10,9},{11,1... | collective-permute-start | bytes 491528 | tf_op jit(solution)/shard_map/ppermute | solution.py:434
  114.2 12.6 %collective-permute-start.13 = (bf16[128,1280]{1,0:T(8,128)(2,1)}, bf16[128,1280]{1,0:T(8,128)(2,1)}, u32[]{:S(2)}, u32[]{:S(2)}) collective-permute-start(bf16[128,1280]{1,0:T(8,128)(2,1)} %layer_out.5), channel_id=1, source_target_pairs={{0,16},{16,32},{32,48},{1,17},{17,33},{33,49},{2,18},{18,34},{34,5... | collective-permute-start | bytes 983048 | tf_op jit(solution)/shard_map/ppermute | solution.py:462
  128.8 5.7 %collective-permute-start.14 = (bf16[64,1280]{1,0:T(8,128)(2,1)S(1)}, bf16[64,1280]{1,0:T(8,128)(2,1)S(1)}, u32[]{:S(2)}, u32[]{:S(2)}) collective-permute-start(bf16[64,1280]{1,0:T(8,128)(2,1)S(1)} %get-tuple-element.69.last_ref), channel_id=1, source_target_pairs={{0,1},{1,2},{2,3},{3,4},{4,5},{5,6},{6,7},{7,8},{8,9},{9,10},{10,1... | collective-permute-start | bytes 491528 | tf_op jit(solution)/shard_map/ppermute | solution.py:433
  131.1 4.0 %collective-permute-start.15 = (bf16[64,1280]{1,0:T(8,128)(2,1)S(1)}, bf16[64,1280]{1,0:T(8,128)(2,1)S(1)}, u32[]{:S(2)}, u32[]{:S(2)}) collective-permute-start(bf16[64,1280]{1,0:T(8,128)(2,1)S(1)} %get-tuple-element.68.first_ref), channel_id=1, source_target_pairs={{1,0},{2,1},{3,2},{4,3},{5,4},{6,5},{7,6},{8,7},{9,8},{10,9},{11,1... | collective-permute-start | bytes 491528 | tf_op jit(solution)/shard_map/ppermute | solution.py:434
  137.5 9.8 %collective-permute-start.16 = (bf16[128,1280]{1,0:T(8,128)(2,1)}, bf16[128,1280]{1,0:T(8,128)(2,1)}, u32[]{:S(2)}, u32[]{:S(2)}) collective-permute-start(bf16[128,1280]{1,0:T(8,128)(2,1)} %layer_out.6), channel_id=1, source_target_pairs={{0,16},{16,32},{32,48},{1,17},{17,33},{33,49},{2,18},{18,34},{34,5... | collective-permute-start | bytes 983048 | tf_op jit(solution)/shard_map/ppermute | solution.py:462
  147.3 12.4 %copy-start.13 = (bf16[640,640]{1,0:T(8,128)(2,1)S(1)}, bf16[640,640]{1,0:T(8,128)(2,1)}, u32[]{:S(2)}) copy-start(bf16[640,640]{1,0:T(8,128)(2,1)} %get-tuple-element.61.near_ref) | copy-start | bytes 2457604
  149.3 13.3 %copy-start.5 = (bf16[640,640]{1,0:T(8,128)(2,1)S(1)}, bf16[640,640]{1,0:T(8,128)(2,1)}, u32[]{:S(2)}) copy-start(bf16[640,640]{1,0:T(8,128)(2,1)} %get-tuple-element.65.near_ref) | copy-start | bytes 2457604
  149.3 13.3 %copy-start.9 = (bf16[640,640]{1,0:T(8,128)(2,1)S(1)}, bf16[640,640]{1,0:T(8,128)(2,1)}, u32[]{:S(2)}) copy-start(bf16[640,640]{1,0:T(8,128)(2,1)} %copy-done.7) | copy-start | bytes 2457604
  149.3 12.5 %collective-permute-start.17 = (bf16[64,1280]{1,0:T(8,128)(2,1)S(1)}, bf16[64,1280]{1,0:T(8,128)(2,1)S(1)}, u32[]{:S(2)}, u32[]{:S(2)}) collective-permute-start(bf16[64,1280]{1,0:T(8,128)(2,1)S(1)} %get-tuple-element.77.last_ref), channel_id=1, source_target_pairs={{0,1},{1,2},{2,3},{3,4},{4,5},{5,6},{6,7},{7,8},{8,9},{9,10},{10,1... | collective-permute-start | bytes 491528 | tf_op jit(solution)/shard_map/ppermute | solution.py:433
  158.3 4.3 %collective-permute-start.18 = (bf16[64,1280]{1,0:T(8,128)(2,1)S(1)}, bf16[64,1280]{1,0:T(8,128)(2,1)S(1)}, u32[]{:S(2)}, u32[]{:S(2)}) collective-permute-start(bf16[64,1280]{1,0:T(8,128)(2,1)S(1)} %get-tuple-element.76.first_ref), channel_id=1, source_target_pairs={{1,0},{2,1},{3,2},{4,3},{5,4},{6,5},{7,6},{8,7},{9,8},{10,9},{11,1... | collective-permute-start | bytes 491528 | tf_op jit(solution)/shard_map/ppermute | solution.py:434
  165.3 10.2 %collective-permute-start.19 = (bf16[128,1280]{1,0:T(8,128)(2,1)}, bf16[128,1280]{1,0:T(8,128)(2,1)}, u32[]{:S(2)}, u32[]{:S(2)}) collective-permute-start(bf16[128,1280]{1,0:T(8,128)(2,1)} %layer_out.7), channel_id=1, source_target_pairs={{0,16},{16,32},{32,48},{1,17},{17,33},{33,49},{2,18},{18,34},{34,5... | collective-permute-start | bytes 983048 | tf_op jit(solution)/shard_map/ppermute | solution.py:462
  172.6 11.9 %copy-start.14 = (bf16[640,640]{1,0:T(8,128)(2,1)S(1)}, bf16[640,640]{1,0:T(8,128)(2,1)}, u32[]{:S(2)}) copy-start(bf16[640,640]{1,0:T(8,128)(2,1)} %get-tuple-element.61.near_ref) | copy-start | bytes 2457604
  172.6 22.7 %slice-start = ((s8[5242880]{0:T(1024)(128)(4,1)}), s8[1048576]{0:T(1024)(128)(4,1)S(1)}, s32[]{:S(2)}) async-start(s8[5242880]{0:T(1024)(128)(4,1)} %bitcast.26), calls=%async_computation.4 | async-start | bytes 2097152
  175.5 19.9 %slice-start.1 = ((s8[5242880]{0:T(1024)(128)(4,1)}), s8[4194304]{0:T(1024)(128)(4,1)S(1)}, s32[]{:S(2)}) async-start(s8[5242880]{0:T(1024)(128)(4,1)} %bitcast.26), calls=%async_computation.5 | async-start | bytes 8388608
  177.5 8.9 %collective-permute-start.20 = (bf16[64,1280]{1,0:T(8,128)(2,1)S(1)}, bf16[64,1280]{1,0:T(8,128)(2,1)S(1)}, u32[]{:S(2)}, u32[]{:S(2)}) collective-permute-start(bf16[64,1280]{1,0:T(8,128)(2,1)S(1)} %get-tuple-element.86.last_ref), channel_id=1, source_target_pairs={{0,1},{1,2},{2,3},{3,4},{4,5},{5,6},{6,7},{7,8},{8,9},{9,10},{10,1... | collective-permute-start | bytes 491528 | tf_op jit(solution)/shard_map/ppermute | solution.py:433
  183.2 4.7 %collective-permute-start.21 = (bf16[64,1280]{1,0:T(8,128)(2,1)S(1)}, bf16[64,1280]{1,0:T(8,128)(2,1)S(1)}, u32[]{:S(2)}, u32[]{:S(2)}) collective-permute-start(bf16[64,1280]{1,0:T(8,128)(2,1)S(1)} %get-tuple-element.85.first_ref), channel_id=1, source_target_pairs={{1,0},{2,1},{3,2},{4,3},{5,4},{6,5},{7,6},{8,7},{9,8},{10,9},{11,1... | collective-permute-start | bytes 491528 | tf_op jit(solution)/shard_map/ppermute | solution.py:434
  190.6 9.8 %collective-permute-start.24 = (bf16[128,1280]{1,0:T(8,128)(2,1)}, bf16[128,1280]{1,0:T(8,128)(2,1)S(1)}, u32[]{:S(2)}, u32[]{:S(2)}) collective-permute-start(bf16[128,1280]{1,0:T(8,128)(2,1)} %layer_out.8.refs_0_), channel_id=1, source_target_pairs={{0,16},{16,32},{32,48},{1,17},{17,33},{33,49},{2,18},{18,34},{34,5... | collective-permute-start | bytes 983048 | tf_op jit(solution)/shard_map/ppermute | solution.py:462
  193.9 16.6 %collective-permute-start.22 = (bf16[128,1280]{1,0:T(8,128)(2,1)}, bf16[128,1280]{1,0:T(8,128)(2,1)}, u32[]{:S(2)}, u32[]{:S(2)}) collective-permute-start(bf16[128,1280]{1,0:T(8,128)(2,1)} %layer_out.8.refs_0_), channel_id=1, source_target_pairs={{48,0},{49,1},{50,2},{51,3},{52,4},{53,5},{54,6},{55,7},{56,8},{57... | collective-permute-start | bytes 983048 | tf_op jit(solution)/shard_map/ppermute | solution.py:457
  201.3 10.1 %collective-permute-start.26 = (bf16[64,1280]{1,0:T(8,128)(2,1)S(1)}, bf16[64,1280]{1,0:T(8,128)(2,1)S(1)}, u32[]{:S(2)}, u32[]{:S(2)}) collective-permute-start(bf16[64,1280]{1,0:T(8,128)(2,1)S(1)} %get-tuple-element.93.last_ref), channel_id=1, source_target_pairs={{0,1},{1,2},{2,3},{3,4},{4,5},{5,6},{6,7},{7,8},{8,9},{9,10},{10,1... | collective-permute-start | bytes 491528 | tf_op jit(solution)/shard_map/ppermute | solution.py:433
  205.9 5.5 %collective-permute-start.27 = (bf16[64,1280]{1,0:T(8,128)(2,1)S(1)}, bf16[64,1280]{1,0:T(8,128)(2,1)S(1)}, u32[]{:S(2)}, u32[]{:S(2)}) collective-permute-start(bf16[64,1280]{1,0:T(8,128)(2,1)S(1)} %get-tuple-element.92.first_ref), channel_id=1, source_target_pairs={{1,0},{2,1},{3,2},{4,3},{5,4},{6,5},{7,6},{8,7},{9,8},{10,9},{11,1... | collective-permute-start | bytes 491528 | tf_op jit(solution)/shard_map/ppermute | solution.py:434
  207.2 10.6 %collective-permute-start.23 = (bf16[128,1280]{1,0:T(8,128)(2,1)}, bf16[128,1280]{1,0:T(8,128)(2,1)S(1)}, u32[]{:S(2)}, u32[]{:S(2)}) collective-permute-start(bf16[128,1280]{1,0:T(8,128)(2,1)} %layer_out.8.refs_0_), channel_id=1, source_target_pairs={{48,32},{49,33},{50,34},{51,35},{52,36},{53,37},{54,38},{55,39},{5... | collective-permute-start | bytes 983048 | tf_op jit(solution)/shard_map/ppermute | solution.py:457
  210.5 22.2 %copy-start.18 = (bf16[1280,512]{1,0:T(8,128)(2,1)S(1)}, bf16[1280,512]{1,0:T(8,128)(2,1)}, u32[]{:S(2)}) copy-start(bf16[1280,512]{1,0:T(8,128)(2,1)} %copy-done.17) | copy-start | bytes 3932164
  210.6 7.3 %collective-permute-start.25 = (bf16[128,1280]{1,0:T(8,128)(2,1)}, bf16[128,1280]{1,0:T(8,128)(2,1)S(1)}, u32[]{:S(2)}, u32[]{:S(2)}) collective-permute-start(bf16[128,1280]{1,0:T(8,128)(2,1)} %collective-permute-done.22.refs_1_), channel_id=1, source_target_pairs={{0,16},{1,17},{2,18},{3,19},{4,20},{5,21},{6,22},{7,23},{8,24},{9,... | collective-permute-start | bytes 983048 | tf_op jit(solution)/shard_map/ppermute | solution.py:445
  213.0 4.8 %collective-permute-start.28 = (bf16[128,1280]{1,0:T(8,128)(2,1)S(1)}, bf16[128,1280]{1,0:T(8,128)(2,1)S(1)}, u32[]{:S(2)}, u32[]{:S(2)}) collective-permute-start(bf16[128,1280]{1,0:T(8,128)(2,1)S(1)} %layer_out.9.refs_4_), channel_id=1, source_target_pairs={{48,16},{49,17},{50,18},{51,19},{52,20},{53,21},{54,22},{55,23},{5... | collective-permute-start | bytes 983048 | tf_op jit(solution)/shard_map/ppermute | solution.py:457
  213.7 19.1 %collective-permute-start.29 = (bf16[128,1280]{1,0:T(8,128)(2,1)S(1)}, bf16[128,1280]{1,0:T(8,128)(2,1)S(1)}, u32[]{:S(2)}, u32[]{:S(2)}) collective-permute-start(bf16[128,1280]{1,0:T(8,128)(2,1)S(1)} %layer_out.9.refs_4_), channel_id=1, source_target_pairs={{48,32},{49,33},{50,34},{51,35},{52,36},{53,37},{54,38},{55,39},{5... | collective-permute-start | bytes 983048 | tf_op jit(solution)/shard_map/ppermute | solution.py:457
  215.0 17.8 %collective-permute-start.30 = (bf16[128,1280]{1,0:T(8,128)(2,1)S(1)}, bf16[128,1280]{1,0:T(8,128)(2,1)S(1)}, u32[]{:S(2)}, u32[]{:S(2)}) collective-permute-start(bf16[128,1280]{1,0:T(8,128)(2,1)S(1)} %layer_out.9.refs_4_), channel_id=1, source_target_pairs={{48,0},{49,1},{50,2},{51,3},{52,4},{53,5},{54,6},{55,7},{56,8},{57... | collective-permute-start | bytes 983048 | tf_op jit(solution)/shard_map/ppermute | solution.py:457
  (24 other events, 103.3 us)
Sparse Core Ops, SparseCore 0:
  11.7 88.6 all-gather.6
  102.5 43.5 all-gather.4
